TPU v7x, 256 devices: a whole 4x4x8 slice. The times are simulated.
256 devices in a mesh: col: 4 (over z_lo), grp: 64 (over x, z_hi, y, core).
Axes of the slice: x: 4, y: 4, z: 8 (z_hi: 2, z_lo: 4; z = z_hi * 4 + z_lo), core: 2. Of those that a mesh axis runs over, the one named last changes fastest.
Arguments:
- table_rows: bfloat16 [64, 256, 256], P('grp', None, 'col'), may hold values from -1.5 to 1.5
- pool_index: int32 [64, 4, 8192], P('grp'), may hold values from 0 to 255
- bag_length: int32 [64, 8192], P('grp'), may hold values from 1 to 4
- table_slot: int32 [64], replicated, may hold values from 0 to 63, each once
- dense_input: bfloat16 [8192, 13], P('grp'), may hold values from -6 to 6
- bottom_weight: bfloat16 [13, 256], replicated, may hold values from -1.75 to 1.75
- top_weight: bfloat16 [2336, 2048], P(None, 'col'), may hold values from -0.125 to 0.125
- out_weight: bfloat16 [2048], P('col'), may hold values from -0.125 to 0.125
- labels: int32 [8192], P('grp'), may hold values 0 or 1
Outputs:
- logits: float32 [8192], P('grp')
- grad_top: float32 [2336, 2048], P(None, ('col', 'grp'))
- grad_out: float32 [2048], P(('col', 'grp'))
- grad_bottom: float32 [13, 256], replicated
- grad_rows: float32 [64, 256, 256], P('grp', None, 'col')
Inputs may be any that keep to these rules, and one draw needn't show every extreme that they name: `pool_index`: each entry names one of its table's 256 looked-up rows. `bag_length`: slots at or past a bag's length are unused. `table_slot`: every feature is held by exactly one shard.
All inputs are finite; a program needn't handle non-finite values. No bound on the sum of `labels` on one device may be relied on, other than what follows from the above.
Results may differ from a plain program's by a relative error of at most 0.0071.
Values may be sent and summed in bfloat16 or wider, within the bound.
No kernel may reach another device: no remote copies, remote signals or barrier semaphores. Data moves between devices by JAX's collectives and lax.ppermute only.
A program may use at most 128 MiB of HBM per device.

v0:
```python
import jax
import jax.numpy as jnp
import numpy as np
from jax import lax
from jax.sharding import Mesh
from jax.sharding import PartitionSpec as P

COL_GRP = ("col", "grp_0", "grp_1", "grp_2", "grp_3")
GRP = ("grp_0", "grp_1", "grp_2", "grp_3")


def cut_along(x, dim, peers):
    lengths = x.shape
    pieces = x.reshape(*lengths[:dim], peers, lengths[dim] // peers, *lengths[dim + 1 :])
    return jnp.moveaxis(pieces, dim, 0)


def joined_along(pieces, dim):
    lengths = list(pieces.shape[1:])
    lengths[dim] *= pieces.shape[0]
    return jnp.moveaxis(pieces, 0, dim).reshape(lengths)


def joined_exchange(x, axis, axes, splits, concats):
    sizes = [lax.axis_size(a) for a in axes]
    pieces = cut_along(x, splits[0], sizes[0])
    pieces = jnp.moveaxis(cut_along(pieces, splits[1] + 1, sizes[1]), 0, 1)
    inside = pieces.shape[2:]
    pieces = pieces.reshape(-1, *inside)
    pieces = lax.all_to_all(pieces, axis, split_axis=0, concat_axis=0, tiled=True)
    pieces = joined_along(pieces.reshape(*sizes, *inside), concats[0] + 1)
    return joined_along(pieces, concats[1])


def sent_to_all(x, axis):
    copies = jnp.broadcast_to(x, (lax.axis_size(axis), *x.shape))
    return lax.all_to_all(copies, axis, split_axis=0, concat_axis=0, tiled=True)


def gather_directly(x, axis, dim):
    pieces = sent_to_all(x, axis)
    return joined_along(pieces, dim)


def over_copies(x, axis):
    everything = sent_to_all(x, axis)
    return jnp.sum(everything, axis=0)


def scatter_pairs(x, chips, core, dim):
    sizes = (lax.axis_size(chips), lax.axis_size(core))
    pieces = cut_along(x, dim, sizes[0] * sizes[1])
    inside = pieces.shape[1:]
    pieces = pieces.reshape(*sizes, *inside).swapaxes(0, 1).reshape(-1, *inside)
    pieces = lax.psum_scatter(pieces, core, scatter_dimension=0, tiled=True)
    return lax.psum_scatter(pieces, chips, scatter_dimension=0, tiled=True)[0]


def sum_at_owner(x, axis, dim):
    peers = lax.axis_size(axis)
    pieces = lax.all_to_all(cut_along(x, dim, peers), axis, 0, 0, tiled=True)
    return jnp.sum(pieces, axis=0)


def over_pieces(x, axis):
    pieces = lax.all_gather(x, axis)
    return pieces.sum(axis=0)


def count_block(index_block, length_block, uniq_count):
    slot_iota = lax.broadcasted_iota(jnp.int32, index_block.shape, 1)
    row_ids = jnp.where(slot_iota < length_block[:, None, :], index_block, -1)
    values = lax.broadcasted_iota(jnp.int32, (1, 1, uniq_count), 2)
    counts = jnp.zeros((index_block.shape[0], index_block.shape[2], uniq_count), jnp.bfloat16)
    for slot_index in range(index_block.shape[1]):
        counts = counts + jnp.where(row_ids[:, slot_index, :, None] == values, 1.0, 0.0).astype(
            jnp.bfloat16
        )
    return counts


def pair_table(fields):
    upper_a, upper_b = np.triu_indices(fields, 1)
    return upper_a * fields + upper_b


def silu_slope(values):
    sigma = jax.nn.sigmoid(values)
    return sigma * (1.0 + values * (1.0 - sigma))


def interact(vectors):
    fields = vectors.shape[0]
    gram_matrix = jnp.einsum("asc,bsc->abs", vectors, vectors, preferred_element_type=jnp.float32)
    return gram_matrix.reshape(fields * fields, -1)[pair_table(fields)]


def spread(dpairs, vectors):
    fields = vectors.shape[0]
    symmetric = (
        jnp.zeros((fields * fields, dpairs.shape[0]), jnp.bfloat16)
        .at[pair_table(fields)]
        .set(dpairs.T)
    )
    symmetric = symmetric.reshape(fields, fields, -1)
    symmetric = symmetric + jnp.transpose(symmetric, (1, 0, 2))
    return jnp.einsum("abs,bsc->asc", symmetric, vectors, preferred_element_type=jnp.float32)


def body(
    table_rows,
    pool_index,
    bag_length,
    table_slot,
    dense_input,
    bottom_weight,
    top_weight,
    out_weight,
    labels,
):
    tab_count, uniq_count, col_width = table_rows.shape
    bag_slots = pool_index.shape[1]
    samples = pool_index.shape[2]
    local_rows = dense_input.shape[0]
    emb_width = bottom_weight.shape[1]
    stride = min(1024, samples)
    nblocks = samples // stride
    index_blocks = jnp.transpose(
        pool_index.reshape(tab_count, bag_slots, nblocks, stride), (2, 0, 1, 3)
    )
    length_blocks = jnp.transpose(bag_length.reshape(tab_count, nblocks, stride), (1, 0, 2))

    def pool_one(inputs):
        counts = count_block(inputs[0], inputs[1], uniq_count)
        return jnp.einsum(
            "tbu,tuc->tbc", counts, table_rows, preferred_element_type=jnp.float32
        ).astype(jnp.bfloat16)

    pooled_blocks = lax.map(pool_one, (index_blocks, length_blocks))
    pooled = jnp.transpose(pooled_blocks, (1, 0, 2, 3)).reshape(tab_count, samples, col_width)
    inverse = jnp.argsort(table_slot)
    bottom_pre = jnp.dot(dense_input, bottom_weight, preferred_element_type=jnp.float32)
    bottom_out = jax.nn.silu(bottom_pre).astype(jnp.bfloat16)
    quarter_rows = local_rows // lax.axis_size("col")
    first_row = lax.axis_index("col") * quarter_rows
    sectioned = pooled.reshape(
        tab_count, samples // local_rows, lax.axis_size("col"), quarter_rows, col_width
    )
    arrived = joined_exchange(sectioned, COL_GRP, ("col", GRP), (2, 1), (4, 0))
    tables = jnp.take(arrived.reshape(-1, quarter_rows, emb_width), inverse, axis=0)
    mine_pre = lax.dynamic_slice_in_dim(bottom_pre, first_row, quarter_rows, 0)
    mine_out = lax.dynamic_slice_in_dim(bottom_out, first_row, quarter_rows, 0)
    mine_dense = lax.dynamic_slice_in_dim(dense_input, first_row, quarter_rows, 0)
    vectors = jnp.concatenate([mine_out[None], tables], axis=0)
    pair_values = interact(vectors)
    feature_part = jnp.concatenate([mine_out.astype(jnp.float32), pair_values.T], axis=1).astype(
        jnp.bfloat16
    )
    features = gather_directly(feature_part, "col", 0)
    hidden_pre = jnp.dot(features, top_weight, preferred_element_type=jnp.float32)
    hidden = jax.nn.silu(hidden_pre).astype(jnp.bfloat16)
    logits = over_copies(jnp.dot(hidden, out_weight, preferred_element_type=jnp.float32), "col")
    dlogit = (jax.nn.sigmoid(logits) - labels.astype(jnp.float32)) / local_rows
    grad_out_part = jnp.dot(hidden.astype(jnp.float32).T, dlogit, precision=lax.Precision.HIGHEST)
    out_delta = (
        dlogit[:, None] * out_weight.astype(jnp.float32)[None, :] * silu_slope(hidden_pre)
    ).astype(jnp.bfloat16)
    grad_top_part = lax.dot_general(
        features, out_delta, (((0,), (0,)), ((), ())), preferred_element_type=jnp.float32
    )
    grad_top, grad_out = (
        scatter_pairs(grad_top_part, ("grp_0", "grp_1", "grp_2"), "grp_3", 1),
        scatter_pairs(grad_out_part, ("grp_0", "grp_1", "grp_2"), "grp_3", 0),
    )
    delta_rows = lax.slice_in_dim(out_delta, 0, quarter_rows * lax.axis_size("col"), axis=0)
    dfeatures = sum_at_owner(
        lax.dot_general(
            delta_rows, top_weight, (((1,), (1,)), ((), ())), preferred_element_type=jnp.float32
        ),
        "col",
        0,
    )
    dpairs = dfeatures[:, emb_width:].astype(jnp.bfloat16)
    dvectors = spread(dpairs, vectors)
    dbottom = (dfeatures[:, :emb_width] + dvectors[0]) * silu_slope(mine_pre)
    bottom_part = jnp.dot(
        mine_dense.astype(jnp.float32).T, dbottom, precision=lax.Precision.HIGHEST
    )
    dtables = jnp.take(dvectors[1:], table_slot, axis=0)
    grad_bottom = over_pieces(bottom_part, COL_GRP)
    sectioned_back = dtables.astype(jnp.bfloat16).reshape(
        dtables.shape[0], 1, 1, quarter_rows, emb_width
    )
    returned = joined_exchange(sectioned_back, COL_GRP, ("col", GRP), (4, 0), (2, 1))
    dpooled = returned.reshape(tab_count, samples, col_width)
    dpooled_blocks = jnp.transpose(
        dpooled.reshape(tab_count, nblocks, stride, col_width), (1, 0, 2, 3)
    )

    def accumulate(running, inputs):
        counts = count_block(inputs[0], inputs[1], uniq_count)
        return (
            running
            + jnp.einsum("tbu,tbc->tuc", counts, inputs[2], preferred_element_type=jnp.float32),
            None,
        )

    grad_rows, _ = lax.scan(
        accumulate,
        jnp.zeros((tab_count, uniq_count, col_width), jnp.float32),
        (index_blocks, length_blocks, dpooled_blocks),
    )
    return (logits, grad_top, grad_out, grad_bottom, grad_rows)


def solution(mesh):
    torus = Mesh(
        mesh.devices.reshape(mesh.shape["col"], 4, 2, 4, 2),
        ("col", "grp_0", "grp_1", "grp_2", "grp_3"),
    )
    return jax.shard_map(
        body,
        mesh=torus,
        in_specs=(
            P(GRP, None, "col"),
            P(GRP, None, None),
            P(GRP, None),
            P(),
            P(GRP, None),
            P(),
            P(None, "col"),
            P("col"),
            P(GRP),
        ),
        out_specs=(P(GRP), P(None, COL_GRP), P(COL_GRP), P(), P(GRP, None, "col")),
        check_vma=False,
    )
```

profile of v0, /device:TPU:4, one launch (start us, length us, event | category | flops | bytes accessed | tf_op | source)
XLA Modules:
  0.0 645.5 jit_solution(4349524137017782892)
XLA Ops:
  8.0 26.5 %while.21 = (s32[]{:T(128)}, bf16[8,1,1024,64]{2,3,1,0:T(8,128)(2,1)S(1)}, s32[8,1,1024]{2,1,0:T(1,128)}, s32[8,1,4,1024]{3,2,1,0:T(4,128)}, bf16[1,256,64]{1,2,0:T(8,128)(2,1)}, /*index=5*/s32[]{:T(128)}) while((s32[]{:T(128)}, bf16[8,1,1024,64]{2,3,1,0:T(8,128)(2,1)S(1)}, s32[8,1,1024]{2,1,0:T(1,128)}, s32[8,1,4,1024]{3,2,1,0:T(4,128)}, ...), condition=%wide.region_2.3_spmd, body=%wide.region_1.2_spmd.sunk | while | flops 38871040 | bytes 258137 | solution.py:139
  9.6 1.8 fusion.96
  12.9 1.8 fusion.96
  16.2 1.8 fusion.96
  19.5 1.8 fusion.96
  22.8 1.8 fusion.96
  26.1 1.8 fusion.96
  29.4 1.8 fusion.96
  32.7 1.8 fusion.96
  34.6 1.8 copy.136
  36.4 3.3 copy.163
  39.7 4.7 reshape.771
  44.4 14.7 %all-to-all-start = ((bf16[256,2,1024]{2,1,0:T(2,128)(2,1)}), bf16[256,2,1024]{2,1,0:T(2,128)(2,1)S(1)}, u32[]{:S(2)}, u32[]{:S(2)}) async-start(bf16[256,2,1024]{2,1,0:T(2,128)(2,1)} %reshape.771), calls=%async_computation | async-start | bytes 2097152 | tf_op jit(solution)/shard_map/all_to_all | solution.py:30
  60.0 2.0 sort.17
  64.0 25.3 %all-to-all-done = bf16[256,2,1024]{2,1,0:T(2,128)(2,1)S(1)} async-done(((bf16[256,2,1024]{2,1,0:T(2,128)(2,1)}), bf16[256,2,1024]{2,1,0:T(2,128)(2,1)S(1)}, u32[]{:S(2)}, u32[]{:S(2)}) %all-to-all-start) | async-done | bytes 1048608 | tf_op jit(solution)/shard_map/all_to_all | solution.py:30
  89.3 2.2 reshape.772
  91.5 5.6 copy.180
  97.1 3.5 reshape_reshape_reshape.3
  100.6 1.6 gather_fusion
  102.2 1.9 copy_select_fusion
  106.4 1.4 copy.142
  108.9 1.5 copy.143
  110.4 5.5 gather_fusion.1
  118.1 3.7 all-to-all-start.1
  121.8 16.8 %all-to-all-done.1 = bf16[4,32,2336]{2,1,0:T(8,128)(2,1)S(1)} async-done(((bf16[4,32,2336]{2,1,0:T(8,128)(2,1)}), bf16[4,32,2336]{2,1,0:T(8,128)(2,1)S(1)}, u32[]{:S(2)}, u32[]{:S(2)}) %all-to-all-start.1) | async-done | bytes 598048 | tf_op jit(solution)/shard_map/all_to_all | solution.py:37
  140.0 3.2 all-to-all-start.2
  143.2 5.4 all-to-all-done.2
  150.2 3.0 convolution_bitcast_fusion.1
  153.3 7.0 %reshape.712 = f32[32,2,2336,8]{2,1,0,3:T(2,128)} reshape(f32[64,2336,8]{1,0,2:T(8,128)} %convolution_bitcast_fusion.1) | data formatting | bytes 9568256 | tf_op jit(solution)/shard_map/reshape | solution.py:54
  160.3 7.5 %copy.149 = f32[2,32,2336,8]{2,3,1,0:T(8,128)} copy(f32[2,32,2336,8]{2,0,1,3:T(2,128)} %bitcast.179) | data formatting | bytes 9568256 | tf_op jit(solution)/shard_map/transpose | solution.py:54
  169.4 30.8 %all_to_all.26 = f32[4,32,2336]{2,1,0:T(8,128)S(1)} all-to-all(f32[4,32,2336]{2,1,0:T(8,128)S(1)} %bitcast.189), channel_id=1, replica_groups=mesh['col'=4,'grp_0'=4,'grp_1'=2,'grp_2'=4,'grp_3'=2] {'col'}, dimensions={0} | all-to-all | bytes 2392064 | tf_op jit(solution)/shard_map/all_to_all | solution.py:61
  200.7 10.4 %scatter_custom_fusion = bf16[4225,32]{1,0:T(8,128)(2,1)S(1)} fusion(s32[2080]{0:T(1024)S(1)} %copy-done.7, bf16[2080,32]{1,0:T(8,128)(2,1)S(1)} %copy.152, bf16[]{:T(256)} %constant.89.clone.1), kind=kCustom, calls=%fused_computation.71 | custom fusion | bytes 270402 | tf_op jit(solution)/shard_map/scatter | solution.py:103
  213.1 1.9 fusion.34
  215.7 1.4 copy-done.2
  217.2 1.6 convolution_bitcast_fusion.3
  218.8 1.7 slice.62
  221.1 1.9 gather.16
  223.0 5.0 copy.156
  228.0 3.0 fusion.33
  231.1 3.5 copy.165
  234.6 2.0 reshape.773
  236.7 7.3 %all-to-all-start.4 = ((bf16[256,2,1024]{2,1,0:T(2,128)(2,1)}), bf16[256,2,1024]{2,1,0:T(2,128)(2,1)S(1)}, u32[]{:S(2)}, u32[]{:S(2)}) async-start(bf16[256,2,1024]{2,1,0:T(2,128)(2,1)} %reshape.773), calls=%async_computation.5 | async-start | bytes 2097152 | tf_op jit(solution)/shard_map/all_to_all | solution.py:30
  245.4 115.2 %all-reduce.1 = f32[32,8]{0,1:T(8,128)S(1)} all-reduce(f32[32,8]{0,1:T(8,128)S(1)} %copy.168), channel_id=6, replica_groups=mesh['col'=4,'grp_0'=4,'grp_1'=2,'grp_2'=4,'grp_3'=2] {'grp_0','grp_1','..., use_global_device_ids=true, to_apply=%region_7.8.clone | all-reduce | flops 256 | bytes 2048
  363.3 3.1 copy.166
  366.3 4.9 copy.159
  371.3 18.7 %while.22 = (s32[]{:T(128)}, f32[1,256,64]{1,2,0:T(8,128)S(1)}, s32[8,1,1024]{2,1,0:T(1,128)}, s32[8,1,4,1024]{3,2,1,0:T(4,128)}, bf16[8,1,1024,64]{3,2,1,0:T(8,128)(2,1)S(1)}, /*index=5*/s32[]{:T(128)}, s32[]{:T(128)}) while((s32[]{:T(128)}, f32[1,256,64]{1,2,0:T(8,128)S(1)}, s32[8,1,1024]{2,1,0:T(1,128)}, ...), condition=%wide.region_12.13_spmd.clone, body=%wide.region_11.12_spmd.clone.sunk | while | flops 38838272 | bytes 487531 | solution.py:208
  390.0 245.3 %all-gather.4.cloned.1.call-done = f32[256,13,256]{2,1,0:T(8,128)} async-done(((f32[1,13,256]{2,1,0:T(8,128)}), f32[256,13,256]{2,1,0:T(8,128)}) %all-gather.4.cloned.1.call-update) | async-done | bytes 3407888 | tf_op jit(solution)/shard_map/all_gather | solution.py:66
  635.3 3.1 reduce_sum.29
  (151 shorter events, 50.8 us)
Async XLA Ops:
  8.0 130.7 %copy-start = (bf16[2336,512]{1,0:T(8,128)(2,1)S(1)}, bf16[2336,512]{1,0:T(8,128)(2,1)}, u32[]{:S(2)}) copy-start(bf16[2336,512]{1,0:T(8,128)(2,1)} %param.23) | copy-start | bytes 7176196
  39.7 19.4 %copy-start.8 = (bf16[13,256]{1,0:T(8,128)(2,1)S(1)}, bf16[13,256]{1,0:T(8,128)(2,1)}, u32[]{:S(2)}) copy-start(bf16[13,256]{1,0:T(8,128)(2,1)} %param.22) | copy-start | bytes 19972
  39.7 19.4 %copy-start.9 = (bf16[128,13]{0,1:T(8,128)(2,1)S(1)}, bf16[128,13]{0,1:T(8,128)(2,1)}, u32[]{:S(2)}) copy-start(bf16[128,13]{0,1:T(8,128)(2,1)} %param.21) | copy-start | bytes 9988
  39.7 20.3 %copy-start.14 = (s32[64]{0:T(128)S(1)}, s32[64]{0:T(128)}, u32[]{:S(2)}) copy-start(s32[64]{0:T(128)} %param.20) | copy-start | bytes 772
  39.7 22.9 %copy-start.7 = (s32[2080]{0:T(1024)S(1)}, s32[2080]{0:T(1024)}, u32[]{:S(2)}) copy-start(s32[2080]{0:T(1024)} %constant.101) | copy-start | bytes 24964
  44.4 44.9 %all-to-all-start = ((bf16[256,2,1024]{2,1,0:T(2,128)(2,1)}), bf16[256,2,1024]{2,1,0:T(2,128)(2,1)S(1)}, u32[]{:S(2)}, u32[]{:S(2)}) async-start(bf16[256,2,1024]{2,1,0:T(2,128)(2,1)} %reshape.771), calls=%async_computation | async-start | bytes 2097152 | tf_op jit(solution)/shard_map/all_to_all | solution.py:30
  59.3 0.7 copy-start.4
  60.0 44.0 %copy-start.5 = (bf16[1,32,256]{2,0,1:T(2,128)(2,1)}, bf16[1,32,256]{2,0,1:T(2,128)(2,1)S(1)}, u32[]{:S(2)}) copy-start(bf16[1,32,256]{2,0,1:T(2,128)(2,1)S(1)} %copy.141) | copy-start | bytes 49156
  104.1 1.0 copy-start.3
  116.0 5.9 copy-start.11
  118.1 20.5 %all-to-all-start.1 = ((bf16[4,32,2336]{2,1,0:T(8,128)(2,1)}), bf16[4,32,2336]{2,1,0:T(8,128)(2,1)S(1)}, u32[]{:S(2)}, u32[]{:S(2)}) async-start(bf16[4,32,2336]{2,1,0:T(8,128)(2,1)} %broadcast_in_dim.95), calls=%async_computation.1 | async-start | bytes 1245184 | tf_op jit(solution)/shard_map/all_to_all | solution.py:37
  138.7 10.0 %copy-start.18 = (s32[128]{0:T(128)S(1)}, s32[128]{0:T(128)}, u32[]{:S(2)}) copy-start(s32[128]{0:T(128)} %param.25) | copy-start | bytes 1540
  140.0 8.7 %all-to-all-start.2 = ((f32[4,1,128]{2,1,0:T(1,128)}), f32[4,1,128]{2,1,0:T(1,128)S(1)}, u32[]{:S(2)}, u32[]{:S(2)}) async-start(f32[4,1,128]{2,1,0:T(1,128)} %broadcast_in_dim.96), calls=%async_computation.2 | async-start | bytes 4096 | tf_op jit(solution)/shard_map/all_to_all | solution.py:37
  143.2 101.5 %reduce-scatter.12.cloned.1.call-start = ((), (), s32[]{:S(2)}) async-start(), calls=%async_computation.10 | async-start | bytes 49152
  148.7 0.5 copy-start.17
  148.7 1.3 copy-start.15
  149.9 221.3 %reduce-scatter.10.cloned.1.call-start = ((), (), s32[]{:S(2)}) async-start(), calls=%async_computation.8 | async-start | bytes 7471104 | tf_op jit(solution)/shard_map/reduce_scatter | solution.py:55
  167.8 0.7 copy-start.16
  167.8 467.4 %all-gather.4.cloned.1.call-start = ((), (), s32[]{:S(2)}) async-start(), calls=%async_computation.9 | async-start | bytes 4210688 | tf_op jit(solution)/shard_map/all_gather | solution.py:66
  200.6 12.5 %copy-start.6 = (bf16[1,32,256]{2,0,1:T(2,128)(2,1)S(1)}, bf16[1,32,256]{2,0,1:T(2,128)(2,1)}, u32[]{:S(2)}) copy-start(bf16[1,32,256]{2,0,1:T(2,128)(2,1)} %copy-done.5) | copy-start | bytes 49156
  215.0 2.2 copy-start.10
  215.0 3.8 copy-start.13
  215.7 1.5 copy-start.2
  223.0 5.0 copy-start.12
  234.6 9.4 %copy-start.20 = (u32[256]{0:T(256)S(1)}, u32[256]{0:T(256)}, u32[]{:S(2)}) copy-start(u32[256]{0:T(256)} %constant.105) | copy-start | bytes 3076
  236.7 125.4 %all-to-all-start.4 = ((bf16[256,2,1024]{2,1,0:T(2,128)(2,1)}), bf16[256,2,1024]{2,1,0:T(2,128)(2,1)S(1)}, u32[]{:S(2)}, u32[]{:S(2)}) async-start(bf16[256,2,1024]{2,1,0:T(2,128)(2,1)} %reshape.773), calls=%async_computation.5 | async-start | bytes 2097152 | tf_op jit(solution)/shard_map/all_to_all | solution.py:30
  244.0 394.4 %reduce-scatter.14.cloned.1.call-start = ((), (), s32[]{:S(2)}) async-start(), calls=%async_computation.11 | async-start | bytes 2568192
  390.0 248.4 %copy-start.19 = (f32[1,256,64]{1,2,0:T(8,128)}, f32[1,256,64]{1,2,0:T(8,128)S(1)}, u32[]{:S(2)}) copy-start(f32[1,256,64]{1,2,0:T(8,128)S(1)} %get-tuple-element.59) | copy-start | bytes 196612
  390.0 248.4 %copy-start.1 = (bf16[2336,512]{1,0:T(8,128)(2,1)S(1)}, bf16[2336,512]{1,0:T(8,128)(2,1)}, u32[]{:S(2)}) copy-start(bf16[2336,512]{1,0:T(8,128)(2,1)} %param.23) | copy-start | bytes 7176196
Sparse Core Ops, SparseCore 0:
  150.1 7.9 reduce-scatter.11
  168.0 13.3 reduce-scatter.9
  371.4 217.9 reduce-scatter.13
Sparse Core Ops, SparseCore 1:
  218.8 416.4 all-gather.3
where the time goes:
time: 649 us; the launch traced here: 646 us
  waiting for transfers between devices  293 us (45%)
  blocking collectives  146 us (22%)
  local copies, waits for them, and re-layouts  106 us (16%)
  matrix products  31.7 us (5%)
  starting transfers between devices  29 us (4%)
  other arithmetic  23.8 us (4%)
  between operations  15.7 us (2%)
    all_gather x1, waiting for transfers between devices, over_pieces(): pieces = lax.all_gather(x, axis)  245 us
    unnamed x1, blocking collectives  115 us
    all_to_all x1, blocking collectives, sum_at_owner(): pieces = lax.all_to_all(cut_along(x, dim, peers), axis, 0, 0, tiled=True)  30.8 us
    all_to_all x2, waiting for transfers between devices, joined_exchange(): lax.all_to_all(pieces, axis, split_axis=0, concat_axis=0, tiled=True)  25.3 us
    all_to_all x2, waiting for transfers between devices, sent_to_all(): return lax.all_to_all(copies, axis, split_axis=0, concat_axis=0, tiled=True)  22.2 us
    all_to_all x2, starting transfers between devices, joined_exchange(): lax.all_to_all(pieces, axis, split_axis=0, concat_axis=0, tiled=True)  22 us
    unnamed x50, local copies, waits for them, and re-layouts  16.2 us
    dot_general x8, matrix products, pool_one(): jnp.einsum('tbu,tuc->tbc', counts, table_rows, preferred_element_type=jnp...  14.8 us
  transfers between devices with their start and end apart: 8, of which 4 were waited for; matrix products, arithmetic and copies ran while one was open for 14% of the time, Pallas kernels for 0%

commit v1 on v0

v1 whole, which is shorter than its diff:
```python
import jax
import jax.numpy as jnp
import numpy as np
from jax import lax
from jax.experimental import pallas as pl
from jax.experimental.pallas import tpu as pltpu
from jax.sharding import Mesh
from jax.sharding import PartitionSpec as P

COL_GRP = ("col", "grp_0", "grp_1", "grp_2", "grp_3")
GRP = ("grp_0", "grp_1", "grp_2", "grp_3")
F32 = jnp.float32
BF16 = jnp.bfloat16

TAB = 64
ROWS = 16
LANES = 128
HALF = 64
EMB = 256
FEAT = 2336
WIDE = 2432
STEP = 8


def pieces():
    found = [(-1, 0, TAB, EMB)]
    place = EMB + TAB
    for row in range(TAB - 1):
        found.append((row, row + 1, TAB - 1 - row, place))
        place += TAB - 1 - row
    return found


def parts_of(place, count):
    found = []
    for tile in range(place // LANES, (place + count - 1) // LANES + 1):
        first = max(place, tile * LANES) - tile * LANES
        end = min(place + count, (tile + 1) * LANES) - tile * LANES
        found.append((tile, first, end))
    return found


def lane_iota(rows):
    return lax.broadcasted_iota(jnp.int32, (rows, LANES), 1)


def low_lanes(rows):
    return lane_iota(rows) < HALF


def turned(x, shift):
    shift %= LANES
    return x if shift == 0 else pltpu.roll(x, shift, 1)


def dot_t(a, b):
    return lax.dot_general(a, b, (((1,), (1,)), ((), ())), preferred_element_type=F32)


def pool_kernel(index_ref, length_ref, rows_ref, out_ref, weights, counted):
    @pl.when(pl.program_id(0) == 0)
    def _():
        weights[...] = jnp.zeros_like(weights)
        weights[0:HALF, 0:256] = rows_ref[0]
        weights[HALF:LANES, 256:512] = rows_ref[0]

    values = lax.broadcasted_iota(jnp.int32, (LANES, 256), 1)
    slots = lax.broadcasted_iota(jnp.int32, (8, LANES), 0)
    for group in range(STEP):
        lanes = slice(group * LANES, (group + 1) * LANES)
        index = index_ref[0, :, lanes]
        index = jnp.concatenate([index, index], axis=0)
        ids = jnp.where(slots < length_ref[0:1, lanes], index, -1).T
        counts = jnp.zeros((LANES, 256), F32)
        for slot in range(4):
            counts = counts + jnp.where(ids[:, slot : slot + 1] == values, 1.0, 0.0)
        counts = counts.astype(BF16)
        counted[group * HALF : (group + 1) * HALF, 0:256] = counts[0:HALF]
        counted[group * HALF : (group + 1) * HALF, 256:512] = counts[HALF:LANES]
    pooled = dot_t(counted[...], weights[...]).astype(BF16)
    for group in range(STEP):
        for peer in range(4):
            first = group * HALF + peer * ROWS
            out_ref[peer, group] = pooled[first : first + ROWS]


def pool(pool_index, bag_length, rows):
    return pl.pallas_call(
        pool_kernel,
        grid=(TAB // STEP,),
        in_specs=[
            pl.BlockSpec((1, 4, STEP * LANES), lambda i: (0, 0, i)),
            pl.BlockSpec((1, STEP * LANES), lambda i: (0, i)),
            pl.BlockSpec((1, HALF, 256), lambda i: (0, 0, 0)),
        ],
        out_specs=pl.BlockSpec((4, STEP, ROWS, LANES), lambda i: (0, i, 0, 0)),
        out_shape=jax.ShapeDtypeStruct((4, TAB, ROWS, LANES), BF16),
        scratch_shapes=[
            pltpu.VMEM((LANES, 512), BF16),
            pltpu.VMEM((STEP * HALF, 512), BF16),
        ],
        compiler_params=pltpu.CompilerParams(vmem_limit_bytes=12 << 20),
        name="pool",
    )(pool_index, bag_length, rows)


def packed_bottom(mine_ref):
    low = low_lanes(ROWS)
    tiles = []
    for pair in range(2):
        lanes = slice(pair * LANES, (pair + 1) * LANES)
        first, second = mine_ref[0:ROWS, lanes], mine_ref[ROWS : 2 * ROWS, lanes]
        tiles.append(jnp.where(low, first, turned(second, HALF)))
        tiles.append(jnp.where(low, turned(first, HALF), second))
    return jnp.concatenate(tiles, axis=1)


def interact_kernel(slot_ref, arrived_ref, mine_ref, out_ref, vectors_ref, spaced, gram, edge):
    def place(table, carry):
        start = pl.multiple_of(slot_ref[table] * ROWS, ROWS)
        for part in range(4):
            spaced[part, pl.ds(start, ROWS), :] = arrived_ref[part, table].astype(F32)
        return carry

    lax.fori_loop(0, TAB, place, 0, unroll=8)
    bottom = packed_bottom(mine_ref)
    low = jnp.concatenate([low_lanes(TAB)] * 4, axis=1)
    for row in range(ROWS):
        vectors = jnp.concatenate(
            [spaced[part, pl.ds(row, TAB, stride=ROWS), :] for part in range(4)], axis=1
        )
        narrow = vectors.astype(BF16)
        vectors_ref[row] = narrow
        right = jnp.concatenate(
            [jnp.where(low, vectors, 0.0), jnp.where(low, 0.0, vectors)], axis=0
        ).astype(BF16)
        extra = jnp.broadcast_to(bottom[row : row + 1], (ROWS, 512)).astype(BF16)
        product = dot_t(jnp.concatenate([narrow, extra], axis=0), right)
        gram[pl.ds(row, TAB, stride=ROWS), :] = product[0:TAB]
        edge[row : row + 1, :] = product[TAB : TAB + 1]

    lane = lane_iota(ROWS)
    for half in range(2):
        where = slice(half * ROWS, (half + 1) * ROWS)
        out_ref[where, 0:EMB] = mine_ref[where, :].astype(BF16)
        tile, filled = EMB // LANES, jnp.zeros((ROWS, LANES), F32)
        for row, start, count, spot in pieces():
            source = edge[...] if row < 0 else gram[row * ROWS : (row + 1) * ROWS, :]
            moved = turned(source, spot - start - half * HALF)
            for at, first, end in parts_of(spot, count):
                if at != tile:
                    out_ref[where, tile * LANES : (tile + 1) * LANES] = filled.astype(BF16)
                    tile, filled = at, jnp.zeros((ROWS, LANES), F32)
                filled = jnp.where((lane >= first) & (lane < end), moved, filled)
        out_ref[where, tile * LANES : (tile + 1) * LANES] = filled.astype(BF16)


def whole(shape):
    return pl.BlockSpec(shape, lambda *_: (0,) * len(shape))


def interact(table_slot, arrived, mine):
    return pl.pallas_call(
        interact_kernel,
        in_specs=[
            pl.BlockSpec(memory_space=pltpu.SMEM),
            pl.BlockSpec(memory_space=pltpu.VMEM),
            pl.BlockSpec(memory_space=pltpu.VMEM),
        ],
        out_specs=[pl.BlockSpec(memory_space=pltpu.VMEM)] * 2,
        out_shape=[
            jax.ShapeDtypeStruct((2 * ROWS, WIDE), BF16),
            jax.ShapeDtypeStruct((ROWS, TAB, 512), BF16),
        ],
        scratch_shapes=[
            pltpu.VMEM((4, TAB * ROWS, LANES), F32),
            pltpu.VMEM((TAB * ROWS, LANES), F32),
            pltpu.VMEM((ROWS, LANES), F32),
        ],
        compiler_params=pltpu.CompilerParams(vmem_limit_bytes=16 << 20),
        name="interact",
    )(table_slot, arrived, mine)


def top_kernel(f0, f1, f2, f3, weight_ref, out_weight_ref, all_ref, z_ref, partial_ref, delta_ref, hidden_ref):
    for part, ref in enumerate((f0, f1, f2, f3)):
        all_ref[part * 32 : (part + 1) * 32, :] = ref[...]
    weight = weight_ref[...]
    pre = jnp.dot(all_ref[:, 0:FEAT], weight, preferred_element_type=F32)
    sigma = jax.nn.sigmoid(pre)
    hidden = (pre * sigma).astype(BF16)
    slope = sigma * (1.0 + pre * (1.0 - sigma))
    out_weight = out_weight_ref[0:1, :]
    delta = (out_weight * slope).astype(BF16)
    hidden_ref[...] = hidden
    delta_ref[...] = delta
    partial_ref[...] = dot_t(jnp.broadcast_to(out_weight, (16, 512)).astype(BF16), hidden)[0:8]
    z = dot_t(delta, weight).astype(BF16)
    for part in range(4):
        z_ref[part, :, 0:FEAT] = z[part * 32 : (part + 1) * 32]
        z_ref[part, :, FEAT:WIDE] = jnp.zeros((32, WIDE - FEAT), BF16)


def top(parts, top_weight, out_weight):
    return pl.pallas_call(
        top_kernel,
        in_specs=[pl.BlockSpec(memory_space=pltpu.VMEM)] * 6,
        out_specs=[pl.BlockSpec(memory_space=pltpu.VMEM)] * 5,
        out_shape=[
            jax.ShapeDtypeStruct((128, WIDE), BF16),
            jax.ShapeDtypeStruct((4, 32, WIDE), BF16),
            jax.ShapeDtypeStruct((8, LANES), F32),
            jax.ShapeDtypeStruct((128, 512), BF16),
            jax.ShapeDtypeStruct((128, 512), BF16),
        ],
        compiler_params=pltpu.CompilerParams(vmem_limit_bytes=24 << 20),
        name="top",
    )(*parts, top_weight, out_weight)


def weight_grad_kernel(p0, p1, p2, p3, labels_ref, all_ref, delta_ref, hidden_ref, grad_ref, logit_ref, dlogit_ref):
    logits = (p0[...] + turned(p2[...], 64)) + (turned(p1[...], 32) + turned(p3[...], 96))
    logit_ref[...] = logits
    dlogit = (jax.nn.sigmoid(logits) - labels_ref[0:1, :]) * (1.0 / 128.0)
    dlogit_ref[...] = dlogit
    column = dlogit.T[:, 0:1]
    delta = (delta_ref[...].astype(F32) * column).astype(BF16)
    last = WIDE - LANES
    grad_ref[:, 0:last] = lax.dot_general(
        delta, all_ref[:, 0:last], (((0,), (0,)), ((), ())), preferred_element_type=F32
    ).astype(BF16)
    lane = lane_iota(128)
    coarse = column.astype(BF16).astype(F32)
    spots = jnp.where(lane == 32, coarse, jnp.where(lane == 33, column - coarse, 0.0)).astype(BF16)
    grad_ref[:, last:WIDE] = lax.dot_general(
        jnp.concatenate([delta, hidden_ref[...]], axis=0),
        jnp.concatenate([all_ref[:, last:WIDE], spots], axis=0),
        (((0,), (0,)), ((), ())),
        preferred_element_type=F32,
    ).astype(BF16)


def weight_grad(partials, labels, features, delta, hidden):
    return pl.pallas_call(
        weight_grad_kernel,
        in_specs=[pl.BlockSpec(memory_space=pltpu.VMEM)] * 8,
        out_specs=[pl.BlockSpec(memory_space=pltpu.VMEM)] * 3,
        out_shape=[
            jax.ShapeDtypeStruct((512, WIDE), BF16),
            jax.ShapeDtypeStruct((8, LANES), F32),
            jax.ShapeDtypeStruct((8, LANES), F32),
        ],
        compiler_params=pltpu.CompilerParams(vmem_limit_bytes=24 << 20),
        name="weight_grad",
    )(*partials, labels, features, delta, hidden)


def spread_kernel(
    slot_ref, z0, z1, z2, z3, dlogit_ref, vectors_ref, mine_ref, slope_ref, dense_ref,
    back_ref, bottom_ref, dfeat, upper, edge, right, dvec, dedge,
):
    column = dlogit_ref[...].T[0:32, 0:1]
    summed = z0[...].astype(F32) + z1[...].astype(F32) + z2[...].astype(F32) + z3[...].astype(F32)
    dfeat[...] = summed * column
    lane = lane_iota(ROWS)
    for row, start, count, spot in pieces():
        filled = jnp.zeros((ROWS, LANES), F32)
        for half in range(2):
            for at, first, end in parts_of(spot, count):
                source = dfeat[half * ROWS : (half + 1) * ROWS, at * LANES : (at + 1) * LANES]
                moved = turned(source, start + half * HALF - spot)
                shift = start + half * HALF - spot + at * LANES
                inside = (lane >= first + shift) & (lane < end + shift)
                filled = jnp.where(inside, moved, filled)
        filled = filled.astype(BF16).astype(F32)
        if row < 0:
            edge[...] = filled
        else:
            upper[row * ROWS : (row + 1) * ROWS, :] = filled
    upper[(TAB - 1) * ROWS :, :] = jnp.zeros((ROWS, LANES), F32)
    right[...] = jnp.zeros_like(right)
    bottom = packed_bottom(mine_ref)
    low = low_lanes(TAB)
    low_wide = jnp.concatenate([low] * 4, axis=1)
    low_few = jnp.concatenate([low_lanes(16)] * 4, axis=1)
    top_row = lax.broadcasted_iota(jnp.int32, (16, 512), 0) == 0
    for row in range(ROWS):
        half = upper[pl.ds(row, TAB, stride=ROWS), :]
        zeroth = jnp.broadcast_to(edge[row : row + 1, :], (TAB, LANES))
        flipped = jnp.concatenate([half, zeroth], axis=0).T
        first, second = flipped[0:TAB], turned(flipped[TAB : 2 * TAB], HALF)
        whole_matrix = half + jnp.where(low, first, second)
        edges = jnp.where(low, second, first)
        left = jnp.concatenate(
            [
                jnp.concatenate([whole_matrix, edges], axis=1),
                jnp.concatenate([zeroth[0:16], jnp.zeros((16, LANES), F32)], axis=1),
            ],
            axis=0,
        ).astype(BF16)
        vectors = vectors_ref[row].astype(F32)
        right[0:TAB, :] = jnp.where(low_wide, vectors, 0.0).astype(BF16)
        right[TAB : 2 * TAB, :] = jnp.where(low_wide, 0.0, vectors).astype(BF16)
        own = jnp.broadcast_to(bottom[row : row + 1], (16, 512))
        right[128:144, :] = jnp.where(top_row & ~low_few, own, 0.0).astype(BF16)
        right[192:208, :] = jnp.where(top_row & low_few, own, 0.0).astype(BF16)
        product = jnp.dot(left, right[...], preferred_element_type=F32)
        for part in range(4):
            lanes = slice(part * LANES, (part + 1) * LANES)
            dvec[part, pl.ds(row, TAB, stride=ROWS), :] = product[0:TAB, lanes]
        dedge[row : row + 1, :] = product[TAB : TAB + 1]

    def place(table, carry):
        start = pl.multiple_of(slot_ref[table] * ROWS, ROWS)
        for part in range(4):
            back_ref[part, table] = dvec[part, pl.ds(start, ROWS), :].astype(BF16)
        return carry

    lax.fori_loop(0, TAB, place, 0, unroll=8)
    low = low_lanes(ROWS)
    tiles = [dedge[:, part * LANES : (part + 1) * LANES] for part in range(4)]
    own_rows = [
        jnp.concatenate(
            [jnp.where(low, tiles[2 * p], turned(tiles[2 * p + 1], HALF)) for p in range(2)], axis=1
        ),
        jnp.concatenate(
            [jnp.where(low, turned(tiles[2 * p], HALF), tiles[2 * p + 1]) for p in range(2)], axis=1
        ),
    ]
    dbottom = (dfeat[:, 0:EMB] + jnp.concatenate(own_rows, axis=0)) * slope_ref[...]
    bottom_ref[...] = lax.dot_general(
        dense_ref[...],
        dbottom,
        (((0,), (0,)), ((), ())),
        precision=lax.Precision.HIGHEST,
        preferred_element_type=F32,
    )


def spread(table_slot, zs, dlogit, vectors, mine, slope, dense):
    return pl.pallas_call(
        spread_kernel,
        in_specs=[pl.BlockSpec(memory_space=pltpu.SMEM)]
        + [pl.BlockSpec(memory_space=pltpu.VMEM)] * 9,
        out_specs=[pl.BlockSpec(memory_space=pltpu.VMEM)] * 2,
        out_shape=[
            jax.ShapeDtypeStruct((4, TAB, ROWS, LANES), BF16),
            jax.ShapeDtypeStruct((16, EMB), F32),
        ],
        scratch_shapes=[
            pltpu.VMEM((2 * ROWS, WIDE), F32),
            pltpu.VMEM((TAB * ROWS, LANES), F32),
            pltpu.VMEM((ROWS, LANES), F32),
            pltpu.VMEM((256, 512), BF16),
            pltpu.VMEM((4, TAB * ROWS, LANES), F32),
            pltpu.VMEM((ROWS, 512), F32),
        ],
        compiler_params=pltpu.CompilerParams(vmem_limit_bytes=16 << 20),
        name="spread",
    )(table_slot, *zs, dlogit, vectors, mine, slope, dense)


def row_grad_kernel(index_ref, length_ref, back_ref, out_ref, total, counted, moved):
    step = pl.program_id(0)

    @pl.when(step == 0)
    def _():
        total[...] = jnp.zeros_like(total)

    values = lax.broadcasted_iota(jnp.int32, (256, LANES), 0)
    low = low_lanes(HALF)
    for group in range(STEP):
        lanes = slice(group * LANES, (group + 1) * LANES)
        length = length_ref[0:1, lanes]
        counts = jnp.zeros((256, LANES), F32)
        for slot in range(4):
            ids = jnp.where(slot < length, index_ref[0, slot : slot + 1, lanes], -1)
            counts = counts + jnp.where(ids == values, 1.0, 0.0)
        counted[:, lanes] = counts.astype(BF16)
        rows = jnp.concatenate([back_ref[peer, group].astype(F32) for peer in range(4)], axis=0)
        moved[group * LANES : group * LANES + HALF, :] = jnp.where(low, rows, 0.0).astype(BF16)
        moved[group * LANES + HALF : (group + 1) * LANES, :] = jnp.where(low, 0.0, rows).astype(BF16)
    total[...] += jnp.dot(counted[...], moved[...], preferred_element_type=F32)

    @pl.when(step == pl.num_programs(0) - 1)
    def _():
        flipped = total[...].T
        out_ref[0] = flipped[0:HALF] + flipped[HALF:LANES]


def row_grad(pool_index, bag_length, back):
    return pl.pallas_call(
        row_grad_kernel,
        grid=(TAB // STEP,),
        in_specs=[
            pl.BlockSpec((1, 4, STEP * LANES), lambda i: (0, 0, i)),
            pl.BlockSpec((1, STEP * LANES), lambda i: (0, i)),
            pl.BlockSpec((4, STEP, ROWS, LANES), lambda i: (0, i, 0, 0)),
        ],
        out_specs=pl.BlockSpec((1, HALF, 256), lambda i: (0, 0, 0)),
        out_shape=jax.ShapeDtypeStruct((1, HALF, 256), F32),
        scratch_shapes=[
            pltpu.VMEM((256, LANES), F32),
            pltpu.VMEM((256, STEP * LANES), BF16),
            pltpu.VMEM((STEP * LANES, LANES), BF16),
        ],
        compiler_params=pltpu.CompilerParams(vmem_limit_bytes=12 << 20),
        name="row_grad",
    )(pool_index, bag_length, back)


def shifted(x, axis, shift):
    size = lax.axis_size(axis)
    return lax.ppermute(x, axis, [(i, (i + shift) % size) for i in range(size)])


def exchange(x, axes):
    return lax.all_to_all(x, axes, split_axis=0, concat_axis=0, tiled=True)


def summed_over(x, axis):
    if lax.axis_size(axis) == 2:
        return x + shifted(x, axis, 1)
    return (x + shifted(x, axis, 2)) + (shifted(x, axis, 1) + shifted(x, axis, 3))


def silu_slope(values):
    sigma = jax.nn.sigmoid(values)
    return sigma * (1.0 + values * (1.0 - sigma))


def picked(x, which):
    return lax.dynamic_index_in_dim(x, which, 1, keepdims=False)


def body(
    table_rows,
    pool_index,
    bag_length,
    table_slot,
    dense_input,
    bottom_weight,
    top_weight,
    out_weight,
    labels,
):
    me = lax.axis_index("col")
    rows = jnp.transpose(table_rows, (0, 2, 1))
    pooled = pool(pool_index, bag_length, rows)
    arrived = exchange(pooled.reshape(4 * TAB, ROWS, LANES), COL_GRP).reshape(4, TAB, ROWS, LANES)

    dense_mine = lax.dynamic_index_in_dim(
        dense_input.reshape(2, 4, ROWS, -1), me, 1, keepdims=False
    ).reshape(2 * ROWS, -1)
    mine_pre = jnp.dot(dense_mine, bottom_weight, preferred_element_type=F32)
    mine = jax.nn.silu(mine_pre).astype(BF16).astype(F32)
    mine_slope = silu_slope(mine_pre)
    dense_wide = jnp.pad(dense_mine.astype(F32), ((0, 0), (0, 16 - dense_mine.shape[1])))
    order = (me - jnp.arange(4)) % 4
    labels_rel = jnp.take(
        jnp.transpose(labels.reshape(2, 4, ROWS), (1, 0, 2)), order, axis=0
    ).reshape(1, LANES).astype(F32)
    out_weight_row = out_weight.astype(F32).reshape(1, -1)

    part, vectors = interact(table_slot, arrived, mine)
    parts = [part] + [shifted(part, "col", away) for away in (1, 2, 3)]
    features, z, partial, delta, hidden = top(parts, top_weight, out_weight_row)
    partials = [partial] + [shifted(partial, "col", away) for away in (1, 2, 3)]
    zs = [z[0]] + [shifted(z[away], "col", -away) for away in (1, 2, 3)]
    grad, logits_rel, dlogit = weight_grad(partials, labels_rel, features, delta, hidden)
    back, bottom_part = spread(table_slot, zs, dlogit, vectors, mine, mine_slope, dense_wide)
    returned = exchange(back.reshape(4 * TAB, ROWS, LANES), COL_GRP).reshape(4, TAB, ROWS, LANES)
    grad_rows = jnp.transpose(row_grad(pool_index, bag_length, returned), (0, 2, 1))

    logits = jnp.take(logits_rel[0].reshape(4, 2, ROWS), order, axis=0)
    logits = jnp.transpose(logits, (1, 0, 2)).reshape(LANES)

    core, upper = lax.axis_index("grp_3"), lax.axis_index("grp_1")
    grad = grad.reshape(32, 2, 8, WIDE)
    other = shifted(picked(grad, 1 - core), "grp_3", 1)
    grad = picked(grad, core).astype(F32) + other.astype(F32)
    grad = jnp.transpose(grad.astype(BF16).reshape(4, 2, 4, 8, WIDE), (0, 2, 1, 3, 4))
    grad = exchange(grad.reshape(16, 16, WIDE), ("grp_0", "grp_2"))
    grad = jnp.sum(grad.astype(F32), axis=0).reshape(1, 2, 8, WIDE)
    other = shifted(picked(grad, 1 - upper).astype(BF16), "grp_1", 1)
    grad = (picked(grad, upper) + other.astype(F32))[0]
    grad_top = jnp.transpose(grad[:, 0:FEAT])
    grad_out = grad[:, FEAT] + grad[:, FEAT + 1]

    bottom = bottom_part
    for axis in ("grp_3", "col", "grp_0", "grp_2", "grp_1"):
        bottom = summed_over(bottom, axis)
    grad_bottom = bottom[0 : bottom_weight.shape[0]]
    return (logits, grad_top, grad_out, grad_bottom, grad_rows)


def solution(mesh):
    torus = Mesh(
        mesh.devices.reshape(mesh.shape["col"], 4, 2, 4, 2),
        ("col", "grp_0", "grp_1", "grp_2", "grp_3"),
    )
    return jax.shard_map(
        body,
        mesh=torus,
        in_specs=(
            P(GRP, None, "col"),
            P(GRP, None, None),
            P(GRP, None),
            P(),
            P(GRP, None),
            P(),
            P(None, "col"),
            P("col"),
            P(GRP),
        ),
        out_specs=(P(GRP), P(None, COL_GRP), P(COL_GRP), P(), P(GRP, None, "col")),
        check_vma=False,
    )
```

time: 649 us -> 196 us (0.30)
  waiting for transfers between devices: 293 us -> 82.2 us
  blocking collectives: 146 us -> 0 us
  local copies, waits for them, and re-layouts: 106 us -> 14.6 us
  starting transfers between devices: 29 us -> 65.3 us
  matrix products: 31.7 us -> 0.14 us
  Pallas kernels: 0 us -> 26.8 us
  other arithmetic: 23.8 us -> 3.33 us
  between operations: 15.7 us -> 0.87 us
    all_gather x1 -> x0, waiting for transfers between devices: 245 us -> none  [over_pieces(): pieces = lax.all_gather(x, axis)]
    unnamed x1 -> x0, blocking collectives: 115 us -> none
    ppermute x0 -> x22, waiting for transfers between devices: none -> 52.4 us  [shifted(): return lax.ppermute(x, axis, [(i, (i + shift) % size) for i in range(size)])]
    ppermute x0 -> x22, starting transfers between devices: none -> 37 us  [shifted(): return lax.ppermute(x, axis, [(i, (i + shift) % size) for i in range(size)])]
    dot_general x25 -> x1, matrix products: 31.7 us -> 0.14 us  [body(): mine_pre = jnp.dot(dense_mine, bottom_weight, preferred_element_type=F32)]
    all_to_all x1 -> x0, blocking collectives: 30.8 us -> none  [sum_at_owner(): pieces = lax.all_to_all(cut_along(x, dim, peers), axis, 0, 0, tiled=True)]
    pallas_call x0 -> x6, Pallas kernels: none -> 26.8 us  [the longest x1 9.55 us: pool(): pl.pallas_call(pool_kernel, grid=(TAB // STEP,), in_specs=[pl.BlockSpec((...]
    reshape x7 -> x4, local copies, waits for them, and re-layouts: 20 us -> 0.78 us  [the longest x1 0.6 us: body(): logits = jnp.transpose(logits, (1, 0, 2)).reshape(LANES)]
  transfers between devices with their start and end apart: 8 -> 25, of which waited for: 4 -> 15; matrix products, arithmetic and copies ran while one was open for 14% -> 2% of each run, Pallas kernels for 0% -> 6%
where the time goes in v1:
time: 196 us; the launch traced here: 193 us
  waiting for transfers between devices  82.2 us (42%)
  starting transfers between devices  65.3 us (33%)
  Pallas kernels  26.8 us (14%)
  local copies, waits for them, and re-layouts  14.6 us (7%)
  other arithmetic  3.33 us (2%)
    ppermute x22, waiting for transfers between devices, shifted(): return lax.ppermute(x, axis, [(i, (i + shift) % size) for i in range(size)])  52.4 us
    ppermute x22, starting transfers between devices, shifted(): return lax.ppermute(x, axis, [(i, (i + shift) % size) for i in range(size)])  37 us
    all_to_all x3, waiting for transfers between devices, exchange(): return lax.all_to_all(x, axes, split_axis=0, concat_axis=0, tiled=True)  29.8 us
    all_to_all x3, starting transfers between devices, exchange(): return lax.all_to_all(x, axes, split_axis=0, concat_axis=0, tiled=True)  28.3 us
    pallas_call x1, Pallas kernels, pool(): pl.pallas_call(pool_kernel, grid=(TAB // STEP,), in_specs=[pl.BlockSpec((...  9.55 us
    unnamed x43, local copies, waits for them, and re-layouts  9.38 us
    pallas_call x1, Pallas kernels, row_grad(): pl.pallas_call(row_grad_kernel, grid=(TAB // STEP,), in_specs=[pl.BlockSp...  7.09 us
    pallas_call x1, Pallas kernels, spread(): pl.pallas_call(spread_kernel, in_specs=[pl.BlockSpec(memory_space=pltpu.S...  4.17 us
  transfers between devices with their start and end apart: 25, of which 15 were waited for; matrix products, arithmetic and copies ran while one was open for 2% of the time, Pallas kernels for 6%

profile of v1, /device:TPU:4, one launch (start us, length us, event | category | flops | bytes accessed | tf_op | source)
XLA Modules:
  0.0 193.3 jit_solution(9520364502942570110)
XLA Ops:
  0.7 0.9 copy-done.8
  1.6 0.8 copy-done.14
  3.1 9.5 %pool.1 = bf16[4,64,16,128]{3,2,1,0:T(8,128)(2,1)} custom-call(s32[1,4,8192]{2,1,0:T(4,128)S(1)} %copy-done.8, s32[1,8192]{1,0:T(1,128)S(1)} %copy-done.14, bf16[1,64,256]{2,1,0:T(8,128)(2,1)S(1)} %bitcast.54), custom_call_target="tpu_custom_call" | custom-call | tf_op jit(solution)/shard_map/pool/pallas_call | solution.py:88
  12.6 14.7 %all-to-all-start = ((bf16[256,16,128]{2,1,0:T(8,128)(2,1)}), bf16[256,16,128]{2,1,0:T(8,128)(2,1)S(1)}, u32[]{:S(2)}, u32[]{:S(2)}) async-start(bf16[256,16,128]{2,1,0:T(8,128)(2,1)} %bitcast.1), calls=%async_computation | async-start | bytes 2097152 | tf_op jit(solution)/shard_map/all_to_all | solution.py:418
  27.7 29.8 %all-to-all-done = bf16[256,16,128]{2,1,0:T(8,128)(2,1)S(1)} async-done(((bf16[256,16,128]{2,1,0:T(8,128)(2,1)}), bf16[256,16,128]{2,1,0:T(8,128)(2,1)S(1)}, u32[]{:S(2)}, u32[]{:S(2)}) %all-to-all-start) | async-done | bytes 1048608 | tf_op jit(solution)/shard_map/all_to_all | solution.py:418
  57.5 2.6 %interact.1 = (bf16[32,2432]{1,0:T(8,128)(2,1)}, bf16[16,64,512]{2,1,0:T(8,128)(2,1)S(1)}) custom-call(s32[64]{0:T(128)S(1)} %copy-done.17, bf16[4,64,16,128]{3,2,1,0:T(8,128)(2,1)S(1)} %bitcast.51, f32[32,256]{1,0:T(8,128)S(1)} %get-tuple-element.34.mine_ref), custom_call_target="tpu_custom_call" | custom-call | tf_op jit(solution)/shard_map/interact/pallas_call | solution.py:163
  60.1 1.0 copy-done.2
  61.1 1.1 collective-permute-start
  62.2 1.0 collective-permute-start.1
  63.2 2.4 %collective-permute-start.2 = (bf16[32,2432]{1,0:T(8,128)(2,1)}, bf16[32,2432]{1,0:T(8,128)(2,1)S(1)}, u32[]{:S(2)}, u32[]{:S(2)}) collective-permute-start(bf16[32,2432]{1,0:T(8,128)(2,1)} %get-tuple-element.17.f0), channel_id=1, source_target_pairs={{0,192},{64,0},{128,64},{192,128},{1,193},{65,1},{129,65},{193,129... | collective-permute-start | bytes 466952 | tf_op jit(solution)/shard_map/ppermute | solution.py:414
  66.3 3.9 %collective-permute-done.f1 = bf16[32,2432]{1,0:T(8,128)(2,1)S(1)} collective-permute-done((bf16[32,2432]{1,0:T(8,128)(2,1)}, bf16[32,2432]{1,0:T(8,128)(2,1)S(1)}, u32[]{:S(2)}, u32[]{:S(2)}) %collective-permute-start) | collective-permute-done | bytes 155680 | tf_op jit(solution)/shard_map/ppermute | solution.py:414
  70.2 5.7 %collective-permute-done.1.f2 = bf16[32,2432]{1,0:T(8,128)(2,1)S(1)} collective-permute-done((bf16[32,2432]{1,0:T(8,128)(2,1)}, bf16[32,2432]{1,0:T(8,128)(2,1)S(1)}, u32[]{:S(2)}, u32[]{:S(2)}) %collective-permute-start.1) | collective-permute-done | bytes 155680 | tf_op jit(solution)/shard_map/ppermute | solution.py:414
  75.9 2.3 %top.1 = (bf16[128,2432]{1,0:T(8,128)(2,1)S(1)}, bf16[4,32,2432]{2,1,0:T(8,128)(2,1)S(1)}, f32[8,128]{1,0:T(8,128)S(1)}, bf16[128,512]{1,0:T(8,128)(2,1)S(1)}, bf16[128,512]{1,0:T(8,128)(2,1)S(1)}) custom-call(bf16[32,2432]{1,0:T(8,128)(2,1)} %get-tuple-element.17.f0, bf16[32,2432]{1,0:T(8,128)(2,1)S(1)} %collective-permute-done.f1, ...), custom_call_target="tpu_custom_call" | custom-call | tf_op jit(solution)/shard_map/top/pallas_call | solution.py:205
  78.2 0.8 copy-done.4
  79.0 0.8 copy-done.6
  81.1 3.7 %collective-permute-start.3 = (f32[8,128]{1,0:T(8,128)S(1)}, f32[8,128]{1,0:T(8,128)S(1)}, u32[]{:S(2)}, u32[]{:S(2)}) collective-permute-start(f32[8,128]{1,0:T(8,128)S(1)} %get-tuple-element.18.p0), channel_id=1, source_target_pairs={{0,64},{64,128},{128,192},{192,0},{1,65},{65,129},{129,193},{193,1... | collective-permute-start | bytes 12296 | tf_op jit(solution)/shard_map/ppermute | solution.py:414
  84.8 2.4 %collective-permute-start.5 = (f32[8,128]{1,0:T(8,128)S(1)}, f32[8,128]{1,0:T(8,128)S(1)}, u32[]{:S(2)}, u32[]{:S(2)}) collective-permute-start(f32[8,128]{1,0:T(8,128)S(1)} %get-tuple-element.18.p0), channel_id=1, source_target_pairs={{0,192},{64,0},{128,64},{192,128},{1,193},{65,1},{129,65},{193,129... | collective-permute-start | bytes 12296 | tf_op jit(solution)/shard_map/ppermute | solution.py:414
  87.4 2.0 %collective-permute-done.4.p2 = f32[8,128]{1,0:T(8,128)S(1)} collective-permute-done((f32[8,128]{1,0:T(8,128)S(1)}, f32[8,128]{1,0:T(8,128)S(1)}, u32[]{:S(2)}, u32[]{:S(2)}) %collective-permute-start.4) | collective-permute-done | bytes 4128 | tf_op jit(solution)/shard_map/ppermute | solution.py:414
  89.3 1.1 copy-done.7
  90.4 0.9 copy-done.11
  91.3 0.9 copy-done.13
  92.2 1.1 weight_grad.1
  93.3 1.2 dynamic-slice_bitcast_fusion
  94.5 3.3 %collective-permute-done.6 = bf16[32,8,2432]{2,1,0:T(8,128)(2,1)} collective-permute-done((bf16[32,8,2432]{2,1,0:T(8,128)(2,1)}, bf16[32,8,2432]{2,1,0:T(8,128)(2,1)}, u32[]{:S(2)}, u32[]{:S(2)}) %collective-permute-start.6) | collective-permute-done | bytes 1245216 | tf_op jit(solution)/shard_map/ppermute | solution.py:414
  97.8 1.6 fusion
  99.4 1.2 copy.23
  100.6 5.1 %all-to-all-start.1 = ((bf16[16,16,2432]{2,1,0:T(8,128)(2,1)}), bf16[16,16,2432]{2,1,0:T(8,128)(2,1)S(1)}, u32[]{:S(2)}, u32[]{:S(2)}) async-start(bf16[16,16,2432]{2,1,0:T(8,128)(2,1)} %bitcast.56), calls=%async_computation.1 | async-start | bytes 2490368 | tf_op jit(solution)/shard_map/all_to_all | solution.py:418
  106.5 3.2 %collective-permute-start.8 = (bf16[32,2432]{1,0:T(8,128)(2,1)S(1)}, bf16[32,2432]{1,0:T(8,128)(2,1)S(1)}, u32[]{:S(2)}, u32[]{:S(2)}) collective-permute-start(bf16[32,2432]{1,0:T(8,128)(2,1)S(1)} %get-tuple-element.31), channel_id=1, source_target_pairs={{0,192},{64,0},{128,64},{192,128},{1,193},{65,1},{129,65},{193,129... | collective-permute-start | bytes 466952 | tf_op jit(solution)/shard_map/ppermute | solution.py:414
  110.0 4.7 %collective-permute-done.10.z3 = bf16[32,2432]{1,0:T(8,128)(2,1)S(1)} collective-permute-done((bf16[32,2432]{1,0:T(8,128)(2,1)S(1)}, bf16[32,2432]{1,0:T(8,128)(2,1)S(1)}, u32[]{:S(2)}, u32[]{:S(2)}) %collective-permute-start.10) | collective-permute-done | bytes 155680 | tf_op jit(solution)/shard_map/ppermute | solution.py:414
  114.6 0.9 collective-permute-done.8.z1
  115.6 7.9 %collective-permute-done.9.z2 = bf16[32,2432]{1,0:T(8,128)(2,1)S(1)} collective-permute-done((bf16[32,2432]{1,0:T(8,128)(2,1)S(1)}, bf16[32,2432]{1,0:T(8,128)(2,1)S(1)}, u32[]{:S(2)}, u32[]{:S(2)}) %collective-permute-start.9) | collective-permute-done | bytes 155680 | tf_op jit(solution)/shard_map/ppermute | solution.py:414
  123.5 4.2 %spread.1 = (bf16[4,64,16,128]{3,2,1,0:T(8,128)(2,1)}, f32[16,256]{1,0:T(8,128)S(1)}) custom-call(s32[64]{0:T(128)S(1)} %copy-done.17, bf16[32,2432]{1,0:T(8,128)(2,1)S(1)} %get-tuple-element.32.z0, bf16[32,2432]{1,0:T(8,128)(2,1)S(1)} %collective-permute-done.8.z1, bf16[32,2432]{1,0:T(8,128)(2,1)S(1)} %collective-permute-done.9.z2, ...), custom_call_target="tpu_custom_call" | custom-call | tf_op jit(solution)/shard_map/spread/pallas_call | solution.py:341
  127.6 8.5 %all-to-all-start.2 = ((bf16[256,16,128]{2,1,0:T(8,128)(2,1)}), bf16[256,16,128]{2,1,0:T(8,128)(2,1)S(1)}, u32[]{:S(2)}, u32[]{:S(2)}) async-start(bf16[256,16,128]{2,1,0:T(8,128)(2,1)} %bitcast.23), calls=%async_computation.2 | async-start | bytes 2097152 | tf_op jit(solution)/shard_map/all_to_all | solution.py:418
  136.4 1.1 collective-permute-done.11
  137.5 2.8 %collective-permute-start.12 = (f32[16,256]{1,0:T(8,128)S(1)}, f32[16,256]{1,0:T(8,128)S(1)}, u32[]{:S(2)}, u32[]{:S(2)}) collective-permute-start(f32[16,256]{1,0:T(8,128)S(1)} %add.124), channel_id=1, source_target_pairs={{0,128},{64,192},{128,0},{192,64},{1,129},{65,193},{129,1},{193,65... | collective-permute-start | bytes 49160 | tf_op jit(solution)/shard_map/ppermute | solution.py:414
  140.3 1.7 collective-permute-start.13
  142.0 2.1 %collective-permute-start.14 = (f32[16,256]{1,0:T(8,128)S(1)}, f32[16,256]{1,0:T(8,128)S(1)}, u32[]{:S(2)}, u32[]{:S(2)}) collective-permute-start(f32[16,256]{1,0:T(8,128)S(1)} %add.124), channel_id=1, source_target_pairs={{0,192},{64,0},{128,64},{192,128},{1,193},{65,1},{129,65},{193,129... | collective-permute-start | bytes 49160 | tf_op jit(solution)/shard_map/ppermute | solution.py:414
  144.1 16.7 %collective-permute-done.12 = f32[16,256]{1,0:T(8,128)S(1)} collective-permute-done((f32[16,256]{1,0:T(8,128)S(1)}, f32[16,256]{1,0:T(8,128)S(1)}, u32[]{:S(2)}, u32[]{:S(2)}) %collective-permute-start.12) | collective-permute-done | bytes 16416 | tf_op jit(solution)/shard_map/ppermute | solution.py:414
  162.1 2.0 %collective-permute-start.16 = (f32[16,256]{1,0:T(8,128)S(1)}, f32[16,256]{1,0:T(8,128)S(1)}, u32[]{:S(2)}, u32[]{:S(2)}) collective-permute-start(f32[16,256]{1,0:T(8,128)S(1)} %add_add_fusion.2), channel_id=1, source_target_pairs={{0,16},{16,32},{32,48},{48,0},{1,17},{17,33},{33,49},{49,1},{2,18}... | collective-permute-start | bytes 49160 | tf_op jit(solution)/shard_map/ppermute | solution.py:414
  165.0 1.7 collective-permute-done.15
  166.7 1.2 collective-permute-done.17
  167.9 3.3 %collective-permute-start.18 = (f32[16,256]{1,0:T(8,128)S(1)}, f32[16,256]{1,0:T(8,128)S(1)}, u32[]{:S(2)}, u32[]{:S(2)}) collective-permute-start(f32[16,256]{1,0:T(8,128)S(1)} %add_add_fusion.1), channel_id=1, source_target_pairs={{0,4},{2,6},{4,0},{6,2},{1,5},{3,7},{5,1},{7,3},{8,12},{10,14},{12... | collective-permute-start | bytes 49160 | tf_op jit(solution)/shard_map/ppermute | solution.py:414
  171.7 2.8 %collective-permute-start.20 = (f32[16,256]{1,0:T(8,128)S(1)}, f32[16,256]{1,0:T(8,128)S(1)}, u32[]{:S(2)}, u32[]{:S(2)}) collective-permute-start(f32[16,256]{1,0:T(8,128)S(1)} %add_add_fusion.1), channel_id=1, source_target_pairs={{0,6},{2,0},{4,2},{6,4},{1,7},{3,1},{5,3},{7,5},{8,14},{10,8},{12,... | collective-permute-start | bytes 49160 | tf_op jit(solution)/shard_map/ppermute | solution.py:414
  175.1 1.0 collective-permute-done.19
  176.2 4.8 %collective-permute-start.21 = (f32[16,256]{1,0:T(8,128)S(1)}, f32[16,256]{1,0:T(8,128)S(1)}, u32[]{:S(2)}, u32[]{:S(2)}) collective-permute-start(f32[16,256]{1,0:T(8,128)S(1)} %add_add_fusion), channel_id=1, source_target_pairs={{0,8},{8,0},{1,9},{9,1},{2,10},{10,2},{3,11},{11,3},{4,12},{12,4},... | collective-permute-start | bytes 49160 | tf_op jit(solution)/shard_map/ppermute | solution.py:414
  181.1 1.3 collective-permute-start.7
  182.5 1.8 collective-permute-done.21
  184.9 7.1 %row_grad.1 = f32[1,64,256]{2,1,0:T(8,128)} custom-call(s32[1,4,8192]{2,1,0:T(4,128)S(1)} %copy-done.9, s32[1,8192]{1,0:T(1,128)S(1)} %copy-done.15, bf16[4,64,16,128]{3,2,1,0:T(8,128)(2,1)S(1)} %bitcast.50), custom_call_target="tpu_custom_call" | custom-call | tf_op jit(solution)/shard_map/row_grad/pallas_call | solution.py:392
  (84 shorter events, 10.1 us)
Async XLA Ops:
  0.6 26.9 %copy-start = (bf16[13,256]{1,0:T(8,128)(2,1)S(1)}, bf16[13,256]{1,0:T(8,128)(2,1)}, u32[]{:S(2)}) copy-start(bf16[13,256]{1,0:T(8,128)(2,1)} %param.14) | copy-start | bytes 19972
  0.6 0.9 copy-start.8
  1.6 0.8 copy-start.14
  2.3 0.8 copy-start.16
  12.6 14.7 %copy-start.18 = (bf16[128,13]{0,1:T(8,128)(2,1)S(1)}, bf16[128,13]{0,1:T(8,128)(2,1)}, u32[]{:S(2)}) copy-start(bf16[128,13]{0,1:T(8,128)(2,1)} %param.13) | copy-start | bytes 9988
  12.6 44.9 %copy-start.17 = (s32[64]{0:T(128)S(1)}, s32[64]{0:T(128)}, u32[]{:S(2)}) copy-start(s32[64]{0:T(128)} %slot_ref.3) | copy-start | bytes 772
  12.6 52.9 %copy-start.19 = (bf16[512]{0:T(512)(128)(2,1)S(1)}, bf16[512]{0:T(512)(128)(2,1)}, u32[]{:S(2)}) copy-start(bf16[512]{0:T(512)(128)(2,1)} %param.16) | copy-start | bytes 3076
  12.6 53.0 %copy-start.20 = (s32[128]{0:T(128)S(1)}, s32[128]{0:T(128)}, u32[]{:S(2)}) copy-start(s32[128]{0:T(128)} %param.17) | copy-start | bytes 1540
  12.6 63.3 %copy-start.1 = (bf16[2336,512]{1,0:T(8,128)(2,1)S(1)}, bf16[2336,512]{1,0:T(8,128)(2,1)}, u32[]{:S(2)}) copy-start(bf16[2336,512]{1,0:T(8,128)(2,1)} %weight_ref.1) | copy-start | bytes 7176196
  12.6 44.9 %all-to-all-start = ((bf16[256,16,128]{2,1,0:T(8,128)(2,1)}), bf16[256,16,128]{2,1,0:T(8,128)(2,1)S(1)}, u32[]{:S(2)}, u32[]{:S(2)}) async-start(bf16[256,16,128]{2,1,0:T(8,128)(2,1)} %bitcast.1), calls=%async_computation | async-start | bytes 2097152 | tf_op jit(solution)/shard_map/all_to_all | solution.py:418
  60.1 1.0 copy-start.2
  61.1 9.0 %collective-permute-start = (bf16[32,2432]{1,0:T(8,128)(2,1)}, bf16[32,2432]{1,0:T(8,128)(2,1)S(1)}, u32[]{:S(2)}, u32[]{:S(2)}) collective-permute-start(bf16[32,2432]{1,0:T(8,128)(2,1)} %get-tuple-element.17.f0), channel_id=1, source_target_pairs={{0,64},{64,128},{128,192},{192,0},{1,65},{65,129},{129,193},{193,1... | collective-permute-start | bytes 466952 | tf_op jit(solution)/shard_map/ppermute | solution.py:414
  62.2 13.7 %collective-permute-start.1 = (bf16[32,2432]{1,0:T(8,128)(2,1)}, bf16[32,2432]{1,0:T(8,128)(2,1)S(1)}, u32[]{:S(2)}, u32[]{:S(2)}) collective-permute-start(bf16[32,2432]{1,0:T(8,128)(2,1)} %get-tuple-element.17.f0), channel_id=1, source_target_pairs={{0,128},{64,192},{128,0},{192,64},{1,129},{65,193},{129,1},{193,65... | collective-permute-start | bytes 466952 | tf_op jit(solution)/shard_map/ppermute | solution.py:414
  63.2 12.7 %collective-permute-start.2 = (bf16[32,2432]{1,0:T(8,128)(2,1)}, bf16[32,2432]{1,0:T(8,128)(2,1)S(1)}, u32[]{:S(2)}, u32[]{:S(2)}) collective-permute-start(bf16[32,2432]{1,0:T(8,128)(2,1)} %get-tuple-element.17.f0), channel_id=1, source_target_pairs={{0,192},{64,0},{128,64},{192,128},{1,193},{65,1},{129,65},{193,129... | collective-permute-start | bytes 466952 | tf_op jit(solution)/shard_map/ppermute | solution.py:414
  78.2 0.8 copy-start.4
  79.0 0.8 copy-start.6
  79.8 0.7 copy-start.10
  80.5 0.6 copy-start.12
  81.1 6.2 %collective-permute-start.3 = (f32[8,128]{1,0:T(8,128)S(1)}, f32[8,128]{1,0:T(8,128)S(1)}, u32[]{:S(2)}, u32[]{:S(2)}) collective-permute-start(f32[8,128]{1,0:T(8,128)S(1)} %get-tuple-element.18.p0), channel_id=1, source_target_pairs={{0,64},{64,128},{128,192},{192,0},{1,65},{65,129},{129,193},{193,1... | collective-permute-start | bytes 12296 | tf_op jit(solution)/shard_map/ppermute | solution.py:414
  84.8 4.5 %collective-permute-start.4 = (f32[8,128]{1,0:T(8,128)S(1)}, f32[8,128]{1,0:T(8,128)S(1)}, u32[]{:S(2)}, u32[]{:S(2)}) collective-permute-start(f32[8,128]{1,0:T(8,128)S(1)} %get-tuple-element.18.p0), channel_id=1, source_target_pairs={{0,128},{64,192},{128,0},{192,64},{1,129},{65,193},{129,1},{193,65... | collective-permute-start | bytes 12296 | tf_op jit(solution)/shard_map/ppermute | solution.py:414
  84.8 4.5 %collective-permute-start.5 = (f32[8,128]{1,0:T(8,128)S(1)}, f32[8,128]{1,0:T(8,128)S(1)}, u32[]{:S(2)}, u32[]{:S(2)}) collective-permute-start(f32[8,128]{1,0:T(8,128)S(1)} %get-tuple-element.18.p0), channel_id=1, source_target_pairs={{0,192},{64,0},{128,64},{192,128},{1,193},{65,1},{129,65},{193,129... | collective-permute-start | bytes 12296 | tf_op jit(solution)/shard_map/ppermute | solution.py:414
  89.3 1.1 copy-start.7
  90.4 0.9 copy-start.11
  91.3 0.9 copy-start.13
  94.5 3.3 %collective-permute-start.6 = (bf16[32,8,2432]{2,1,0:T(8,128)(2,1)}, bf16[32,8,2432]{2,1,0:T(8,128)(2,1)}, u32[]{:S(2)}, u32[]{:S(2)}) collective-permute-start(bf16[32,8,2432]{2,1,0:T(8,128)(2,1)} %dynamic-slice_bitcast_fusion), channel_id=1, source_target_pairs={{0,1},{1,0},{2,3},{3,2},{4,5},{5,4},{6,7},{7,6},{8,9},{9,8},{10,11... | collective-permute-start | bytes 3735560 | tf_op jit(solution)/shard_map/ppermute | solution.py:414
  100.6 5.2 %copy-start.5 = (bf16[4,32,2432]{2,1,0:T(8,128)(2,1)S(1)}, bf16[4,32,2432]{2,1,0:T(8,128)(2,1)}, u32[]{:S(2)}) copy-start(bf16[4,32,2432]{2,1,0:T(8,128)(2,1)} %copy-done.4) | copy-start | bytes 1867780
  100.6 27.0 %all-to-all-start.1 = ((bf16[16,16,2432]{2,1,0:T(8,128)(2,1)}), bf16[16,16,2432]{2,1,0:T(8,128)(2,1)S(1)}, u32[]{:S(2)}, u32[]{:S(2)}) async-start(bf16[16,16,2432]{2,1,0:T(8,128)(2,1)} %bitcast.56), calls=%async_computation.1 | async-start | bytes 2490368 | tf_op jit(solution)/shard_map/all_to_all | solution.py:418
  105.8 17.7 %copy-start.3 = (bf16[16,64,512]{2,1,0:T(8,128)(2,1)S(1)}, bf16[16,64,512]{2,1,0:T(8,128)(2,1)}, u32[]{:S(2)}) copy-start(bf16[16,64,512]{2,1,0:T(8,128)(2,1)} %copy-done.2) | copy-start | bytes 3145732
  105.8 8.8 %collective-permute-start.10 = (bf16[32,2432]{1,0:T(8,128)(2,1)S(1)}, bf16[32,2432]{1,0:T(8,128)(2,1)S(1)}, u32[]{:S(2)}, u32[]{:S(2)}) collective-permute-start(bf16[32,2432]{1,0:T(8,128)(2,1)S(1)} %get-tuple-element.29), channel_id=1, source_target_pairs={{0,64},{64,128},{128,192},{192,0},{1,65},{65,129},{129,193},{193,1... | collective-permute-start | bytes 466952 | tf_op jit(solution)/shard_map/ppermute | solution.py:414
  106.5 9.1 %collective-permute-start.8 = (bf16[32,2432]{1,0:T(8,128)(2,1)S(1)}, bf16[32,2432]{1,0:T(8,128)(2,1)S(1)}, u32[]{:S(2)}, u32[]{:S(2)}) collective-permute-start(bf16[32,2432]{1,0:T(8,128)(2,1)S(1)} %get-tuple-element.31), channel_id=1, source_target_pairs={{0,192},{64,0},{128,64},{192,128},{1,193},{65,1},{129,65},{193,129... | collective-permute-start | bytes 466952 | tf_op jit(solution)/shard_map/ppermute | solution.py:414
  109.7 13.7 %collective-permute-start.9 = (bf16[32,2432]{1,0:T(8,128)(2,1)S(1)}, bf16[32,2432]{1,0:T(8,128)(2,1)S(1)}, u32[]{:S(2)}, u32[]{:S(2)}) collective-permute-start(bf16[32,2432]{1,0:T(8,128)(2,1)S(1)} %get-tuple-element.30), channel_id=1, source_target_pairs={{0,128},{64,192},{128,0},{192,64},{1,129},{65,193},{129,1},{193,65... | collective-permute-start | bytes 466952 | tf_op jit(solution)/shard_map/ppermute | solution.py:414
  127.6 57.2 %all-to-all-start.2 = ((bf16[256,16,128]{2,1,0:T(8,128)(2,1)}), bf16[256,16,128]{2,1,0:T(8,128)(2,1)S(1)}, u32[]{:S(2)}, u32[]{:S(2)}) async-start(bf16[256,16,128]{2,1,0:T(8,128)(2,1)} %bitcast.23), calls=%async_computation.2 | async-start | bytes 2097152 | tf_op jit(solution)/shard_map/all_to_all | solution.py:418
  136.2 48.7 %copy-start.9 = (s32[1,4,8192]{2,1,0:T(4,128)S(1)}, s32[1,4,8192]{2,1,0:T(4,128)}, u32[]{:S(2)}) copy-start(s32[1,4,8192]{2,1,0:T(4,128)} %index_ref.3) | copy-start | bytes 393220
  136.2 48.7 %copy-start.15 = (s32[1,8192]{1,0:T(1,128)S(1)}, s32[1,8192]{1,0:T(1,128)}, u32[]{:S(2)}) copy-start(s32[1,8192]{1,0:T(1,128)} %length_ref.3) | copy-start | bytes 98308
  136.2 1.3 collective-permute-start.11
  137.5 23.3 %collective-permute-start.12 = (f32[16,256]{1,0:T(8,128)S(1)}, f32[16,256]{1,0:T(8,128)S(1)}, u32[]{:S(2)}, u32[]{:S(2)}) collective-permute-start(f32[16,256]{1,0:T(8,128)S(1)} %add.124), channel_id=1, source_target_pairs={{0,128},{64,192},{128,0},{192,64},{1,129},{65,193},{129,1},{193,65... | collective-permute-start | bytes 49160 | tf_op jit(solution)/shard_map/ppermute | solution.py:414
  140.3 21.1 %collective-permute-start.13 = (f32[16,256]{1,0:T(8,128)S(1)}, f32[16,256]{1,0:T(8,128)S(1)}, u32[]{:S(2)}, u32[]{:S(2)}) collective-permute-start(f32[16,256]{1,0:T(8,128)S(1)} %add.124), channel_id=1, source_target_pairs={{0,64},{64,128},{128,192},{192,0},{1,65},{65,129},{129,193},{193,1... | collective-permute-start | bytes 49160 | tf_op jit(solution)/shard_map/ppermute | solution.py:414
  142.0 19.4 %collective-permute-start.14 = (f32[16,256]{1,0:T(8,128)S(1)}, f32[16,256]{1,0:T(8,128)S(1)}, u32[]{:S(2)}, u32[]{:S(2)}) collective-permute-start(f32[16,256]{1,0:T(8,128)S(1)} %add.124), channel_id=1, source_target_pairs={{0,192},{64,0},{128,64},{192,128},{1,193},{65,1},{129,65},{193,129... | collective-permute-start | bytes 49160 | tf_op jit(solution)/shard_map/ppermute | solution.py:414
  161.4 5.3 %collective-permute-start.15 = (f32[16,256]{1,0:T(8,128)S(1)}, f32[16,256]{1,0:T(8,128)S(1)}, u32[]{:S(2)}, u32[]{:S(2)}) collective-permute-start(f32[16,256]{1,0:T(8,128)S(1)} %add_add_fusion.2), channel_id=1, source_target_pairs={{0,32},{16,48},{32,0},{48,16},{1,33},{17,49},{33,1},{49,17},{2,34}... | collective-permute-start | bytes 49160 | tf_op jit(solution)/shard_map/ppermute | solution.py:414
  162.1 4.6 %collective-permute-start.16 = (f32[16,256]{1,0:T(8,128)S(1)}, f32[16,256]{1,0:T(8,128)S(1)}, u32[]{:S(2)}, u32[]{:S(2)}) collective-permute-start(f32[16,256]{1,0:T(8,128)S(1)} %add_add_fusion.2), channel_id=1, source_target_pairs={{0,16},{16,32},{32,48},{48,0},{1,17},{17,33},{33,49},{49,1},{2,18}... | collective-permute-start | bytes 49160 | tf_op jit(solution)/shard_map/ppermute | solution.py:414
  164.1 3.8 %collective-permute-start.17 = (f32[16,256]{1,0:T(8,128)S(1)}, f32[16,256]{1,0:T(8,128)S(1)}, u32[]{:S(2)}, u32[]{:S(2)}) collective-permute-start(f32[16,256]{1,0:T(8,128)S(1)} %add_add_fusion.2), channel_id=1, source_target_pairs={{0,48},{16,0},{32,16},{48,32},{1,49},{17,1},{33,17},{49,33},{2,50}... | collective-permute-start | bytes 49160 | tf_op jit(solution)/shard_map/ppermute | solution.py:414
  167.9 7.2 %collective-permute-start.18 = (f32[16,256]{1,0:T(8,128)S(1)}, f32[16,256]{1,0:T(8,128)S(1)}, u32[]{:S(2)}, u32[]{:S(2)}) collective-permute-start(f32[16,256]{1,0:T(8,128)S(1)} %add_add_fusion.1), channel_id=1, source_target_pairs={{0,4},{2,6},{4,0},{6,2},{1,5},{3,7},{5,1},{7,3},{8,12},{10,14},{12... | collective-permute-start | bytes 49160 | tf_op jit(solution)/shard_map/ppermute | solution.py:414
  171.2 4.9 %collective-permute-start.19 = (f32[16,256]{1,0:T(8,128)S(1)}, f32[16,256]{1,0:T(8,128)S(1)}, u32[]{:S(2)}, u32[]{:S(2)}) collective-permute-start(f32[16,256]{1,0:T(8,128)S(1)} %add_add_fusion.1), channel_id=1, source_target_pairs={{0,2},{2,4},{4,6},{6,0},{1,3},{3,5},{5,7},{7,1},{8,10},{10,12},{12... | collective-permute-start | bytes 49160 | tf_op jit(solution)/shard_map/ppermute | solution.py:414
  171.7 4.5 %collective-permute-start.20 = (f32[16,256]{1,0:T(8,128)S(1)}, f32[16,256]{1,0:T(8,128)S(1)}, u32[]{:S(2)}, u32[]{:S(2)}) collective-permute-start(f32[16,256]{1,0:T(8,128)S(1)} %add_add_fusion.1), channel_id=1, source_target_pairs={{0,6},{2,0},{4,2},{6,4},{1,7},{3,1},{5,3},{7,5},{8,14},{10,8},{12,... | collective-permute-start | bytes 49160 | tf_op jit(solution)/shard_map/ppermute | solution.py:414
  176.2 8.1 %collective-permute-start.21 = (f32[16,256]{1,0:T(8,128)S(1)}, f32[16,256]{1,0:T(8,128)S(1)}, u32[]{:S(2)}, u32[]{:S(2)}) collective-permute-start(f32[16,256]{1,0:T(8,128)S(1)} %add_add_fusion), channel_id=1, source_target_pairs={{0,8},{8,0},{1,9},{9,1},{2,10},{10,2},{3,11},{11,3},{4,12},{12,4},... | collective-permute-start | bytes 49160 | tf_op jit(solution)/shard_map/ppermute | solution.py:414
  181.1 10.8 %collective-permute-start.7 = (bf16[1,8,2432]{2,1,0:T(8,128)(2,1)S(1)}, bf16[1,8,2432]{2,1,0:T(8,128)(2,1)S(1)}, u32[]{:S(2)}, u32[]{:S(2)}) collective-permute-start(bf16[1,8,2432]{2,1,0:T(8,128)(2,1)S(1)} %fusion.2), channel_id=1, source_target_pairs={{0,8},{8,0},{1,9},{9,1},{2,10},{10,2},{3,11},{11,3},{4,12},{12,4},... | collective-permute-start | bytes 116744 | tf_op jit(solution)/shard_map/ppermute | solution.py:414

commit v2 on v1

--- a/solution.py
+++ b/solution.py
@@ -1,11 +1,11 @@
 import jax
 import jax.numpy as jnp
-import numpy as np
 from jax import lax
 from jax.experimental import pallas as pl
 from jax.experimental.pallas import tpu as pltpu
 from jax.sharding import Mesh
 from jax.sharding import PartitionSpec as P
+
 
 COL_GRP = ("col", "grp_0", "grp_1", "grp_2", "grp_3")
 GRP = ("grp_0", "grp_1", "grp_2", "grp_3")
@@ -55,6 +55,14 @@
 
 def dot_t(a, b):
     return lax.dot_general(a, b, (((1,), (1,)), ((), ())), preferred_element_type=F32)
+
+
+def hbm(shape, dtype):
+    return pltpu.HBM(shape, dtype)
+
+
+def vmem_specs(count):
+    return [pl.BlockSpec(memory_space=pltpu.VMEM)] * count
 
 
 def pool_kernel(index_ref, length_ref, rows_ref, out_ref, weights, counted):
@@ -94,7 +102,7 @@
             pl.BlockSpec((1, HALF, 256), lambda i: (0, 0, 0)),
         ],
         out_specs=pl.BlockSpec((4, STEP, ROWS, LANES), lambda i: (0, i, 0, 0)),
-        out_shape=jax.ShapeDtypeStruct((4, TAB, ROWS, LANES), BF16),
+        out_shape=hbm((4, TAB, ROWS, LANES), BF16),
         scratch_shapes=[
             pltpu.VMEM((LANES, 512), BF16),
             pltpu.VMEM((STEP * HALF, 512), BF16),
@@ -155,10 +163,6 @@
         out_ref[where, tile * LANES : (tile + 1) * LANES] = filled.astype(BF16)
 
 
-def whole(shape):
-    return pl.BlockSpec(shape, lambda *_: (0,) * len(shape))
-
-
 def interact(table_slot, arrived, mine):
     return pl.pallas_call(
         interact_kernel,
@@ -170,7 +174,7 @@
         out_specs=[pl.BlockSpec(memory_space=pltpu.VMEM)] * 2,
         out_shape=[
             jax.ShapeDtypeStruct((2 * ROWS, WIDE), BF16),
-            jax.ShapeDtypeStruct((ROWS, TAB, 512), BF16),
+            hbm((ROWS, TAB, 512), BF16),
         ],
         scratch_shapes=[
             pltpu.VMEM((4, TAB * ROWS, LANES), F32),
@@ -182,7 +186,10 @@
     )(table_slot, arrived, mine)
 
 
-def top_kernel(f0, f1, f2, f3, weight_ref, out_weight_ref, all_ref, z_ref, partial_ref, delta_ref, hidden_ref):
+def top_kernel(
+    f0, f1, f2, f3, weight_ref, out_weight_ref,
+    all_ref, z0, z1, z2, z3, partial_ref, delta_ref, hidden_ref,
+):
     for part, ref in enumerate((f0, f1, f2, f3)):
         all_ref[part * 32 : (part + 1) * 32, :] = ref[...]
     weight = weight_ref[...]
@@ -196,29 +203,32 @@
     delta_ref[...] = delta
     partial_ref[...] = dot_t(jnp.broadcast_to(out_weight, (16, 512)).astype(BF16), hidden)[0:8]
     z = dot_t(delta, weight).astype(BF16)
-    for part in range(4):
-        z_ref[part, :, 0:FEAT] = z[part * 32 : (part + 1) * 32]
-        z_ref[part, :, FEAT:WIDE] = jnp.zeros((32, WIDE - FEAT), BF16)
+    for part, ref in enumerate((z0, z1, z2, z3)):
+        ref[:, 0:FEAT] = z[part * 32 : (part + 1) * 32]
+        ref[:, FEAT:WIDE] = jnp.zeros((32, WIDE - FEAT), BF16)
 
 
 def top(parts, top_weight, out_weight):
     return pl.pallas_call(
         top_kernel,
-        in_specs=[pl.BlockSpec(memory_space=pltpu.VMEM)] * 6,
-        out_specs=[pl.BlockSpec(memory_space=pltpu.VMEM)] * 5,
-        out_shape=[
-            jax.ShapeDtypeStruct((128, WIDE), BF16),
-            jax.ShapeDtypeStruct((4, 32, WIDE), BF16),
+        in_specs=vmem_specs(6),
+        out_specs=vmem_specs(8),
+        out_shape=[hbm((128, WIDE), BF16), hbm((32, WIDE), BF16)]
+        + [jax.ShapeDtypeStruct((32, WIDE), BF16)] * 3
+        + [
             jax.ShapeDtypeStruct((8, LANES), F32),
-            jax.ShapeDtypeStruct((128, 512), BF16),
-            jax.ShapeDtypeStruct((128, 512), BF16),
+            hbm((128, 512), BF16),
+            hbm((128, 512), BF16),
         ],
         compiler_params=pltpu.CompilerParams(vmem_limit_bytes=24 << 20),
         name="top",
     )(*parts, top_weight, out_weight)
 
 
-def weight_grad_kernel(p0, p1, p2, p3, labels_ref, all_ref, delta_ref, hidden_ref, grad_ref, logit_ref, dlogit_ref):
+def weight_grad_kernel(
+    core_ref, p0, p1, p2, p3, labels_ref, all_ref, delta_ref, hidden_ref,
+    own_ref, other_ref, logit_ref, dlogit_ref, grad,
+):
     logits = (p0[...] + turned(p2[...], 64)) + (turned(p1[...], 32) + turned(p3[...], 96))
     logit_ref[...] = logits
     dlogit = (jax.nn.sigmoid(logits) - labels_ref[0:1, :]) * (1.0 / 128.0)
@@ -226,33 +236,44 @@
     column = dlogit.T[:, 0:1]
     delta = (delta_ref[...].astype(F32) * column).astype(BF16)
     last = WIDE - LANES
-    grad_ref[:, 0:last] = lax.dot_general(
+    grad[:, 0:last] = lax.dot_general(
         delta, all_ref[:, 0:last], (((0,), (0,)), ((), ())), preferred_element_type=F32
-    ).astype(BF16)
+    )
     lane = lane_iota(128)
     coarse = column.astype(BF16).astype(F32)
     spots = jnp.where(lane == 32, coarse, jnp.where(lane == 33, column - coarse, 0.0)).astype(BF16)
-    grad_ref[:, last:WIDE] = lax.dot_general(
+    grad[:, last:WIDE] = lax.dot_general(
         jnp.concatenate([delta, hidden_ref[...]], axis=0),
         jnp.concatenate([all_ref[:, last:WIDE], spots], axis=0),
         (((0,), (0,)), ((), ())),
         preferred_element_type=F32,
-    ).astype(BF16)
-
-
-def weight_grad(partials, labels, features, delta, hidden):
+    )
+    core = core_ref[0]
+    for x in range(4):
+        for y in range(4):
+            for ref, which in ((own_ref, core), (other_ref, 1 - core)):
+                both = []
+                for z in range(2):
+                    first = pl.multiple_of((((x * 2 + z) * 4 + y) * 2 + which) * 8, 8)
+                    both.append(grad[pl.ds(first, 8), :])
+                ref[x * 4 + y] = jnp.concatenate(both, axis=0).astype(BF16)
+
+
+def weight_grad(core, partials, labels, features, delta, hidden):
     return pl.pallas_call(
         weight_grad_kernel,
-        in_specs=[pl.BlockSpec(memory_space=pltpu.VMEM)] * 8,
-        out_specs=[pl.BlockSpec(memory_space=pltpu.VMEM)] * 3,
+        in_specs=[pl.BlockSpec(memory_space=pltpu.SMEM)] + vmem_specs(8),
+        out_specs=vmem_specs(4),
         out_shape=[
-            jax.ShapeDtypeStruct((512, WIDE), BF16),
+            hbm((16, 16, WIDE), BF16),
+            hbm((16, 16, WIDE), BF16),
             jax.ShapeDtypeStruct((8, LANES), F32),
             jax.ShapeDtypeStruct((8, LANES), F32),
         ],
-        compiler_params=pltpu.CompilerParams(vmem_limit_bytes=24 << 20),
+        scratch_shapes=[pltpu.VMEM((512, WIDE), F32)],
+        compiler_params=pltpu.CompilerParams(vmem_limit_bytes=32 << 20),
         name="weight_grad",
-    )(*partials, labels, features, delta, hidden)
+    )(core, *partials, labels, features, delta, hidden)
 
 
 def spread_kernel(
@@ -344,7 +365,7 @@
         + [pl.BlockSpec(memory_space=pltpu.VMEM)] * 9,
         out_specs=[pl.BlockSpec(memory_space=pltpu.VMEM)] * 2,
         out_shape=[
-            jax.ShapeDtypeStruct((4, TAB, ROWS, LANES), BF16),
+            hbm((4, TAB, ROWS, LANES), BF16),
             jax.ShapeDtypeStruct((16, EMB), F32),
         ],
         scratch_shapes=[
@@ -414,14 +435,27 @@
     return lax.ppermute(x, axis, [(i, (i + shift) % size) for i in range(size)])
 
 
-def exchange(x, axes):
-    return lax.all_to_all(x, axes, split_axis=0, concat_axis=0, tiled=True)
+def exchange_all(x):
+    flat = x.reshape(4 * TAB, ROWS, LANES)
+    flat = lax.all_to_all(flat, COL_GRP, split_axis=0, concat_axis=0, tiled=True)
+    return flat.reshape(4, TAB, ROWS, LANES)
 
 
 def summed_over(x, axis):
     if lax.axis_size(axis) == 2:
         return x + shifted(x, axis, 1)
-    return (x + shifted(x, axis, 2)) + (shifted(x, axis, 1) + shifted(x, axis, 3))
+    others = [shifted(x, axis, shift) for shift in (1, 2, 3)]
+    return (x + others[1]) + (others[0] + others[2])
+
+
+def reduced_to(x, axis):
+    me = lax.axis_index(axis)
+    size = lax.axis_size(axis)
+    total = lax.dynamic_index_in_dim(x, me, 0, keepdims=False).astype(F32)
+    for shift in range(1, size):
+        block = lax.dynamic_index_in_dim(x, (me + shift) % size, 0, keepdims=False)
+        total = total + shifted(block.astype(BF16), axis, shift).astype(F32)
+    return total
 
 
 def silu_slope(values):
@@ -429,11 +463,7 @@
     return sigma * (1.0 + values * (1.0 - sigma))
 
 
-def picked(x, which):
-    return lax.dynamic_index_in_dim(x, which, 1, keepdims=False)
-
-
-def body(
+def step(
     table_rows,
     pool_index,
     bag_length,
@@ -444,10 +474,10 @@
     out_weight,
     labels,
 ):
-    me = lax.axis_index("col")
+    me, core = lax.axis_index("col"), lax.axis_index("grp_3")
     rows = jnp.transpose(table_rows, (0, 2, 1))
     pooled = pool(pool_index, bag_length, rows)
-    arrived = exchange(pooled.reshape(4 * TAB, ROWS, LANES), COL_GRP).reshape(4, TAB, ROWS, LANES)
+    arrived = exchange_all(pooled)
 
     dense_mine = lax.dynamic_index_in_dim(
         dense_input.reshape(2, 4, ROWS, -1), me, 1, keepdims=False
@@ -464,31 +494,28 @@
 
     part, vectors = interact(table_slot, arrived, mine)
     parts = [part] + [shifted(part, "col", away) for away in (1, 2, 3)]
-    features, z, partial, delta, hidden = top(parts, top_weight, out_weight_row)
+    features, *zs, partial, delta, hidden = top(parts, top_weight, out_weight_row)
+    zs = [zs[0]] + [shifted(zs[away], "col", -away) for away in (1, 2, 3)]
     partials = [partial] + [shifted(partial, "col", away) for away in (1, 2, 3)]
-    zs = [z[0]] + [shifted(z[away], "col", -away) for away in (1, 2, 3)]
-    grad, logits_rel, dlogit = weight_grad(partials, labels_rel, features, delta, hidden)
-    back, bottom_part = spread(table_slot, zs, dlogit, vectors, mine, mine_slope, dense_wide)
-    returned = exchange(back.reshape(4 * TAB, ROWS, LANES), COL_GRP).reshape(4, TAB, ROWS, LANES)
+    own, other, logits_rel, dlogit = weight_grad(
+        core.astype(jnp.int32).reshape(1), partials, labels_rel, features, delta, hidden
+    )
+    back, bottom = spread(table_slot, zs, dlogit, vectors, mine, mine_slope, dense_wide)
+    returned = exchange_all(back)
     grad_rows = jnp.transpose(row_grad(pool_index, bag_length, returned), (0, 2, 1))
 
     logits = jnp.take(logits_rel[0].reshape(4, 2, ROWS), order, axis=0)
     logits = jnp.transpose(logits, (1, 0, 2)).reshape(LANES)
 
-    core, upper = lax.axis_index("grp_3"), lax.axis_index("grp_1")
-    grad = grad.reshape(32, 2, 8, WIDE)
-    other = shifted(picked(grad, 1 - core), "grp_3", 1)
-    grad = picked(grad, core).astype(F32) + other.astype(F32)
-    grad = jnp.transpose(grad.astype(BF16).reshape(4, 2, 4, 8, WIDE), (0, 2, 1, 3, 4))
-    grad = exchange(grad.reshape(16, 16, WIDE), ("grp_0", "grp_2"))
-    grad = jnp.sum(grad.astype(F32), axis=0).reshape(1, 2, 8, WIDE)
-    other = shifted(picked(grad, 1 - upper).astype(BF16), "grp_1", 1)
-    grad = (picked(grad, upper) + other.astype(F32))[0]
+    other = shifted(other, "grp_3", 1)
+    grad = (own.astype(F32) + other.astype(F32)).astype(BF16).reshape(4, 64, WIDE)
+    grad = reduced_to(grad, "grp_0").reshape(4, 16, WIDE)
+    grad = reduced_to(grad, "grp_2").reshape(2, 8, WIDE)
+    grad = reduced_to(grad, "grp_1")
     grad_top = jnp.transpose(grad[:, 0:FEAT])
     grad_out = grad[:, FEAT] + grad[:, FEAT + 1]
 
-    bottom = bottom_part
-    for axis in ("grp_3", "col", "grp_0", "grp_2", "grp_1"):
+    for axis in ("grp_3", "grp_0", "grp_2", "col", "grp_1"):
         bottom = summed_over(bottom, axis)
     grad_bottom = bottom[0 : bottom_weight.shape[0]]
     return (logits, grad_top, grad_out, grad_bottom, grad_rows)
@@ -500,7 +527,7 @@
         ("col", "grp_0", "grp_1", "grp_2", "grp_3"),
     )
     return jax.shard_map(
-        body,
+        step,
         mesh=torus,
         in_specs=(
             P(GRP, None, "col"),

time: 196 us -> 201 us (1.026)
  waiting for transfers between devices: 82.2 us -> 75 us
  starting transfers between devices: 65.3 us -> 70.9 us
  local copies, waits for them, and re-layouts: 14.6 us -> 18.6 us
  Pallas kernels: 26.8 us -> 29.5 us
    ppermute x22 -> x28, starting transfers between devices: 37 us -> 46.4 us  [shifted(): return lax.ppermute(x, axis, [(i, (i + shift) % size) for i in range(size)])]
    ppermute x22 -> x28, waiting for transfers between devices: 52.4 us -> 45.2 us  [shifted(): return lax.ppermute(x, axis, [(i, (i + shift) % size) for i in range(size)])]
    unnamed x43 -> x55, local copies, waits for them, and re-layouts: 9.38 us -> 14.1 us
    all_to_all x3 -> x2, starting transfers between devices: 28.3 us -> 24.5 us  [exchange_all(): lax.all_to_all(flat, COL_GRP, split_axis=0, concat_axis=0, tiled=True)]
    all_to_all x3 -> x2, waiting for transfers between devices: 29.8 us -> 29.8 us  [exchange_all(): lax.all_to_all(flat, COL_GRP, split_axis=0, concat_axis=0, tiled=True)]
  transfers between devices with their start and end apart: 25 -> 30, of which waited for: 15 -> 13; matrix products, arithmetic and copies ran while one was open for 2% -> 5% of each run, Pallas kernels for 6% -> 2%
where the time goes in v2:
time: 201 us; the launch traced here: 200 us
  waiting for transfers between devices  75 us (37%)
  starting transfers between devices  70.9 us (35%)
  Pallas kernels  29.5 us (15%)
  local copies, waits for them, and re-layouts  18.6 us (9%)
  other arithmetic  5.04 us (3%)
    ppermute x28, starting transfers between devices, shifted(): return lax.ppermute(x, axis, [(i, (i + shift) % size) for i in range(size)])  46.4 us
    ppermute x28, waiting for transfers between devices, shifted(): return lax.ppermute(x, axis, [(i, (i + shift) % size) for i in range(size)])  45.2 us
    all_to_all x2, waiting for transfers between devices, exchange_all(): lax.all_to_all(flat, COL_GRP, split_axis=0, concat_axis=0, tiled=True)  29.8 us
    all_to_all x2, starting transfers between devices, exchange_all(): lax.all_to_all(flat, COL_GRP, split_axis=0, concat_axis=0, tiled=True)  24.5 us
    unnamed x55, local copies, waits for them, and re-layouts  14.1 us
    pallas_call x1, Pallas kernels, pool(): pl.pallas_call(pool_kernel, grid=(TAB // STEP,), in_specs=[pl.BlockSpec((...  9.54 us
    pallas_call x1, Pallas kernels, row_grad(): pl.pallas_call(row_grad_kernel, grid=(TAB // STEP,), in_specs=[pl.BlockSp...  7.08 us
    pallas_call x1, Pallas kernels, spread(): pl.pallas_call(spread_kernel, in_specs=[pl.BlockSpec(memory_space=pltpu.S...  4.17 us
  transfers between devices with their start and end apart: 30, of which 13 were waited for; matrix products, arithmetic and copies ran while one was open for 5% of the time, Pallas kernels for 2%

profile of v2, /device:TPU:4, one launch (start us, length us, event | category | flops | bytes accessed | tf_op | source)
XLA Modules:
  0.0 200.0 jit_solution(14154086087222846333)
XLA Ops:
  3.1 9.5 %pool.1 = bf16[4,64,16,128]{3,2,1,0:T(8,128)(2,1)} custom-call(s32[1,4,8192]{2,1,0:T(4,128)S(1)} %copy-done.4, s32[1,8192]{1,0:T(1,128)S(1)} %copy-done.13, bf16[1,64,256]{2,1,0:T(8,128)(2,1)S(1)} %bitcast.55), custom_call_target="tpu_custom_call" | custom-call | tf_op jit(solution)/shard_map/pool/pallas_call | solution.py:96
  12.6 14.7 %all-to-all-start = ((bf16[256,16,128]{2,1,0:T(8,128)(2,1)}), bf16[256,16,128]{2,1,0:T(8,128)(2,1)S(1)}, u32[]{:S(2)}, u32[]{:S(2)}) async-start(bf16[256,16,128]{2,1,0:T(8,128)(2,1)} %bitcast.59), calls=%async_computation | async-start | bytes 2097152 | tf_op jit(solution)/shard_map/all_to_all | solution.py:440
  27.7 29.8 %all-to-all-done = bf16[256,16,128]{2,1,0:T(8,128)(2,1)S(1)} async-done(((bf16[256,16,128]{2,1,0:T(8,128)(2,1)}), bf16[256,16,128]{2,1,0:T(8,128)(2,1)S(1)}, u32[]{:S(2)}, u32[]{:S(2)}) %all-to-all-start) | async-done | bytes 1048608 | tf_op jit(solution)/shard_map/all_to_all | solution.py:440
  57.5 3.0 %interact.1 = (bf16[32,2432]{1,0:T(8,128)(2,1)}, bf16[16,64,512]{2,1,0:T(8,128)(2,1)}) custom-call(s32[64]{0:T(128)S(1)} %copy-done.18, bf16[4,64,16,128]{3,2,1,0:T(8,128)(2,1)S(1)} %bitcast.54, f32[32,256]{1,0:T(8,128)S(1)} %get-tuple-element.44.mine_ref), custom_call_target="tpu_custom_call" | custom-call | tf_op jit(solution)/shard_map/interact/pallas_call | solution.py:167
  60.5 1.1 collective-permute-start
  61.5 1.0 collective-permute-start.1
  62.5 2.4 %collective-permute-start.2 = (bf16[32,2432]{1,0:T(8,128)(2,1)}, bf16[32,2432]{1,0:T(8,128)(2,1)S(1)}, u32[]{:S(2)}, u32[]{:S(2)}) collective-permute-start(bf16[32,2432]{1,0:T(8,128)(2,1)} %get-tuple-element.21.f0), channel_id=1, source_target_pairs={{0,192},{64,0},{128,64},{192,128},{1,193},{65,1},{129,65},{193,129... | collective-permute-start | bytes 466952 | tf_op jit(solution)/shard_map/ppermute | solution.py:435
  66.3 3.2 %collective-permute-done.f1 = bf16[32,2432]{1,0:T(8,128)(2,1)S(1)} collective-permute-done((bf16[32,2432]{1,0:T(8,128)(2,1)}, bf16[32,2432]{1,0:T(8,128)(2,1)S(1)}, u32[]{:S(2)}, u32[]{:S(2)}) %collective-permute-start) | collective-permute-done | bytes 155680 | tf_op jit(solution)/shard_map/ppermute | solution.py:435
  70.2 5.1 %collective-permute-done.1.f2 = bf16[32,2432]{1,0:T(8,128)(2,1)S(1)} collective-permute-done((bf16[32,2432]{1,0:T(8,128)(2,1)}, bf16[32,2432]{1,0:T(8,128)(2,1)S(1)}, u32[]{:S(2)}, u32[]{:S(2)}) %collective-permute-start.1) | collective-permute-done | bytes 155680 | tf_op jit(solution)/shard_map/ppermute | solution.py:435
  76.6 0.9 copy-done.7
  77.5 0.9 copy-done.9
  78.4 0.9 copy-done.11
  79.3 3.1 %top.1 = (bf16[128,2432]{1,0:T(8,128)(2,1)}, bf16[32,2432]{1,0:T(8,128)(2,1)}, bf16[32,2432]{1,0:T(8,128)(2,1)S(1)}, bf16[32,2432]{1,0:T(8,128)(2,1)S(1)}, bf16[...) custom-call(bf16[32,2432]{1,0:T(8,128)(2,1)} %get-tuple-element.21.f0, ...), custom_call_target="tpu_custom_call" | custom-call | tf_op jit(solution)/shard_map/top/pallas_call | solution.py:212
  84.4 3.0 %collective-permute-start.3 = (f32[8,128]{1,0:T(8,128)S(1)}, f32[8,128]{1,0:T(8,128)S(1)}, u32[]{:S(2)}, u32[]{:S(2)}) collective-permute-start(f32[8,128]{1,0:T(8,128)S(1)} %get-tuple-element.22.p0), channel_id=1, source_target_pairs={{0,64},{64,128},{128,192},{192,0},{1,65},{65,129},{129,193},{193,1... | collective-permute-start | bytes 12296 | tf_op jit(solution)/shard_map/ppermute | solution.py:435
  88.1 1.7 collective-permute-start.5
  90.0 2.0 collective-permute-done.4.p2
  92.0 1.1 copy-done.3
  93.9 0.9 copy-done.16
  94.8 2.7 %weight_grad.1 = (bf16[16,16,2432]{2,1,0:T(8,128)(2,1)}, bf16[16,16,2432]{2,1,0:T(8,128)(2,1)}, f32[8,128]{1,0:T(8,128)S(1)}, f32[8,128]{1,0:T(8,128)S(1)}) custom-call(s32[1]{0:T(128)} %bitcast.core_ref, f32[8,128]{1,0:T(8,128)S(1)} %get-tuple-element.22.p0, f32[8,128]{1,0:T(8,128)S(1)} %collective-permute-done.3.p1, ...), custom_call_target="tpu_custom_call" | custom-call | tf_op jit(solution)/shard_map/weight_grad/pallas_call | solution.py:263
  97.5 3.3 %collective-permute-start.14 = (bf16[32,2432]{1,0:T(8,128)(2,1)}, bf16[32,2432]{1,0:T(8,128)(2,1)S(1)}, u32[]{:S(2)}, u32[]{:S(2)}) collective-permute-start(bf16[32,2432]{1,0:T(8,128)(2,1)} %copy-done.21), channel_id=1, source_target_pairs={{0,192},{64,0},{128,64},{192,128},{1,193},{65,1},{129,65},{193,129... | collective-permute-start | bytes 466952 | tf_op jit(solution)/shard_map/ppermute | solution.py:435
  101.6 4.0 %collective-permute-done.14.z1 = bf16[32,2432]{1,0:T(8,128)(2,1)S(1)} collective-permute-done((bf16[32,2432]{1,0:T(8,128)(2,1)}, bf16[32,2432]{1,0:T(8,128)(2,1)S(1)}, u32[]{:S(2)}, u32[]{:S(2)}) %collective-permute-start.14) | collective-permute-done | bytes 155680 | tf_op jit(solution)/shard_map/ppermute | solution.py:435
  105.6 9.1 %collective-permute-done.15.z2 = bf16[32,2432]{1,0:T(8,128)(2,1)S(1)} collective-permute-done((bf16[32,2432]{1,0:T(8,128)(2,1)}, bf16[32,2432]{1,0:T(8,128)(2,1)S(1)}, u32[]{:S(2)}, u32[]{:S(2)}) %collective-permute-start.15) | collective-permute-done | bytes 155680 | tf_op jit(solution)/shard_map/ppermute | solution.py:435
  114.7 0.9 copy-done.12
  115.6 4.2 %spread.1 = (bf16[4,64,16,128]{3,2,1,0:T(8,128)(2,1)}, f32[16,256]{1,0:T(8,128)S(1)}) custom-call(s32[64]{0:T(128)S(1)} %copy-done.18, bf16[32,2432]{1,0:T(8,128)(2,1)S(1)} %copy-done.12, bf16[32,2432]{1,0:T(8,128)(2,1)S(1)} %collective-permute-done.14.z1, bf16[32,2432]{1,0:T(8,128)(2,1)S(1)} %collective-permute-done.15.z2, ...), custom_call_target="tpu_custom_call" | custom-call | tf_op jit(solution)/shard_map/spread/pallas_call | solution.py:362
  119.8 1.2 collective-permute-done.17
  121.0 1.5 collective-permute-start.18
  122.5 1.6 collective-permute-start.19
  125.2 1.1 collective-permute-done.18
  126.4 1.5 collective-permute-done.20
  128.5 1.2 collective-permute-start.22
  129.7 2.1 %collective-permute-start.23 = (f32[16,256]{1,0:T(8,128)}, f32[16,256]{1,0:T(8,128)}, u32[]{:S(2)}, u32[]{:S(2)}) collective-permute-start(f32[16,256]{1,0:T(8,128)} %add_add_fusion.2), channel_id=1, source_target_pairs={{0,6},{2,0},{4,2},{6,4},{1,7},{3,1},{5,3},{7,5},{8,14},{10,8},{12,... | collective-permute-start | bytes 49160 | tf_op jit(solution)/shard_map/ppermute | solution.py:435
  131.8 1.0 copy-done.22
  132.8 2.0 add_convert_fusion
  134.8 0.9 dynamic-slice_bitcast_fusion.2
  135.7 2.9 %collective-permute-start.7 = (bf16[64,2432]{1,0:T(8,128)(2,1)}, bf16[64,2432]{1,0:T(8,128)(2,1)S(1)}, u32[]{:S(2)}, u32[]{:S(2)}) collective-permute-start(bf16[64,2432]{1,0:T(8,128)(2,1)} %get-tuple-element.37), channel_id=1, source_target_pairs={{0,16},{16,32},{32,48},{48,0},{1,17},{17,33},{33,49},{49,1},{2,18}... | collective-permute-start | bytes 933896 | tf_op jit(solution)/shard_map/ppermute | solution.py:435
  138.8 1.2 collective-permute-start.9
  140.7 9.8 %all-to-all-start.1 = ((bf16[256,16,128]{2,1,0:T(8,128)(2,1)}), bf16[256,16,128]{2,1,0:T(8,128)(2,1)S(1)}, u32[]{:S(2)}, u32[]{:S(2)}) async-start(bf16[256,16,128]{2,1,0:T(8,128)(2,1)} %bitcast.23), calls=%async_computation.1 | async-start | bytes 2097152 | tf_op jit(solution)/shard_map/all_to_all | solution.py:440
  151.3 2.9 %collective-permute-start.24 = (f32[16,256]{1,0:T(8,128)S(1)}, f32[16,256]{1,0:T(8,128)S(1)}, u32[]{:S(2)}, u32[]{:S(2)}) collective-permute-start(f32[16,256]{1,0:T(8,128)S(1)} %add_add_fusion.1), channel_id=1, source_target_pairs={{0,128},{64,192},{128,0},{192,64},{1,129},{65,193},{129,1},{193,65... | collective-permute-start | bytes 49160 | tf_op jit(solution)/shard_map/ppermute | solution.py:435
  154.2 1.7 collective-permute-start.25
  155.9 2.1 %collective-permute-start.26 = (f32[16,256]{1,0:T(8,128)S(1)}, f32[16,256]{1,0:T(8,128)S(1)}, u32[]{:S(2)}, u32[]{:S(2)}) collective-permute-start(f32[16,256]{1,0:T(8,128)S(1)} %add_add_fusion.1), channel_id=1, source_target_pairs={{0,192},{64,0},{128,64},{192,128},{1,193},{65,1},{129,65},{193,129... | collective-permute-start | bytes 49160 | tf_op jit(solution)/shard_map/ppermute | solution.py:435
  158.2 1.6 collective-permute-start.10
  159.8 2.8 %collective-permute-start.11 = (bf16[16,2432]{1,0:T(8,128)(2,1)S(1)}, bf16[16,2432]{1,0:T(8,128)(2,1)S(1)}, u32[]{:S(2)}, u32[]{:S(2)}) collective-permute-start(bf16[16,2432]{1,0:T(8,128)(2,1)S(1)} %get-tuple-element.42), channel_id=1, source_target_pairs={{0,4},{2,6},{4,0},{6,2},{1,5},{3,7},{5,1},{7,3},{8,12},{10,14},{12... | collective-permute-start | bytes 233480 | tf_op jit(solution)/shard_map/ppermute | solution.py:435
  162.6 12.5 %collective-permute-done.24 = f32[16,256]{1,0:T(8,128)S(1)} collective-permute-done((f32[16,256]{1,0:T(8,128)S(1)}, f32[16,256]{1,0:T(8,128)S(1)}, u32[]{:S(2)}, u32[]{:S(2)}) %collective-permute-start.24) | collective-permute-done | bytes 16416 | tf_op jit(solution)/shard_map/ppermute | solution.py:435
  175.1 2.9 %collective-permute-start.12 = (bf16[16,2432]{1,0:T(8,128)(2,1)S(1)}, bf16[16,2432]{1,0:T(8,128)(2,1)S(1)}, u32[]{:S(2)}, u32[]{:S(2)}) collective-permute-start(bf16[16,2432]{1,0:T(8,128)(2,1)S(1)} %get-tuple-element.41), channel_id=1, source_target_pairs={{0,6},{2,0},{4,2},{6,4},{1,7},{3,1},{5,3},{7,5},{8,14},{10,8},{12,... | collective-permute-start | bytes 233480 | tf_op jit(solution)/shard_map/ppermute | solution.py:435
  178.1 5.5 %collective-permute-start.27 = (f32[16,256]{1,0:T(8,128)S(1)}, f32[16,256]{1,0:T(8,128)S(1)}, u32[]{:S(2)}, u32[]{:S(2)}) collective-permute-start(f32[16,256]{1,0:T(8,128)S(1)} %add_add_fusion), channel_id=1, source_target_pairs={{0,8},{8,0},{1,9},{9,1},{2,10},{10,2},{3,11},{11,3},{4,12},{12,4},... | collective-permute-start | bytes 49160 | tf_op jit(solution)/shard_map/ppermute | solution.py:435
  183.6 2.0 collective-permute-start.13
  186.4 5.2 %collective-permute-done.13 = bf16[8,2432]{1,0:T(8,128)(2,1)S(1)} collective-permute-done((bf16[8,2432]{1,0:T(8,128)(2,1)S(1)}, bf16[8,2432]{1,0:T(8,128)(2,1)S(1)}, u32[]{:S(2)}, u32[]{:S(2)}) %collective-permute-start.13) | collective-permute-done | bytes 38944 | tf_op jit(solution)/shard_map/ppermute | solution.py:435
  192.9 7.1 %row_grad.1 = f32[1,64,256]{2,1,0:T(8,128)} custom-call(s32[1,4,8192]{2,1,0:T(4,128)S(1)} %copy-done.5, s32[1,8192]{1,0:T(1,128)S(1)} %copy-done.14, bf16[4,64,16,128]{3,2,1,0:T(8,128)(2,1)S(1)} %bitcast.53), custom_call_target="tpu_custom_call" | custom-call | tf_op jit(solution)/shard_map/row_grad/pallas_call | solution.py:413
  (106 shorter events, 16.7 us)
Async XLA Ops:
  0.6 26.9 %copy-start = (bf16[13,256]{1,0:T(8,128)(2,1)S(1)}, bf16[13,256]{1,0:T(8,128)(2,1)}, u32[]{:S(2)}) copy-start(bf16[13,256]{1,0:T(8,128)(2,1)} %param.14) | copy-start | bytes 19972
  0.6 0.9 copy-start.4
  12.6 14.7 %copy-start.23 = (bf16[128,13]{0,1:T(8,128)(2,1)S(1)}, bf16[128,13]{0,1:T(8,128)(2,1)}, u32[]{:S(2)}) copy-start(bf16[128,13]{0,1:T(8,128)(2,1)} %param.13) | copy-start | bytes 9988
  12.6 44.9 %copy-start.18 = (s32[64]{0:T(128)S(1)}, s32[64]{0:T(128)}, u32[]{:S(2)}) copy-start(s32[64]{0:T(128)} %slot_ref.3) | copy-start | bytes 772
  12.6 52.3 %copy-start.26 = (bf16[512]{0:T(512)(128)(2,1)S(1)}, bf16[512]{0:T(512)(128)(2,1)}, u32[]{:S(2)}) copy-start(bf16[512]{0:T(512)(128)(2,1)} %param.16) | copy-start | bytes 3076
  12.6 64.0 %copy-start.1 = (bf16[2336,512]{1,0:T(8,128)(2,1)S(1)}, bf16[2336,512]{1,0:T(8,128)(2,1)}, u32[]{:S(2)}) copy-start(bf16[2336,512]{1,0:T(8,128)(2,1)} %weight_ref.1) | copy-start | bytes 7176196
  12.6 44.9 %all-to-all-start = ((bf16[256,16,128]{2,1,0:T(8,128)(2,1)}), bf16[256,16,128]{2,1,0:T(8,128)(2,1)S(1)}, u32[]{:S(2)}, u32[]{:S(2)}) async-start(bf16[256,16,128]{2,1,0:T(8,128)(2,1)} %bitcast.59), calls=%async_computation | async-start | bytes 2097152 | tf_op jit(solution)/shard_map/all_to_all | solution.py:440
  60.5 9.1 %collective-permute-start = (bf16[32,2432]{1,0:T(8,128)(2,1)}, bf16[32,2432]{1,0:T(8,128)(2,1)S(1)}, u32[]{:S(2)}, u32[]{:S(2)}) collective-permute-start(bf16[32,2432]{1,0:T(8,128)(2,1)} %get-tuple-element.21.f0), channel_id=1, source_target_pairs={{0,64},{64,128},{128,192},{192,0},{1,65},{65,129},{129,193},{193,1... | collective-permute-start | bytes 466952 | tf_op jit(solution)/shard_map/ppermute | solution.py:435
  61.5 13.7 %collective-permute-start.1 = (bf16[32,2432]{1,0:T(8,128)(2,1)}, bf16[32,2432]{1,0:T(8,128)(2,1)S(1)}, u32[]{:S(2)}, u32[]{:S(2)}) collective-permute-start(bf16[32,2432]{1,0:T(8,128)(2,1)} %get-tuple-element.21.f0), channel_id=1, source_target_pairs={{0,128},{64,192},{128,0},{192,64},{1,129},{65,193},{129,1},{193,65... | collective-permute-start | bytes 466952 | tf_op jit(solution)/shard_map/ppermute | solution.py:435
  62.5 13.4 %collective-permute-start.2 = (bf16[32,2432]{1,0:T(8,128)(2,1)}, bf16[32,2432]{1,0:T(8,128)(2,1)S(1)}, u32[]{:S(2)}, u32[]{:S(2)}) collective-permute-start(bf16[32,2432]{1,0:T(8,128)(2,1)} %get-tuple-element.21.f0), channel_id=1, source_target_pairs={{0,192},{64,0},{128,64},{192,128},{1,193},{65,1},{129,65},{193,129... | collective-permute-start | bytes 466952 | tf_op jit(solution)/shard_map/ppermute | solution.py:435
  66.3 23.5 %copy-start.24 = (pred[4]{0:T(512)(128)(4,1)}, pred[4]{0:T(512)(128)(4,1)S(1)}, u32[]{:S(2)}) copy-start(pred[4]{0:T(512)(128)(4,1)S(1)} %compare_and_fusion) | copy-start | bytes 16
  76.6 0.9 copy-start.7
  77.5 0.9 copy-start.9
  78.4 0.9 copy-start.11
  79.3 35.4 %copy-start.2 = (bf16[16,64,512]{2,1,0:T(8,128)(2,1)S(1)}, bf16[16,64,512]{2,1,0:T(8,128)(2,1)}, u32[]{:S(2)}) copy-start(bf16[16,64,512]{2,1,0:T(8,128)(2,1)} %get-tuple-element.34.vectors_ref) | copy-start | bytes 3145732
  84.4 5.5 %collective-permute-start.3 = (f32[8,128]{1,0:T(8,128)S(1)}, f32[8,128]{1,0:T(8,128)S(1)}, u32[]{:S(2)}, u32[]{:S(2)}) collective-permute-start(f32[8,128]{1,0:T(8,128)S(1)} %get-tuple-element.22.p0), channel_id=1, source_target_pairs={{0,64},{64,128},{128,192},{192,0},{1,65},{65,129},{129,193},{193,1... | collective-permute-start | bytes 12296 | tf_op jit(solution)/shard_map/ppermute | solution.py:435
  87.4 4.5 %collective-permute-start.4 = (f32[8,128]{1,0:T(8,128)S(1)}, f32[8,128]{1,0:T(8,128)S(1)}, u32[]{:S(2)}, u32[]{:S(2)}) collective-permute-start(f32[8,128]{1,0:T(8,128)S(1)} %get-tuple-element.22.p0), channel_id=1, source_target_pairs={{0,128},{64,192},{128,0},{192,64},{1,129},{65,193},{129,1},{193,65... | collective-permute-start | bytes 12296 | tf_op jit(solution)/shard_map/ppermute | solution.py:435
  88.1 3.9 %collective-permute-start.5 = (f32[8,128]{1,0:T(8,128)S(1)}, f32[8,128]{1,0:T(8,128)S(1)}, u32[]{:S(2)}, u32[]{:S(2)}) collective-permute-start(f32[8,128]{1,0:T(8,128)S(1)} %get-tuple-element.22.p0), channel_id=1, source_target_pairs={{0,192},{64,0},{128,64},{192,128},{1,193},{65,1},{129,65},{193,129... | collective-permute-start | bytes 12296 | tf_op jit(solution)/shard_map/ppermute | solution.py:435
  91.9 1.1 copy-start.3
  93.0 0.9 copy-start.15
  97.5 34.3 %collective-permute-start.6 = (bf16[16,16,2432]{2,1,0:T(8,128)(2,1)}, bf16[16,16,2432]{2,1,0:T(8,128)(2,1)S(1)}, u32[]{:S(2)}, u32[]{:S(2)}) collective-permute-start(bf16[16,16,2432]{2,1,0:T(8,128)(2,1)} %get-tuple-element.28), channel_id=1, source_target_pairs={{0,1},{1,0},{2,3},{3,2},{4,5},{5,4},{6,7},{7,6},{8,9},{9,8},{10,11... | collective-permute-start | bytes 3735560 | tf_op jit(solution)/shard_map/ppermute | solution.py:435
  97.5 8.1 %collective-permute-start.14 = (bf16[32,2432]{1,0:T(8,128)(2,1)}, bf16[32,2432]{1,0:T(8,128)(2,1)S(1)}, u32[]{:S(2)}, u32[]{:S(2)}) collective-permute-start(bf16[32,2432]{1,0:T(8,128)(2,1)} %copy-done.21), channel_id=1, source_target_pairs={{0,192},{64,0},{128,64},{192,128},{1,193},{65,1},{129,65},{193,129... | collective-permute-start | bytes 466952 | tf_op jit(solution)/shard_map/ppermute | solution.py:435
  100.8 13.9 %collective-permute-start.15 = (bf16[32,2432]{1,0:T(8,128)(2,1)}, bf16[32,2432]{1,0:T(8,128)(2,1)S(1)}, u32[]{:S(2)}, u32[]{:S(2)}) collective-permute-start(bf16[32,2432]{1,0:T(8,128)(2,1)} %copy-done.20), channel_id=1, source_target_pairs={{0,128},{64,192},{128,0},{192,64},{1,129},{65,193},{129,1},{193,65... | collective-permute-start | bytes 466952 | tf_op jit(solution)/shard_map/ppermute | solution.py:435
  100.8 13.9 %collective-permute-start.16 = (bf16[32,2432]{1,0:T(8,128)(2,1)}, bf16[32,2432]{1,0:T(8,128)(2,1)S(1)}, u32[]{:S(2)}, u32[]{:S(2)}) collective-permute-start(bf16[32,2432]{1,0:T(8,128)(2,1)} %copy-done.19), channel_id=1, source_target_pairs={{0,64},{64,128},{128,192},{192,0},{1,65},{65,129},{129,193},{193,1... | collective-permute-start | bytes 466952 | tf_op jit(solution)/shard_map/ppermute | solution.py:435
  114.7 0.9 copy-start.12
  119.8 1.2 collective-permute-start.17
  121.0 5.3 %collective-permute-start.18 = (f32[16,256]{1,0:T(8,128)S(1)}, f32[16,256]{1,0:T(8,128)S(1)}, u32[]{:S(2)}, u32[]{:S(2)}) collective-permute-start(f32[16,256]{1,0:T(8,128)S(1)} %add.228), channel_id=1, source_target_pairs={{0,32},{16,48},{32,0},{48,16},{1,33},{17,49},{33,1},{49,17},{2,34}... | collective-permute-start | bytes 49160 | tf_op jit(solution)/shard_map/ppermute | solution.py:435
  122.5 3.9 %collective-permute-start.19 = (f32[16,256]{1,0:T(8,128)S(1)}, f32[16,256]{1,0:T(8,128)S(1)}, u32[]{:S(2)}, u32[]{:S(2)}) collective-permute-start(f32[16,256]{1,0:T(8,128)S(1)} %add.228), channel_id=1, source_target_pairs={{0,16},{16,32},{32,48},{48,0},{1,17},{17,33},{33,49},{49,1},{2,18}... | collective-permute-start | bytes 49160 | tf_op jit(solution)/shard_map/ppermute | solution.py:435
  124.1 3.7 %collective-permute-start.20 = (f32[16,256]{1,0:T(8,128)S(1)}, f32[16,256]{1,0:T(8,128)S(1)}, u32[]{:S(2)}, u32[]{:S(2)}) collective-permute-start(f32[16,256]{1,0:T(8,128)S(1)} %add.228), channel_id=1, source_target_pairs={{0,48},{16,0},{32,16},{48,32},{1,49},{17,1},{33,17},{49,33},{2,50}... | collective-permute-start | bytes 49160 | tf_op jit(solution)/shard_map/ppermute | solution.py:435
  128.5 10.3 %collective-permute-start.21 = (f32[16,256]{1,0:T(8,128)}, f32[16,256]{1,0:T(8,128)}, u32[]{:S(2)}, u32[]{:S(2)}) collective-permute-start(f32[16,256]{1,0:T(8,128)} %add_add_fusion.2), channel_id=1, source_target_pairs={{0,4},{2,6},{4,0},{6,2},{1,5},{3,7},{5,1},{7,3},{8,12},{10,14},{12... | collective-permute-start | bytes 49160 | tf_op jit(solution)/shard_map/ppermute | solution.py:435
  128.5 22.0 %collective-permute-start.22 = (f32[16,256]{1,0:T(8,128)}, f32[16,256]{1,0:T(8,128)}, u32[]{:S(2)}, u32[]{:S(2)}) collective-permute-start(f32[16,256]{1,0:T(8,128)} %add_add_fusion.2), channel_id=1, source_target_pairs={{0,2},{2,4},{4,6},{6,0},{1,3},{3,5},{5,7},{7,1},{8,10},{10,12},{12... | collective-permute-start | bytes 49160 | tf_op jit(solution)/shard_map/ppermute | solution.py:435
  129.7 20.8 %collective-permute-start.23 = (f32[16,256]{1,0:T(8,128)}, f32[16,256]{1,0:T(8,128)}, u32[]{:S(2)}, u32[]{:S(2)}) collective-permute-start(f32[16,256]{1,0:T(8,128)} %add_add_fusion.2), channel_id=1, source_target_pairs={{0,6},{2,0},{4,2},{6,4},{1,7},{3,1},{5,3},{7,5},{8,14},{10,8},{12,... | collective-permute-start | bytes 49160 | tf_op jit(solution)/shard_map/ppermute | solution.py:435
  131.8 1.0 copy-start.22
  134.8 5.3 %copy-start.25 = (pred[4]{0:T(512)(128)(4,1)S(1)}, pred[4]{0:T(512)(128)(4,1)}, u32[]{:S(2)}) copy-start(pred[4]{0:T(512)(128)(4,1)} %copy-done.24) | copy-start | bytes 16
  135.7 20.2 %collective-permute-start.7 = (bf16[64,2432]{1,0:T(8,128)(2,1)}, bf16[64,2432]{1,0:T(8,128)(2,1)S(1)}, u32[]{:S(2)}, u32[]{:S(2)}) collective-permute-start(bf16[64,2432]{1,0:T(8,128)(2,1)} %get-tuple-element.37), channel_id=1, source_target_pairs={{0,16},{16,32},{32,48},{48,0},{1,17},{17,33},{33,49},{49,1},{2,18}... | collective-permute-start | bytes 933896 | tf_op jit(solution)/shard_map/ppermute | solution.py:435
  138.6 19.4 %collective-permute-start.8 = (bf16[64,2432]{1,0:T(8,128)(2,1)}, bf16[64,2432]{1,0:T(8,128)(2,1)S(1)}, u32[]{:S(2)}, u32[]{:S(2)}) collective-permute-start(bf16[64,2432]{1,0:T(8,128)(2,1)} %get-tuple-element.39), channel_id=1, source_target_pairs={{0,32},{16,48},{32,0},{48,16},{1,33},{17,49},{33,1},{49,17},{2,34}... | collective-permute-start | bytes 933896 | tf_op jit(solution)/shard_map/ppermute | solution.py:435
  138.8 19.2 %collective-permute-start.9 = (bf16[64,2432]{1,0:T(8,128)(2,1)S(1)}, bf16[64,2432]{1,0:T(8,128)(2,1)S(1)}, u32[]{:S(2)}, u32[]{:S(2)}) collective-permute-start(bf16[64,2432]{1,0:T(8,128)(2,1)S(1)} %get-tuple-element.38), channel_id=1, source_target_pairs={{0,48},{16,0},{32,16},{48,32},{1,49},{17,1},{33,17},{49,33},{2,50}... | collective-permute-start | bytes 933896 | tf_op jit(solution)/shard_map/ppermute | solution.py:435
  140.7 52.2 %all-to-all-start.1 = ((bf16[256,16,128]{2,1,0:T(8,128)(2,1)}), bf16[256,16,128]{2,1,0:T(8,128)(2,1)S(1)}, u32[]{:S(2)}, u32[]{:S(2)}) async-start(bf16[256,16,128]{2,1,0:T(8,128)(2,1)} %bitcast.23), calls=%async_computation.1 | async-start | bytes 2097152 | tf_op jit(solution)/shard_map/all_to_all | solution.py:440
  151.3 23.8 %collective-permute-start.24 = (f32[16,256]{1,0:T(8,128)S(1)}, f32[16,256]{1,0:T(8,128)S(1)}, u32[]{:S(2)}, u32[]{:S(2)}) collective-permute-start(f32[16,256]{1,0:T(8,128)S(1)} %add_add_fusion.1), channel_id=1, source_target_pairs={{0,128},{64,192},{128,0},{192,64},{1,129},{65,193},{129,1},{193,65... | collective-permute-start | bytes 49160 | tf_op jit(solution)/shard_map/ppermute | solution.py:435
  154.2 23.9 %collective-permute-start.25 = (f32[16,256]{1,0:T(8,128)S(1)}, f32[16,256]{1,0:T(8,128)S(1)}, u32[]{:S(2)}, u32[]{:S(2)}) collective-permute-start(f32[16,256]{1,0:T(8,128)S(1)} %add_add_fusion.1), channel_id=1, source_target_pairs={{0,64},{64,128},{128,192},{192,0},{1,65},{65,129},{129,193},{193,1... | collective-permute-start | bytes 49160 | tf_op jit(solution)/shard_map/ppermute | solution.py:435
  155.9 22.1 %collective-permute-start.26 = (f32[16,256]{1,0:T(8,128)S(1)}, f32[16,256]{1,0:T(8,128)S(1)}, u32[]{:S(2)}, u32[]{:S(2)}) collective-permute-start(f32[16,256]{1,0:T(8,128)S(1)} %add_add_fusion.1), channel_id=1, source_target_pairs={{0,192},{64,0},{128,64},{192,128},{1,193},{65,1},{129,65},{193,129... | collective-permute-start | bytes 49160 | tf_op jit(solution)/shard_map/ppermute | solution.py:435
  158.2 34.8 %copy-start.5 = (s32[1,4,8192]{2,1,0:T(4,128)S(1)}, s32[1,4,8192]{2,1,0:T(4,128)}, u32[]{:S(2)}) copy-start(s32[1,4,8192]{2,1,0:T(4,128)} %index_ref.3) | copy-start | bytes 393220
  158.2 34.8 %copy-start.14 = (s32[1,8192]{1,0:T(1,128)S(1)}, s32[1,8192]{1,0:T(1,128)}, u32[]{:S(2)}) copy-start(s32[1,8192]{1,0:T(1,128)} %length_ref.3) | copy-start | bytes 98308
  158.2 25.3 %collective-permute-start.10 = (bf16[16,2432]{1,0:T(8,128)(2,1)S(1)}, bf16[16,2432]{1,0:T(8,128)(2,1)S(1)}, u32[]{:S(2)}, u32[]{:S(2)}) collective-permute-start(bf16[16,2432]{1,0:T(8,128)(2,1)S(1)} %get-tuple-element.40), channel_id=1, source_target_pairs={{0,2},{2,4},{4,6},{6,0},{1,3},{3,5},{5,7},{7,1},{8,10},{10,12},{12... | collective-permute-start | bytes 233480 | tf_op jit(solution)/shard_map/ppermute | solution.py:435
  159.8 23.7 %collective-permute-start.11 = (bf16[16,2432]{1,0:T(8,128)(2,1)S(1)}, bf16[16,2432]{1,0:T(8,128)(2,1)S(1)}, u32[]{:S(2)}, u32[]{:S(2)}) collective-permute-start(bf16[16,2432]{1,0:T(8,128)(2,1)S(1)} %get-tuple-element.42), channel_id=1, source_target_pairs={{0,4},{2,6},{4,0},{6,2},{1,5},{3,7},{5,1},{7,3},{8,12},{10,14},{12... | collective-permute-start | bytes 233480 | tf_op jit(solution)/shard_map/ppermute | solution.py:435
  175.1 8.4 %collective-permute-start.12 = (bf16[16,2432]{1,0:T(8,128)(2,1)S(1)}, bf16[16,2432]{1,0:T(8,128)(2,1)S(1)}, u32[]{:S(2)}, u32[]{:S(2)}) collective-permute-start(bf16[16,2432]{1,0:T(8,128)(2,1)S(1)} %get-tuple-element.41), channel_id=1, source_target_pairs={{0,6},{2,0},{4,2},{6,4},{1,7},{3,1},{5,3},{7,5},{8,14},{10,8},{12,... | collective-permute-start | bytes 233480 | tf_op jit(solution)/shard_map/ppermute | solution.py:435
  178.1 7.7 %collective-permute-start.27 = (f32[16,256]{1,0:T(8,128)S(1)}, f32[16,256]{1,0:T(8,128)S(1)}, u32[]{:S(2)}, u32[]{:S(2)}) collective-permute-start(f32[16,256]{1,0:T(8,128)S(1)} %add_add_fusion), channel_id=1, source_target_pairs={{0,8},{8,0},{1,9},{9,1},{2,10},{10,2},{3,11},{11,3},{4,12},{12,4},... | collective-permute-start | bytes 49160 | tf_op jit(solution)/shard_map/ppermute | solution.py:435
  183.6 8.0 %collective-permute-start.13 = (bf16[8,2432]{1,0:T(8,128)(2,1)S(1)}, bf16[8,2432]{1,0:T(8,128)(2,1)S(1)}, u32[]{:S(2)}, u32[]{:S(2)}) collective-permute-start(bf16[8,2432]{1,0:T(8,128)(2,1)S(1)} %fusion.8), channel_id=1, source_target_pairs={{0,8},{8,0},{1,9},{9,1},{2,10},{10,2},{3,11},{11,3},{4,12},{12,4},... | collective-permute-start | bytes 116744 | tf_op jit(solution)/shard_map/ppermute | solution.py:435
  (9 other events, 6.4 us)

commit v3 on v2

--- a/solution.py
+++ b/solution.py
@@ -65,31 +65,38 @@
     return [pl.BlockSpec(memory_space=pltpu.VMEM)] * count
 
 
-def pool_kernel(index_ref, length_ref, rows_ref, out_ref, weights, counted):
-    @pl.when(pl.program_id(0) == 0)
-    def _():
-        weights[...] = jnp.zeros_like(weights)
-        weights[0:HALF, 0:256] = rows_ref[0]
-        weights[HALF:LANES, 256:512] = rows_ref[0]
-
-    values = lax.broadcasted_iota(jnp.int32, (LANES, 256), 1)
-    slots = lax.broadcasted_iota(jnp.int32, (8, LANES), 0)
+def row_values():
+    return lax.broadcasted_iota(jnp.int32, (256, LANES), 0).astype(F32).astype(BF16)
+
+
+def counts_of(index_ref, length_ref, group, values):
+    lanes = slice(group * LANES, (group + 1) * LANES)
+    length = length_ref[0:1, lanes]
+    one, none = jnp.ones((256, LANES), BF16), jnp.zeros((256, LANES), BF16)
+    counts = none
+    for slot in range(4):
+        ids = jnp.where(slot < length, index_ref[0, slot : slot + 1, lanes], -1).astype(F32)
+        ids = jnp.broadcast_to(ids, (16, LANES)).astype(BF16)
+        counts = counts + jnp.where(jnp.concatenate([ids] * 16, axis=0) == values, one, none)
+    return counts
+
+
+def pool_kernel(index_ref, length_ref, rows_ref, out_ref):
+    values = row_values()
+    low = low_lanes(HALF)
+    right = jnp.concatenate([rows_ref[0], rows_ref[0]], axis=0)
     for group in range(STEP):
-        lanes = slice(group * LANES, (group + 1) * LANES)
-        index = index_ref[0, :, lanes]
-        index = jnp.concatenate([index, index], axis=0)
-        ids = jnp.where(slots < length_ref[0:1, lanes], index, -1).T
-        counts = jnp.zeros((LANES, 256), F32)
-        for slot in range(4):
-            counts = counts + jnp.where(ids[:, slot : slot + 1] == values, 1.0, 0.0)
-        counts = counts.astype(BF16)
-        counted[group * HALF : (group + 1) * HALF, 0:256] = counts[0:HALF]
-        counted[group * HALF : (group + 1) * HALF, 256:512] = counts[HALF:LANES]
-    pooled = dot_t(counted[...], weights[...]).astype(BF16)
-    for group in range(STEP):
+        counts = counts_of(index_ref, length_ref, group, values)
+        pooled = lax.dot_general(
+            counts, right, (((0,), (1,)), ((), ())), preferred_element_type=F32
+        )
+        pooled = jnp.where(low, pooled[0:HALF], pooled[HALF:LANES]).astype(BF16)
         for peer in range(4):
-            first = group * HALF + peer * ROWS
-            out_ref[peer, group] = pooled[first : first + ROWS]
+            out_ref[peer, group] = pooled[peer * ROWS : (peer + 1) * ROWS]
+
+
+def in_hbm(*arrays):
+    return [pltpu.with_memory_space_constraint(x, pltpu.HBM) for x in arrays]
 
 
 def pool(pool_index, bag_length, rows):
@@ -103,13 +110,9 @@
         ],
         out_specs=pl.BlockSpec((4, STEP, ROWS, LANES), lambda i: (0, i, 0, 0)),
         out_shape=hbm((4, TAB, ROWS, LANES), BF16),
-        scratch_shapes=[
-            pltpu.VMEM((LANES, 512), BF16),
-            pltpu.VMEM((STEP * HALF, 512), BF16),
-        ],
         compiler_params=pltpu.CompilerParams(vmem_limit_bytes=12 << 20),
         name="pool",
-    )(pool_index, bag_length, rows)
+    )(*in_hbm(pool_index, bag_length, rows))
 
 
 def packed_bottom(mine_ref):
@@ -273,7 +276,7 @@
         scratch_shapes=[pltpu.VMEM((512, WIDE), F32)],
         compiler_params=pltpu.CompilerParams(vmem_limit_bytes=32 << 20),
         name="weight_grad",
-    )(core, *partials, labels, features, delta, hidden)
+    )(core, *partials, labels, *in_hbm(features, delta, hidden))
 
 
 def spread_kernel(
@@ -388,19 +391,16 @@
     def _():
         total[...] = jnp.zeros_like(total)
 
-    values = lax.broadcasted_iota(jnp.int32, (256, LANES), 0)
+    values = row_values()
     low = low_lanes(HALF)
+    first = jnp.where(low, 1.0, 0.0).astype(BF16)
+    second = jnp.where(low, 0.0, 1.0).astype(BF16)
     for group in range(STEP):
         lanes = slice(group * LANES, (group + 1) * LANES)
-        length = length_ref[0:1, lanes]
-        counts = jnp.zeros((256, LANES), F32)
-        for slot in range(4):
-            ids = jnp.where(slot < length, index_ref[0, slot : slot + 1, lanes], -1)
-            counts = counts + jnp.where(ids == values, 1.0, 0.0)
-        counted[:, lanes] = counts.astype(BF16)
-        rows = jnp.concatenate([back_ref[peer, group].astype(F32) for peer in range(4)], axis=0)
-        moved[group * LANES : group * LANES + HALF, :] = jnp.where(low, rows, 0.0).astype(BF16)
-        moved[group * LANES + HALF : (group + 1) * LANES, :] = jnp.where(low, 0.0, rows).astype(BF16)
+        counted[:, lanes] = counts_of(index_ref, length_ref, group, values)
+        rows = jnp.concatenate([back_ref[peer, group] for peer in range(4)], axis=0)
+        moved[group * LANES : group * LANES + HALF, :] = rows * first
+        moved[group * LANES + HALF : (group + 1) * LANES, :] = rows * second
     total[...] += jnp.dot(counted[...], moved[...], preferred_element_type=F32)
 
     @pl.when(step == pl.num_programs(0) - 1)
@@ -427,7 +427,7 @@
         ],
         compiler_params=pltpu.CompilerParams(vmem_limit_bytes=12 << 20),
         name="row_grad",
-    )(pool_index, bag_length, back)
+    )(*in_hbm(pool_index, bag_length), back)
 
 
 def shifted(x, axis, shift):
@@ -448,14 +448,37 @@
     return (x + others[1]) + (others[0] + others[2])
 
 
-def reduced_to(x, axis):
+def split(x):
+    high = x.astype(BF16)
+    return high, (x - high.astype(F32)).astype(BF16)
+
+
+def reduced_to(x, axis, shared=None):
     me = lax.axis_index(axis)
     size = lax.axis_size(axis)
     total = lax.dynamic_index_in_dim(x, me, 0, keepdims=False).astype(F32)
+    rows, width = total.shape
+    if shared is not None:
+        high, low = split(shared)
+        own = high.astype(F32) + low.astype(F32)
+        cuts = [v[r : r + rows] for v in (high, low) for r in range(0, shared.shape[0], rows)]
+    others = []
     for shift in range(1, size):
-        block = lax.dynamic_index_in_dim(x, (me + shift) % size, 0, keepdims=False)
-        total = total + shifted(block.astype(BF16), axis, shift).astype(F32)
-    return total
+        block = lax.dynamic_index_in_dim(x, (me + shift) % size, 0, keepdims=False).astype(BF16)
+        if shared is not None:
+            block = jnp.concatenate([block, *cuts], axis=1)
+        block = shifted(block, axis, shift).astype(F32)
+        total = total + block[:, 0:width]
+        if shared is not None:
+            wide = shared.shape[1]
+            parts = [block[:, p : p + wide] for p in range(width, block.shape[1], wide)]
+            half = len(parts) // 2
+            others.append(jnp.concatenate([a + b for a, b in zip(parts[:half], parts[half:])], axis=0))
+    if shared is None:
+        return total
+    if size == 2:
+        return total, own + others[0]
+    return total, (own + others[1]) + (others[0] + others[2])
 
 
 def silu_slope(values):
@@ -510,14 +533,13 @@
     other = shifted(other, "grp_3", 1)
     grad = (own.astype(F32) + other.astype(F32)).astype(BF16).reshape(4, 64, WIDE)
     grad = reduced_to(grad, "grp_0").reshape(4, 16, WIDE)
-    grad = reduced_to(grad, "grp_2").reshape(2, 8, WIDE)
-    grad = reduced_to(grad, "grp_1")
+    for axis in ("grp_3", "grp_0"):
+        bottom = summed_over(bottom, axis)
+    grad, bottom = reduced_to(grad, "grp_2", bottom)
+    grad, bottom = reduced_to(grad.reshape(2, 8, WIDE), "grp_1", bottom)
     grad_top = jnp.transpose(grad[:, 0:FEAT])
     grad_out = grad[:, FEAT] + grad[:, FEAT + 1]
-
-    for axis in ("grp_3", "grp_0", "grp_2", "col", "grp_1"):
-        bottom = summed_over(bottom, axis)
-    grad_bottom = bottom[0 : bottom_weight.shape[0]]
+    grad_bottom = summed_over(bottom, "col")[0 : bottom_weight.shape[0]]
     return (logits, grad_top, grad_out, grad_bottom, grad_rows)
 
 

time: 201 us -> 198 us (0.985)
  waiting for transfers between devices: 75 us -> 97.3 us
  starting transfers between devices: 70.9 us -> 55.9 us
  local copies, waits for them, and re-layouts: 18.6 us -> 11.4 us
  Pallas kernels: 29.5 us -> 26.9 us
    ppermute x28 -> x24, waiting for transfers between devices: 45.2 us -> 62.7 us  [shifted(): return lax.ppermute(x, axis, [(i, (i + shift) % size) for i in range(size)])]
    ppermute x28 -> x24, starting transfers between devices: 46.4 us -> 31.3 us  [shifted(): return lax.ppermute(x, axis, [(i, (i + shift) % size) for i in range(size)])]
    unnamed x55 -> x43, local copies, waits for them, and re-layouts: 14.1 us -> 7.83 us
    all_to_all x2, waiting for transfers between devices: 29.8 us -> 34.5 us  [exchange_all(): lax.all_to_all(flat, COL_GRP, split_axis=0, concat_axis=0, tiled=True)]
    pallas_call x1, Pallas kernels: 9.54 us -> 6.36 us  [pool(): pl.pallas_call(pool_kernel, grid=(TAB // STEP,), in_specs=[pl.BlockSpec((...]
  transfers between devices with their start and end apart: 30 -> 26, of which waited for: 13 -> 16; matrix products, arithmetic and copies ran while one was open for 5% -> 4% of each run, Pallas kernels for 2% -> 2%
where the time goes in v3:
time: 198 us; the launch traced here: 196 us
  waiting for transfers between devices  97.3 us (49%)
  starting transfers between devices  55.9 us (28%)
  Pallas kernels  26.9 us (14%)
  local copies, waits for them, and re-layouts  11.4 us (6%)
  other arithmetic  3.45 us (2%)
    ppermute x24, waiting for transfers between devices, shifted(): return lax.ppermute(x, axis, [(i, (i + shift) % size) for i in range(size)])  62.7 us
    all_to_all x2, waiting for transfers between devices, exchange_all(): lax.all_to_all(flat, COL_GRP, split_axis=0, concat_axis=0, tiled=True)  34.5 us
    ppermute x24, starting transfers between devices, shifted(): return lax.ppermute(x, axis, [(i, (i + shift) % size) for i in range(size)])  31.3 us
    all_to_all x2, starting transfers between devices, exchange_all(): lax.all_to_all(flat, COL_GRP, split_axis=0, concat_axis=0, tiled=True)  24.6 us
    unnamed x43, local copies, waits for them, and re-layouts  7.83 us
    pallas_call x1, Pallas kernels, row_grad(): pl.pallas_call(row_grad_kernel, grid=(TAB // STEP,), in_specs=[pl.BlockSp...  6.44 us
    pallas_call x1, Pallas kernels, pool(): pl.pallas_call(pool_kernel, grid=(TAB // STEP,), in_specs=[pl.BlockSpec((...  6.36 us
    pallas_call x1, Pallas kernels, spread(): pl.pallas_call(spread_kernel, in_specs=[pl.BlockSpec(memory_space=pltpu.S...  4.2 us
  transfers between devices with their start and end apart: 26, of which 16 were waited for; matrix products, arithmetic and copies ran while one was open for 4% of the time, Pallas kernels for 2%

profile of v3, /device:TPU:4, one launch (start us, length us, event | category | flops | bytes accessed | tf_op | source)
XLA Modules:
  0.0 195.9 jit_solution(10481963899309908504)
XLA Ops:
  0.6 6.4 %pool.1 = bf16[4,64,16,128]{3,2,1,0:T(8,128)(2,1)} custom-call(s32[1,4,8192]{2,1,0:T(4,128)} %index_ref.3, s32[1,8192]{1,0:T(1,128)} %length_ref.3, bf16[1,64,256]{2,1,0:T(8,128)(2,1)} %bitcast.58), custom_call_target="tpu_custom_call" | custom-call | tf_op jit(solution)/shard_map/pool/pallas_call | solution.py:103
  7.0 14.7 %all-to-all-start = ((bf16[256,16,128]{2,1,0:T(8,128)(2,1)}), bf16[256,16,128]{2,1,0:T(8,128)(2,1)S(1)}, u32[]{:S(2)}, u32[]{:S(2)}) async-start(bf16[256,16,128]{2,1,0:T(8,128)(2,1)} %bitcast.54), calls=%async_computation | async-start | bytes 2097152 | tf_op jit(solution)/shard_map/all_to_all | solution.py:440
  22.1 29.8 %all-to-all-done = bf16[256,16,128]{2,1,0:T(8,128)(2,1)S(1)} async-done(((bf16[256,16,128]{2,1,0:T(8,128)(2,1)}), bf16[256,16,128]{2,1,0:T(8,128)(2,1)S(1)}, u32[]{:S(2)}, u32[]{:S(2)}) %all-to-all-start) | async-done | bytes 1048608 | tf_op jit(solution)/shard_map/all_to_all | solution.py:440
  51.9 3.0 %interact.1 = (bf16[32,2432]{1,0:T(8,128)(2,1)}, bf16[16,64,512]{2,1,0:T(8,128)(2,1)}) custom-call(s32[64]{0:T(128)S(1)} %copy-done.10, bf16[4,64,16,128]{3,2,1,0:T(8,128)(2,1)S(1)} %bitcast.50, f32[32,256]{1,0:T(8,128)S(1)} %get-tuple-element.50.mine_ref), custom_call_target="tpu_custom_call" | custom-call | tf_op jit(solution)/shard_map/interact/pallas_call | solution.py:170
  54.9 1.1 collective-permute-start
  55.9 1.0 collective-permute-start.1
  56.9 2.4 %collective-permute-start.2 = (bf16[32,2432]{1,0:T(8,128)(2,1)}, bf16[32,2432]{1,0:T(8,128)(2,1)S(1)}, u32[]{:S(2)}, u32[]{:S(2)}) collective-permute-start(bf16[32,2432]{1,0:T(8,128)(2,1)} %get-tuple-element.21.f0), channel_id=1, source_target_pairs={{0,192},{64,0},{128,64},{192,128},{1,193},{65,1},{129,65},{193,129... | collective-permute-start | bytes 466952 | tf_op jit(solution)/shard_map/ppermute | solution.py:435
  59.3 0.7 reshape.148
  60.7 3.2 %collective-permute-done.f1 = bf16[32,2432]{1,0:T(8,128)(2,1)S(1)} collective-permute-done((bf16[32,2432]{1,0:T(8,128)(2,1)}, bf16[32,2432]{1,0:T(8,128)(2,1)S(1)}, u32[]{:S(2)}, u32[]{:S(2)}) %collective-permute-start) | collective-permute-done | bytes 155680 | tf_op jit(solution)/shard_map/ppermute | solution.py:435
  64.6 5.1 %collective-permute-done.1.f2 = bf16[32,2432]{1,0:T(8,128)(2,1)S(1)} collective-permute-done((bf16[32,2432]{1,0:T(8,128)(2,1)}, bf16[32,2432]{1,0:T(8,128)(2,1)S(1)}, u32[]{:S(2)}, u32[]{:S(2)}) %collective-permute-start.1) | collective-permute-done | bytes 155680 | tf_op jit(solution)/shard_map/ppermute | solution.py:435
  71.0 0.9 copy-done.4
  71.9 0.9 copy-done.6
  72.8 0.9 copy-done.8
  73.7 3.1 %top.1 = (bf16[128,2432]{1,0:T(8,128)(2,1)}, bf16[32,2432]{1,0:T(8,128)(2,1)}, bf16[32,2432]{1,0:T(8,128)(2,1)S(1)}, bf16[32,2432]{1,0:T(8,128)(2,1)S(1)}, bf16[...) custom-call(bf16[32,2432]{1,0:T(8,128)(2,1)} %get-tuple-element.21.f0, ...), custom_call_target="tpu_custom_call" | custom-call | tf_op jit(solution)/shard_map/top/pallas_call | solution.py:215
  76.8 0.7 copy-done.11
  78.8 3.0 %collective-permute-start.3 = (f32[8,128]{1,0:T(8,128)S(1)}, f32[8,128]{1,0:T(8,128)S(1)}, u32[]{:S(2)}, u32[]{:S(2)}) collective-permute-start(f32[8,128]{1,0:T(8,128)S(1)} %get-tuple-element.22.p0), channel_id=1, source_target_pairs={{0,64},{64,128},{128,192},{192,0},{1,65},{65,129},{129,193},{193,1... | collective-permute-start | bytes 12296 | tf_op jit(solution)/shard_map/ppermute | solution.py:435
  82.5 1.7 collective-permute-start.5
  84.4 2.0 %collective-permute-done.4.p2 = f32[8,128]{1,0:T(8,128)S(1)} collective-permute-done((f32[8,128]{1,0:T(8,128)S(1)}, f32[8,128]{1,0:T(8,128)S(1)}, u32[]{:S(2)}, u32[]{:S(2)}) %collective-permute-start.4) | collective-permute-done | bytes 4128 | tf_op jit(solution)/shard_map/ppermute | solution.py:435
  86.4 3.8 %weight_grad.1 = (bf16[16,16,2432]{2,1,0:T(8,128)(2,1)}, bf16[16,16,2432]{2,1,0:T(8,128)(2,1)}, f32[8,128]{1,0:T(8,128)S(1)}, f32[8,128]{1,0:T(8,128)S(1)}) custom-call(s32[1]{0:T(128)} %bitcast.core_ref, f32[8,128]{1,0:T(8,128)S(1)} %get-tuple-element.22.p0, f32[8,128]{1,0:T(8,128)S(1)} %collective-permute-done.3.p1, ...), custom_call_target="tpu_custom_call" | custom-call | tf_op jit(solution)/shard_map/weight_grad/pallas_call | solution.py:266
  90.2 3.3 %collective-permute-start.10 = (bf16[32,2432]{1,0:T(8,128)(2,1)}, bf16[32,2432]{1,0:T(8,128)(2,1)S(1)}, u32[]{:S(2)}, u32[]{:S(2)}) collective-permute-start(bf16[32,2432]{1,0:T(8,128)(2,1)} %copy-done.13), channel_id=1, source_target_pairs={{0,192},{64,0},{128,64},{192,128},{1,193},{65,1},{129,65},{193,129... | collective-permute-start | bytes 466952 | tf_op jit(solution)/shard_map/ppermute | solution.py:435
  93.5 0.8 collective-permute-start.12
  94.2 4.0 %collective-permute-done.10.z1 = bf16[32,2432]{1,0:T(8,128)(2,1)S(1)} collective-permute-done((bf16[32,2432]{1,0:T(8,128)(2,1)}, bf16[32,2432]{1,0:T(8,128)(2,1)S(1)}, u32[]{:S(2)}, u32[]{:S(2)}) %collective-permute-start.10) | collective-permute-done | bytes 155680 | tf_op jit(solution)/shard_map/ppermute | solution.py:435
  98.3 9.1 %collective-permute-done.11.z2 = bf16[32,2432]{1,0:T(8,128)(2,1)S(1)} collective-permute-done((bf16[32,2432]{1,0:T(8,128)(2,1)}, bf16[32,2432]{1,0:T(8,128)(2,1)S(1)}, u32[]{:S(2)}, u32[]{:S(2)}) %collective-permute-start.11) | collective-permute-done | bytes 155680 | tf_op jit(solution)/shard_map/ppermute | solution.py:435
  107.4 0.9 copy-done.9
  108.3 4.2 %spread.1 = (bf16[4,64,16,128]{3,2,1,0:T(8,128)(2,1)}, f32[16,256]{1,0:T(8,128)S(1)}) custom-call(s32[64]{0:T(128)S(1)} %copy-done.10, bf16[32,2432]{1,0:T(8,128)(2,1)S(1)} %copy-done.9, bf16[32,2432]{1,0:T(8,128)(2,1)S(1)} %collective-permute-done.10.z1, bf16[32,2432]{1,0:T(8,128)(2,1)S(1)} %collective-permute-done.11.z2, ...), custom_call_target="tpu_custom_call" | custom-call | tf_op jit(solution)/shard_map/spread/pallas_call | solution.py:365
  112.5 1.2 collective-permute-done.13
  113.7 1.0 collective-permute-start.15
  114.7 1.0 collective-permute-start.16
  115.7 2.7 %collective-permute-start.14 = (f32[16,256]{1,0:T(8,128)S(1)}, f32[16,256]{1,0:T(8,128)S(1)}, u32[]{:S(2)}, u32[]{:S(2)}) collective-permute-start(f32[16,256]{1,0:T(8,128)S(1)} %add.233), channel_id=1, source_target_pairs={{0,32},{16,48},{32,0},{48,16},{1,33},{17,49},{33,1},{49,17},{2,34}... | collective-permute-start | bytes 49160 | tf_op jit(solution)/shard_map/ppermute | solution.py:435
  118.4 1.6 add_convert_fusion
  120.2 2.5 %collective-permute-start.8 = (bf16[64,2432]{1,0:T(8,128)(2,1)S(1)}, bf16[64,2432]{1,0:T(8,128)(2,1)S(1)}, u32[]{:S(2)}, u32[]{:S(2)}) collective-permute-start(bf16[64,2432]{1,0:T(8,128)(2,1)S(1)} %get-tuple-element.43), channel_id=1, source_target_pairs={{0,32},{16,48},{32,0},{48,16},{1,33},{17,49},{33,1},{49,17},{2,34}... | collective-permute-start | bytes 933896 | tf_op jit(solution)/shard_map/ppermute | solution.py:435
  122.7 1.0 collective-permute-start.7
  123.7 6.7 %collective-permute-done.9 = bf16[64,2432]{1,0:T(8,128)(2,1)S(1)} collective-permute-done((bf16[64,2432]{1,0:T(8,128)(2,1)S(1)}, bf16[64,2432]{1,0:T(8,128)(2,1)S(1)}, u32[]{:S(2)}, u32[]{:S(2)}) %collective-permute-start.9) | collective-permute-done | bytes 311328 | tf_op jit(solution)/shard_map/ppermute | solution.py:435
  130.4 1.6 collective-permute-done.8
  132.1 5.0 %collective-permute-done.7 = bf16[64,2432]{1,0:T(8,128)(2,1)S(1)} collective-permute-done((bf16[64,2432]{1,0:T(8,128)(2,1)S(1)}, bf16[64,2432]{1,0:T(8,128)(2,1)S(1)}, u32[]{:S(2)}, u32[]{:S(2)}) %collective-permute-start.7) | collective-permute-done | bytes 311328 | tf_op jit(solution)/shard_map/ppermute | solution.py:435
  137.3 1.7 collective-permute-start.19
  140.7 2.3 %collective-permute-done.19 = bf16[16,2944]{1,0:T(8,128)(2,1)S(1)} collective-permute-done((bf16[16,2944]{1,0:T(8,128)(2,1)S(1)}, bf16[16,2944]{1,0:T(8,128)(2,1)S(1)}, u32[]{:S(2)}, u32[]{:S(2)}) %collective-permute-start.19) | collective-permute-done | bytes 94240 | tf_op jit(solution)/shard_map/ppermute | solution.py:435
  143.0 2.6 %collective-permute-done.18 = bf16[16,2944]{1,0:T(8,128)(2,1)S(1)} collective-permute-done((bf16[16,2944]{1,0:T(8,128)(2,1)S(1)}, bf16[16,2944]{1,0:T(8,128)(2,1)S(1)}, u32[]{:S(2)}, u32[]{:S(2)}) %collective-permute-start.18) | collective-permute-done | bytes 94240 | tf_op jit(solution)/shard_map/ppermute | solution.py:435
  145.6 0.9 collective-permute-done.17
  146.7 1.6 collective-permute-start.20
  149.0 9.9 %all-to-all-start.1 = ((bf16[256,16,128]{2,1,0:T(8,128)(2,1)}), bf16[256,16,128]{2,1,0:T(8,128)(2,1)S(1)}, u32[]{:S(2)}, u32[]{:S(2)}) async-start(bf16[256,16,128]{2,1,0:T(8,128)(2,1)} %bitcast.23), calls=%async_computation.1 | async-start | bytes 2097152 | tf_op jit(solution)/shard_map/all_to_all | solution.py:440
  159.0 4.0 %collective-permute-start.23 = (f32[16,256]{1,0:T(8,128)S(1)}, f32[16,256]{1,0:T(8,128)S(1)}, u32[]{:S(2)}, u32[]{:S(2)}) collective-permute-start(f32[16,256]{1,0:T(8,128)S(1)} %fusion.12), channel_id=1, source_target_pairs={{0,192},{64,0},{128,64},{192,128},{1,193},{65,1},{129,65},{193,129... | collective-permute-start | bytes 49160 | tf_op jit(solution)/shard_map/ppermute | solution.py:435
  163.0 0.9 collective-permute-start.21
  164.5 0.7 fusion.16
  165.2 17.7 %collective-permute-done.23 = f32[16,256]{1,0:T(8,128)S(1)} collective-permute-done((f32[16,256]{1,0:T(8,128)S(1)}, f32[16,256]{1,0:T(8,128)S(1)}, u32[]{:S(2)}, u32[]{:S(2)}) %collective-permute-start.23) | collective-permute-done | bytes 16416 | tf_op jit(solution)/shard_map/ppermute | solution.py:435
  182.9 1.2 collective-permute-done.22
  184.7 4.8 %all-to-all-done.1 = bf16[256,16,128]{2,1,0:T(8,128)(2,1)S(1)} async-done(((bf16[256,16,128]{2,1,0:T(8,128)(2,1)}), bf16[256,16,128]{2,1,0:T(8,128)(2,1)S(1)}, u32[]{:S(2)}, u32[]{:S(2)}) %all-to-all-start.1) | async-done | bytes 1048608 | tf_op jit(solution)/shard_map/all_to_all | solution.py:440
  189.5 6.4 %row_grad.1 = f32[1,64,256]{2,1,0:T(8,128)} custom-call(s32[1,4,8192]{2,1,0:T(4,128)} %index_ref.3, s32[1,8192]{1,0:T(1,128)} %length_ref.3, bf16[4,64,16,128]{3,2,1,0:T(8,128)(2,1)S(1)} %bitcast.49), custom_call_target="tpu_custom_call" | custom-call | tf_op jit(solution)/shard_map/row_grad/pallas_call | solution.py:413
  (94 shorter events, 9.3 us)
Async XLA Ops:
  0.6 21.3 %copy-start = (bf16[13,256]{1,0:T(8,128)(2,1)S(1)}, bf16[13,256]{1,0:T(8,128)(2,1)}, u32[]{:S(2)}) copy-start(bf16[13,256]{1,0:T(8,128)(2,1)} %param.14) | copy-start | bytes 19972
  7.0 14.7 %copy-start.15 = (bf16[128,13]{0,1:T(8,128)(2,1)S(1)}, bf16[128,13]{0,1:T(8,128)(2,1)}, u32[]{:S(2)}) copy-start(bf16[128,13]{0,1:T(8,128)(2,1)} %param.13) | copy-start | bytes 9988
  7.0 44.9 %copy-start.10 = (s32[64]{0:T(128)S(1)}, s32[64]{0:T(128)}, u32[]{:S(2)}) copy-start(s32[64]{0:T(128)} %slot_ref.3) | copy-start | bytes 772
  7.0 52.3 %copy-start.18 = (bf16[512]{0:T(512)(128)(2,1)S(1)}, bf16[512]{0:T(512)(128)(2,1)}, u32[]{:S(2)}) copy-start(bf16[512]{0:T(512)(128)(2,1)} %param.16) | copy-start | bytes 3076
  7.0 64.0 %copy-start.1 = (bf16[2336,512]{1,0:T(8,128)(2,1)S(1)}, bf16[2336,512]{1,0:T(8,128)(2,1)}, u32[]{:S(2)}) copy-start(bf16[2336,512]{1,0:T(8,128)(2,1)} %weight_ref.1) | copy-start | bytes 7176196
  7.0 44.9 %all-to-all-start = ((bf16[256,16,128]{2,1,0:T(8,128)(2,1)}), bf16[256,16,128]{2,1,0:T(8,128)(2,1)S(1)}, u32[]{:S(2)}, u32[]{:S(2)}) async-start(bf16[256,16,128]{2,1,0:T(8,128)(2,1)} %bitcast.54), calls=%async_computation | async-start | bytes 2097152 | tf_op jit(solution)/shard_map/all_to_all | solution.py:440
  54.9 9.1 %collective-permute-start = (bf16[32,2432]{1,0:T(8,128)(2,1)}, bf16[32,2432]{1,0:T(8,128)(2,1)S(1)}, u32[]{:S(2)}, u32[]{:S(2)}) collective-permute-start(bf16[32,2432]{1,0:T(8,128)(2,1)} %get-tuple-element.21.f0), channel_id=1, source_target_pairs={{0,64},{64,128},{128,192},{192,0},{1,65},{65,129},{129,193},{193,1... | collective-permute-start | bytes 466952 | tf_op jit(solution)/shard_map/ppermute | solution.py:435
  55.9 13.7 %collective-permute-start.1 = (bf16[32,2432]{1,0:T(8,128)(2,1)}, bf16[32,2432]{1,0:T(8,128)(2,1)S(1)}, u32[]{:S(2)}, u32[]{:S(2)}) collective-permute-start(bf16[32,2432]{1,0:T(8,128)(2,1)} %get-tuple-element.21.f0), channel_id=1, source_target_pairs={{0,128},{64,192},{128,0},{192,64},{1,129},{65,193},{129,1},{193,65... | collective-permute-start | bytes 466952 | tf_op jit(solution)/shard_map/ppermute | solution.py:435
  56.9 13.4 %collective-permute-start.2 = (bf16[32,2432]{1,0:T(8,128)(2,1)}, bf16[32,2432]{1,0:T(8,128)(2,1)S(1)}, u32[]{:S(2)}, u32[]{:S(2)}) collective-permute-start(bf16[32,2432]{1,0:T(8,128)(2,1)} %get-tuple-element.21.f0), channel_id=1, source_target_pairs={{0,192},{64,0},{128,64},{192,128},{1,193},{65,1},{129,65},{193,129... | collective-permute-start | bytes 466952 | tf_op jit(solution)/shard_map/ppermute | solution.py:435
  60.7 23.6 %copy-start.16 = (pred[4]{0:T(512)(128)(4,1)}, pred[4]{0:T(512)(128)(4,1)S(1)}, u32[]{:S(2)}) copy-start(pred[4]{0:T(512)(128)(4,1)S(1)} %compare_and_fusion) | copy-start | bytes 16
  63.9 0.7 copy-start.3
  69.7 0.7 copy-start.5
  70.3 0.7 copy-start.7
  71.0 0.9 copy-start.4
  71.9 0.9 copy-start.6
  72.8 0.9 copy-start.8
  73.7 33.7 %copy-start.2 = (bf16[16,64,512]{2,1,0:T(8,128)(2,1)S(1)}, bf16[16,64,512]{2,1,0:T(8,128)(2,1)}, u32[]{:S(2)}) copy-start(bf16[16,64,512]{2,1,0:T(8,128)(2,1)} %get-tuple-element.34.vectors_ref) | copy-start | bytes 3145732
  76.8 0.7 copy-start.11
  77.5 0.7 copy-start.12
  78.2 0.7 copy-start.13
  78.8 5.5 %collective-permute-start.3 = (f32[8,128]{1,0:T(8,128)S(1)}, f32[8,128]{1,0:T(8,128)S(1)}, u32[]{:S(2)}, u32[]{:S(2)}) collective-permute-start(f32[8,128]{1,0:T(8,128)S(1)} %get-tuple-element.22.p0), channel_id=1, source_target_pairs={{0,64},{64,128},{128,192},{192,0},{1,65},{65,129},{129,193},{193,1... | collective-permute-start | bytes 12296 | tf_op jit(solution)/shard_map/ppermute | solution.py:435
  81.9 4.5 %collective-permute-start.4 = (f32[8,128]{1,0:T(8,128)S(1)}, f32[8,128]{1,0:T(8,128)S(1)}, u32[]{:S(2)}, u32[]{:S(2)}) collective-permute-start(f32[8,128]{1,0:T(8,128)S(1)} %get-tuple-element.22.p0), channel_id=1, source_target_pairs={{0,128},{64,192},{128,0},{192,64},{1,129},{65,193},{129,1},{193,65... | collective-permute-start | bytes 12296 | tf_op jit(solution)/shard_map/ppermute | solution.py:435
  82.5 3.9 %collective-permute-start.5 = (f32[8,128]{1,0:T(8,128)S(1)}, f32[8,128]{1,0:T(8,128)S(1)}, u32[]{:S(2)}, u32[]{:S(2)}) collective-permute-start(f32[8,128]{1,0:T(8,128)S(1)} %get-tuple-element.22.p0), channel_id=1, source_target_pairs={{0,192},{64,0},{128,64},{192,128},{1,193},{65,1},{129,65},{193,129... | collective-permute-start | bytes 12296 | tf_op jit(solution)/shard_map/ppermute | solution.py:435
  90.2 28.2 %collective-permute-start.6 = (bf16[16,16,2432]{2,1,0:T(8,128)(2,1)}, bf16[16,16,2432]{2,1,0:T(8,128)(2,1)}, u32[]{:S(2)}, u32[]{:S(2)}) collective-permute-start(bf16[16,16,2432]{2,1,0:T(8,128)(2,1)} %get-tuple-element.28), channel_id=1, source_target_pairs={{0,1},{1,0},{2,3},{3,2},{4,5},{5,4},{6,7},{7,6},{8,9},{9,8},{10,11... | collective-permute-start | bytes 3735560 | tf_op jit(solution)/shard_map/ppermute | solution.py:435
  90.2 8.1 %collective-permute-start.10 = (bf16[32,2432]{1,0:T(8,128)(2,1)}, bf16[32,2432]{1,0:T(8,128)(2,1)S(1)}, u32[]{:S(2)}, u32[]{:S(2)}) collective-permute-start(bf16[32,2432]{1,0:T(8,128)(2,1)} %copy-done.13), channel_id=1, source_target_pairs={{0,192},{64,0},{128,64},{192,128},{1,193},{65,1},{129,65},{193,129... | collective-permute-start | bytes 466952 | tf_op jit(solution)/shard_map/ppermute | solution.py:435
  93.4 13.9 %collective-permute-start.11 = (bf16[32,2432]{1,0:T(8,128)(2,1)}, bf16[32,2432]{1,0:T(8,128)(2,1)S(1)}, u32[]{:S(2)}, u32[]{:S(2)}) collective-permute-start(bf16[32,2432]{1,0:T(8,128)(2,1)} %copy-done.12), channel_id=1, source_target_pairs={{0,128},{64,192},{128,0},{192,64},{1,129},{65,193},{129,1},{193,65... | collective-permute-start | bytes 466952 | tf_op jit(solution)/shard_map/ppermute | solution.py:435
  93.5 13.9 %collective-permute-start.12 = (bf16[32,2432]{1,0:T(8,128)(2,1)}, bf16[32,2432]{1,0:T(8,128)(2,1)S(1)}, u32[]{:S(2)}, u32[]{:S(2)}) collective-permute-start(bf16[32,2432]{1,0:T(8,128)(2,1)} %copy-done.11), channel_id=1, source_target_pairs={{0,64},{64,128},{128,192},{192,0},{1,65},{65,129},{129,193},{193,1... | collective-permute-start | bytes 466952 | tf_op jit(solution)/shard_map/ppermute | solution.py:435
  107.4 0.9 copy-start.9
  108.3 10.1 %copy-start.14 = (bf16[16,16,2432]{2,1,0:T(8,128)(2,1)S(1)}, bf16[16,16,2432]{2,1,0:T(8,128)(2,1)}, u32[]{:S(2)}) copy-start(bf16[16,16,2432]{2,1,0:T(8,128)(2,1)} %get-tuple-element.27) | copy-start | bytes 3735556
  112.5 1.2 collective-permute-start.13
  113.7 9.0 %collective-permute-start.15 = (f32[16,256]{1,0:T(8,128)S(1)}, f32[16,256]{1,0:T(8,128)S(1)}, u32[]{:S(2)}, u32[]{:S(2)}) collective-permute-start(f32[16,256]{1,0:T(8,128)S(1)} %add.233), channel_id=1, source_target_pairs={{0,16},{16,32},{32,48},{48,0},{1,17},{17,33},{33,49},{49,1},{2,18}... | collective-permute-start | bytes 49160 | tf_op jit(solution)/shard_map/ppermute | solution.py:435
  114.7 8.9 %collective-permute-start.16 = (f32[16,256]{1,0:T(8,128)S(1)}, f32[16,256]{1,0:T(8,128)S(1)}, u32[]{:S(2)}, u32[]{:S(2)}) collective-permute-start(f32[16,256]{1,0:T(8,128)S(1)} %add.233), channel_id=1, source_target_pairs={{0,48},{16,0},{32,16},{48,32},{1,49},{17,1},{33,17},{49,33},{2,50}... | collective-permute-start | bytes 49160 | tf_op jit(solution)/shard_map/ppermute | solution.py:435
  115.7 7.9 %collective-permute-start.14 = (f32[16,256]{1,0:T(8,128)S(1)}, f32[16,256]{1,0:T(8,128)S(1)}, u32[]{:S(2)}, u32[]{:S(2)}) collective-permute-start(f32[16,256]{1,0:T(8,128)S(1)} %add.233), channel_id=1, source_target_pairs={{0,32},{16,48},{32,0},{48,16},{1,33},{17,49},{33,1},{49,17},{2,34}... | collective-permute-start | bytes 49160 | tf_op jit(solution)/shard_map/ppermute | solution.py:435
  120.1 10.3 %collective-permute-start.9 = (bf16[64,2432]{1,0:T(8,128)(2,1)S(1)}, bf16[64,2432]{1,0:T(8,128)(2,1)S(1)}, u32[]{:S(2)}, u32[]{:S(2)}) collective-permute-start(bf16[64,2432]{1,0:T(8,128)(2,1)S(1)} %get-tuple-element.42), channel_id=1, source_target_pairs={{0,48},{16,0},{32,16},{48,32},{1,49},{17,1},{33,17},{49,33},{2,50}... | collective-permute-start | bytes 933896 | tf_op jit(solution)/shard_map/ppermute | solution.py:435
  120.2 11.9 %collective-permute-start.8 = (bf16[64,2432]{1,0:T(8,128)(2,1)S(1)}, bf16[64,2432]{1,0:T(8,128)(2,1)S(1)}, u32[]{:S(2)}, u32[]{:S(2)}) collective-permute-start(bf16[64,2432]{1,0:T(8,128)(2,1)S(1)} %get-tuple-element.43), channel_id=1, source_target_pairs={{0,32},{16,48},{32,0},{48,16},{1,33},{17,49},{33,1},{49,17},{2,34}... | collective-permute-start | bytes 933896 | tf_op jit(solution)/shard_map/ppermute | solution.py:435
  122.7 14.4 %collective-permute-start.7 = (bf16[64,2432]{1,0:T(8,128)(2,1)S(1)}, bf16[64,2432]{1,0:T(8,128)(2,1)S(1)}, u32[]{:S(2)}, u32[]{:S(2)}) collective-permute-start(bf16[64,2432]{1,0:T(8,128)(2,1)S(1)} %get-tuple-element.41), channel_id=1, source_target_pairs={{0,16},{16,32},{32,48},{48,0},{1,17},{17,33},{33,49},{49,1},{2,18}... | collective-permute-start | bytes 933896 | tf_op jit(solution)/shard_map/ppermute | solution.py:435
  137.3 11.0 %copy-start.17 = (pred[4]{0:T(512)(128)(4,1)S(1)}, pred[4]{0:T(512)(128)(4,1)}, u32[]{:S(2)}) copy-start(pred[4]{0:T(512)(128)(4,1)} %copy-done.16) | copy-start | bytes 16
  137.3 5.7 %collective-permute-start.19 = (bf16[16,2944]{1,0:T(8,128)(2,1)S(1)}, bf16[16,2944]{1,0:T(8,128)(2,1)S(1)}, u32[]{:S(2)}, u32[]{:S(2)}) collective-permute-start(bf16[16,2944]{1,0:T(8,128)(2,1)S(1)} %get-tuple-element.52), channel_id=1, source_target_pairs={{0,6},{2,0},{4,2},{6,4},{1,7},{3,1},{5,3},{7,5},{8,14},{10,8},{12,... | collective-permute-start | bytes 282632 | tf_op jit(solution)/shard_map/ppermute | solution.py:435
  139.0 6.6 %collective-permute-start.18 = (bf16[16,2944]{1,0:T(8,128)(2,1)S(1)}, bf16[16,2944]{1,0:T(8,128)(2,1)S(1)}, u32[]{:S(2)}, u32[]{:S(2)}) collective-permute-start(bf16[16,2944]{1,0:T(8,128)(2,1)S(1)} %get-tuple-element.53), channel_id=1, source_target_pairs={{0,4},{2,6},{4,0},{6,2},{1,5},{3,7},{5,1},{7,3},{8,12},{10,14},{12... | collective-permute-start | bytes 282632 | tf_op jit(solution)/shard_map/ppermute | solution.py:435
  139.5 7.0 %collective-permute-start.17 = (bf16[16,2944]{1,0:T(8,128)(2,1)S(1)}, bf16[16,2944]{1,0:T(8,128)(2,1)S(1)}, u32[]{:S(2)}, u32[]{:S(2)}) collective-permute-start(bf16[16,2944]{1,0:T(8,128)(2,1)S(1)} %get-tuple-element.51), channel_id=1, source_target_pairs={{0,2},{2,4},{4,6},{6,0},{1,3},{3,5},{5,7},{7,1},{8,10},{10,12},{12... | collective-permute-start | bytes 282632 | tf_op jit(solution)/shard_map/ppermute | solution.py:435
  146.7 12.3 %collective-permute-start.20 = (bf16[8,3456]{1,0:T(8,128)(2,1)S(1)}, bf16[8,3456]{1,0:T(8,128)(2,1)S(1)}, u32[]{:S(2)}, u32[]{:S(2)}) collective-permute-start(bf16[8,3456]{1,0:T(8,128)(2,1)S(1)} %constant_dynamic-update-slice_fusion), channel_id=1, source_target_pairs={{0,8},{8,0},{1,9},{9,1},{2,10},{10,2},{3,11},{11,3},{4,12},{12,4},... | collective-permute-start | bytes 165896 | tf_op jit(solution)/shard_map/ppermute | solution.py:435
  149.0 40.5 %all-to-all-start.1 = ((bf16[256,16,128]{2,1,0:T(8,128)(2,1)}), bf16[256,16,128]{2,1,0:T(8,128)(2,1)S(1)}, u32[]{:S(2)}, u32[]{:S(2)}) async-start(bf16[256,16,128]{2,1,0:T(8,128)(2,1)} %bitcast.23), calls=%async_computation.1 | async-start | bytes 2097152 | tf_op jit(solution)/shard_map/all_to_all | solution.py:440
  159.0 23.9 %collective-permute-start.23 = (f32[16,256]{1,0:T(8,128)S(1)}, f32[16,256]{1,0:T(8,128)S(1)}, u32[]{:S(2)}, u32[]{:S(2)}) collective-permute-start(f32[16,256]{1,0:T(8,128)S(1)} %fusion.12), channel_id=1, source_target_pairs={{0,192},{64,0},{128,64},{192,128},{1,193},{65,1},{129,65},{193,129... | collective-permute-start | bytes 49160 | tf_op jit(solution)/shard_map/ppermute | solution.py:435
  163.0 21.1 %collective-permute-start.22 = (f32[16,256]{1,0:T(8,128)S(1)}, f32[16,256]{1,0:T(8,128)S(1)}, u32[]{:S(2)}, u32[]{:S(2)}) collective-permute-start(f32[16,256]{1,0:T(8,128)S(1)} %fusion.12), channel_id=1, source_target_pairs={{0,64},{64,128},{128,192},{192,0},{1,65},{65,129},{129,193},{193,1... | collective-permute-start | bytes 49160 | tf_op jit(solution)/shard_map/ppermute | solution.py:435
  163.0 21.1 %collective-permute-start.21 = (f32[16,256]{1,0:T(8,128)S(1)}, f32[16,256]{1,0:T(8,128)S(1)}, u32[]{:S(2)}, u32[]{:S(2)}) collective-permute-start(f32[16,256]{1,0:T(8,128)S(1)} %fusion.12), channel_id=1, source_target_pairs={{0,128},{64,192},{128,0},{192,64},{1,129},{65,193},{129,1},{193,65... | collective-permute-start | bytes 49160 | tf_op jit(solution)/shard_map/ppermute | solution.py:435

commit v4 on v3

--- a/solution.py
+++ b/solution.py
@@ -20,6 +20,7 @@
 FEAT = 2336
 WIDE = 2432
 STEP = 8
+LABEL_LANE = 36
 
 
 def pieces():
@@ -126,7 +127,7 @@
     return jnp.concatenate(tiles, axis=1)
 
 
-def interact_kernel(slot_ref, arrived_ref, mine_ref, out_ref, vectors_ref, spaced, gram, edge):
+def interact_kernel(slot_ref, arrived_ref, mine_ref, label_ref, out_ref, vectors_ref, spaced, gram, edge):
     def place(table, carry):
         start = pl.multiple_of(slot_ref[table] * ROWS, ROWS)
         for part in range(4):
@@ -163,16 +164,16 @@
                     out_ref[where, tile * LANES : (tile + 1) * LANES] = filled.astype(BF16)
                     tile, filled = at, jnp.zeros((ROWS, LANES), F32)
                 filled = jnp.where((lane >= first) & (lane < end), moved, filled)
+        filled = jnp.where(lane == LABEL_LANE, label_ref[where, :], filled)
         out_ref[where, tile * LANES : (tile + 1) * LANES] = filled.astype(BF16)
 
 
-def interact(table_slot, arrived, mine):
+def interact(table_slot, arrived, mine, labels):
     return pl.pallas_call(
         interact_kernel,
         in_specs=[
             pl.BlockSpec(memory_space=pltpu.SMEM),
-            pl.BlockSpec(memory_space=pltpu.VMEM),
-            pl.BlockSpec(memory_space=pltpu.VMEM),
+            *vmem_specs(3),
         ],
         out_specs=[pl.BlockSpec(memory_space=pltpu.VMEM)] * 2,
         out_shape=[
@@ -186,7 +187,7 @@
         ],
         compiler_params=pltpu.CompilerParams(vmem_limit_bytes=16 << 20),
         name="interact",
-    )(table_slot, arrived, mine)
+    )(table_slot, arrived, mine, labels)
 
 
 def top_kernel(
@@ -228,15 +229,32 @@
     )(*parts, top_weight, out_weight)
 
 
+def own_logits(even, r0, up1, down1, up2, down2):
+    return (r0 + turned(up1, -32)) + (turned(down1, -64) + turned(jnp.where(even, up2, down2), -96))
+
+
 def weight_grad_kernel(
-    core_ref, p0, p1, p2, p3, labels_ref, all_ref, delta_ref, hidden_ref,
-    own_ref, other_ref, logit_ref, dlogit_ref, grad,
+    place_ref, p0, p1, p2, p3, p4, p5, all_ref, delta_ref, hidden_ref, own_ref, other_ref, grad,
 ):
-    logits = (p0[...] + turned(p2[...], 64)) + (turned(p1[...], 32) + turned(p3[...], 96))
-    logit_ref[...] = logits
-    dlogit = (jax.nn.sigmoid(logits) - labels_ref[0:1, :]) * (1.0 / 128.0)
-    dlogit_ref[...] = dlogit
-    column = dlogit.T[:, 0:1]
+    even = place_ref[1] == 0
+    r0, up1, down1, up2, down2, far = (p[...] for p in (p0, p1, p2, p3, p4, p5))
+
+    def at(x, slot, to):
+        return turned(x, 32 * (to - slot))
+
+    own = own_logits(even, r0, up1, down1, up2, down2)
+    below = at(down1, 0, 1) + r0 + at(down2, 2, 1) + at(jnp.where(even, far, up1), 3, 1)
+    above = at(up1, 0, 2) + at(up2, 1, 2) + r0 + at(jnp.where(even, down1, far), 3, 2)
+    across = r0 + jnp.where(
+        even,
+        at(down2, 0, 3) + at(down1, 1, 3) + at(far, 2, 3),
+        at(up2, 0, 3) + at(far, 1, 3) + at(up1, 2, 3),
+    )
+    block = lane_iota(8) // 32
+    logits = jnp.where(block == 0, own, jnp.where(block == 1, below, jnp.where(block == 2, above, across)))
+    tile = all_ref[:, WIDE - LANES : WIDE].astype(F32)
+    labels = jnp.sum(jnp.where(lane_iota(128) == LABEL_LANE, tile, 0.0), axis=1, keepdims=True)
+    column = (jax.nn.sigmoid(logits.T[:, 0:1]) - labels) * (1.0 / 128.0)
     delta = (delta_ref[...].astype(F32) * column).astype(BF16)
     last = WIDE - LANES
     grad[:, 0:last] = lax.dot_general(
@@ -251,7 +269,7 @@
         (((0,), (0,)), ((), ())),
         preferred_element_type=F32,
     )
-    core = core_ref[0]
+    core = place_ref[0]
     for x in range(4):
         for y in range(4):
             for ref, which in ((own_ref, core), (other_ref, 1 - core)):
@@ -262,28 +280,29 @@
                 ref[x * 4 + y] = jnp.concatenate(both, axis=0).astype(BF16)
 
 
-def weight_grad(core, partials, labels, features, delta, hidden):
+def weight_grad(place, partials, features, delta, hidden):
     return pl.pallas_call(
         weight_grad_kernel,
-        in_specs=[pl.BlockSpec(memory_space=pltpu.SMEM)] + vmem_specs(8),
-        out_specs=vmem_specs(4),
+        in_specs=[pl.BlockSpec(memory_space=pltpu.SMEM)] + vmem_specs(9),
+        out_specs=vmem_specs(2),
         out_shape=[
             hbm((16, 16, WIDE), BF16),
             hbm((16, 16, WIDE), BF16),
-            jax.ShapeDtypeStruct((8, LANES), F32),
-            jax.ShapeDtypeStruct((8, LANES), F32),
         ],
         scratch_shapes=[pltpu.VMEM((512, WIDE), F32)],
         compiler_params=pltpu.CompilerParams(vmem_limit_bytes=32 << 20),
         name="weight_grad",
-    )(core, *partials, labels, *in_hbm(features, delta, hidden))
+    )(place, *partials, *in_hbm(features, delta, hidden))
 
 
 def spread_kernel(
-    slot_ref, z0, z1, z2, z3, dlogit_ref, vectors_ref, mine_ref, slope_ref, dense_ref,
-    back_ref, bottom_ref, dfeat, upper, edge, right, dvec, dedge,
+    slot_ref, place_ref, z0, z1, z2, z3, p0, p1, p2, p3, p4, label_ref, vectors_ref, mine_ref,
+    slope_ref, dense_ref, back_ref, bottom_ref, logit_ref, dfeat, upper, edge, right, dvec, dedge,
 ):
-    column = dlogit_ref[...].T[0:32, 0:1]
+    logits = own_logits(place_ref[1] == 0, p0[...], p1[...], p2[...], p3[...], p4[...])
+    logit_ref[...] = logits
+    labels = jnp.sum(jnp.where(lane_iota(32) == LABEL_LANE, label_ref[...], 0.0), axis=1, keepdims=True)
+    column = (jax.nn.sigmoid(logits.T[0:32, 0:1]) - labels) * (1.0 / 128.0)
     summed = z0[...].astype(F32) + z1[...].astype(F32) + z2[...].astype(F32) + z3[...].astype(F32)
     dfeat[...] = summed * column
     lane = lane_iota(ROWS)
@@ -361,15 +380,15 @@
     )
 
 
-def spread(table_slot, zs, dlogit, vectors, mine, slope, dense):
+def spread(table_slot, place, zs, partials, labels, vectors, mine, slope, dense):
     return pl.pallas_call(
         spread_kernel,
-        in_specs=[pl.BlockSpec(memory_space=pltpu.SMEM)]
-        + [pl.BlockSpec(memory_space=pltpu.VMEM)] * 9,
-        out_specs=[pl.BlockSpec(memory_space=pltpu.VMEM)] * 2,
+        in_specs=[pl.BlockSpec(memory_space=pltpu.SMEM)] * 2 + vmem_specs(14),
+        out_specs=vmem_specs(3),
         out_shape=[
             hbm((4, TAB, ROWS, LANES), BF16),
             jax.ShapeDtypeStruct((16, EMB), F32),
+            jax.ShapeDtypeStruct((8, LANES), F32),
         ],
         scratch_shapes=[
             pltpu.VMEM((2 * ROWS, WIDE), F32),
@@ -381,7 +400,7 @@
         ],
         compiler_params=pltpu.CompilerParams(vmem_limit_bytes=16 << 20),
         name="spread",
-    )(table_slot, *zs, dlogit, vectors, mine, slope, dense)
+    )(table_slot, place, *zs, *partials, labels, *in_hbm(vectors), mine, slope, dense)
 
 
 def row_grad_kernel(index_ref, length_ref, back_ref, out_ref, total, counted, moved):
@@ -433,6 +452,14 @@
 def shifted(x, axis, shift):
     size = lax.axis_size(axis)
     return lax.ppermute(x, axis, [(i, (i + shift) % size) for i in range(size)])
+
+
+def ring_sent(x, moves):
+    def spot(place):
+        return place % 4 * 2 + place % 8 // 4
+
+    pairs = [(spot(p), spot(p + moves(p))) for p in range(8)]
+    return lax.ppermute(x, ("col", "grp_1"), pairs)
 
 
 def exchange_all(x):
@@ -509,26 +536,39 @@
     mine = jax.nn.silu(mine_pre).astype(BF16).astype(F32)
     mine_slope = silu_slope(mine_pre)
     dense_wide = jnp.pad(dense_mine.astype(F32), ((0, 0), (0, 16 - dense_mine.shape[1])))
-    order = (me - jnp.arange(4)) % 4
-    labels_rel = jnp.take(
-        jnp.transpose(labels.reshape(2, 4, ROWS), (1, 0, 2)), order, axis=0
-    ).reshape(1, LANES).astype(F32)
+    labels_mine = lax.dynamic_index_in_dim(labels.reshape(2, 4, ROWS), me, 1, keepdims=False)
+    labels_mine = jnp.broadcast_to(labels_mine.astype(F32).reshape(2 * ROWS, 1), (2 * ROWS, LANES))
+    place = jnp.stack([core, me % 2]).astype(jnp.int32)
     out_weight_row = out_weight.astype(F32).reshape(1, -1)
 
-    part, vectors = interact(table_slot, arrived, mine)
-    parts = [part] + [shifted(part, "col", away) for away in (1, 2, 3)]
+    part, vectors = interact(table_slot, arrived, mine, labels_mine)
+    parts = [
+        part,
+        ring_sent(part, lambda p: 1),
+        ring_sent(part, lambda p: -1),
+        ring_sent(part, lambda p: -2 if p % 2 else 2),
+    ]
     features, *zs, partial, delta, hidden = top(parts, top_weight, out_weight_row)
-    zs = [zs[0]] + [shifted(zs[away], "col", -away) for away in (1, 2, 3)]
-    partials = [partial] + [shifted(partial, "col", away) for away in (1, 2, 3)]
-    own, other, logits_rel, dlogit = weight_grad(
-        core.astype(jnp.int32).reshape(1), partials, labels_rel, features, delta, hidden
+    zs = [
+        zs[0],
+        ring_sent(zs[1], lambda p: -1),
+        ring_sent(zs[2], lambda p: 1),
+        ring_sent(zs[3], lambda p: 2 if p % 2 else -2),
+    ]
+    partials = [
+        partial,
+        ring_sent(partial, lambda p: -1),
+        ring_sent(partial, lambda p: 1),
+        ring_sent(partial, lambda p: -2),
+        ring_sent(partial, lambda p: 2),
+        ring_sent(partial, lambda p: 3 if p % 2 else -3),
+    ]
+    own, other = weight_grad(place, partials, features, delta, hidden)
+    back, bottom, logits_mine = spread(
+        table_slot, place, zs, partials[:5], labels_mine, vectors, mine, mine_slope, dense_wide
     )
-    back, bottom = spread(table_slot, zs, dlogit, vectors, mine, mine_slope, dense_wide)
     returned = exchange_all(back)
     grad_rows = jnp.transpose(row_grad(pool_index, bag_length, returned), (0, 2, 1))
-
-    logits = jnp.take(logits_rel[0].reshape(4, 2, ROWS), order, axis=0)
-    logits = jnp.transpose(logits, (1, 0, 2)).reshape(LANES)
 
     other = shifted(other, "grp_3", 1)
     grad = (own.astype(F32) + other.astype(F32)).astype(BF16).reshape(4, 64, WIDE)
@@ -539,7 +579,14 @@
     grad, bottom = reduced_to(grad.reshape(2, 8, WIDE), "grp_1", bottom)
     grad_top = jnp.transpose(grad[:, 0:FEAT])
     grad_out = grad[:, FEAT] + grad[:, FEAT + 1]
-    grad_bottom = summed_over(bottom, "col")[0 : bottom_weight.shape[0]]
+    spots = jnp.tile(logits_mine[0:1, 0:32], (1, EMB // 32))
+    row = lax.broadcasted_iota(jnp.int32, bottom.shape, 0)
+    lane = lax.broadcasted_iota(jnp.int32, bottom.shape, 1)
+    spare = bottom_weight.shape[0]
+    bottom = jnp.where(row == spare, jnp.where(lane // 32 == me, spots, 0.0), bottom)
+    bottom = summed_over(bottom, "col")
+    grad_bottom = bottom[0:spare]
+    logits = jnp.transpose(bottom[spare, 0:LANES].reshape(4, 2, ROWS), (1, 0, 2)).reshape(LANES)
     return (logits, grad_top, grad_out, grad_bottom, grad_rows)
 
 

time: 198 us -> 186 us (0.939)
  waiting for transfers between devices: 97.3 us -> 87.7 us
  local copies, waits for them, and re-layouts: 11.4 us -> 3.45 us
  starting transfers between devices: 55.9 us -> 61.2 us
    ppermute x24 -> x15, waiting for transfers between devices: 62.7 us -> 37.5 us  [shifted(): return lax.ppermute(x, axis, [(i, (i + shift) % size) for i in range(size)])]
    ppermute x0 -> x11, waiting for transfers between devices: none -> 16.4 us  [ring_sent(): return lax.ppermute(x, ('col', 'grp_1'), pairs)]
    ppermute x0 -> x11, starting transfers between devices: none -> 14.7 us  [ring_sent(): return lax.ppermute(x, ('col', 'grp_1'), pairs)]
    ppermute x24 -> x15, starting transfers between devices: 31.3 us -> 21.5 us  [shifted(): return lax.ppermute(x, axis, [(i, (i + shift) % size) for i in range(size)])]
    unnamed x43 -> x25, local copies, waits for them, and re-layouts: 7.83 us -> 1.53 us
  transfers between devices with their start and end apart: 26 -> 28, of which waited for: 16 -> 17; matrix products, arithmetic and copies ran while one was open for 4% -> 2% of each run, Pallas kernels for 2% -> 3%
where the time goes in v4:
time: 186 us; the launch traced here: 183 us
  waiting for transfers between devices  87.7 us (47%)
  starting transfers between devices  61.2 us (33%)
  Pallas kernels  27.6 us (15%)
  local copies, waits for them, and re-layouts  3.45 us (2%)
  other arithmetic  2.22 us (1%)
    ppermute x15, waiting for transfers between devices, shifted(): return lax.ppermute(x, axis, [(i, (i + shift) % size) for i in range(size)])  37.5 us
    all_to_all x2, waiting for transfers between devices, exchange_all(): lax.all_to_all(flat, COL_GRP, split_axis=0, concat_axis=0, tiled=True)  33.8 us
    all_to_all x2, starting transfers between devices, exchange_all(): lax.all_to_all(flat, COL_GRP, split_axis=0, concat_axis=0, tiled=True)  24.9 us
    ppermute x15, starting transfers between devices, shifted(): return lax.ppermute(x, axis, [(i, (i + shift) % size) for i in range(size)])  21.5 us
    ppermute x11, waiting for transfers between devices, ring_sent(): return lax.ppermute(x, ('col', 'grp_1'), pairs)  16.4 us
    ppermute x11, starting transfers between devices, ring_sent(): return lax.ppermute(x, ('col', 'grp_1'), pairs)  14.7 us
    pallas_call x1, Pallas kernels, row_grad(): pl.pallas_call(row_grad_kernel, grid=(TAB // STEP,), in_specs=[pl.BlockSp...  6.44 us
    pallas_call x1, Pallas kernels, pool(): pl.pallas_call(pool_kernel, grid=(TAB // STEP,), in_specs=[pl.BlockSpec((...  6.33 us
  transfers between devices with their start and end apart: 28, of which 17 were waited for; matrix products, arithmetic and copies ran while one was open for 2% of the time, Pallas kernels for 3%

profile of v4, /device:TPU:4, one launch (start us, length us, event | category | flops | bytes accessed | tf_op | source)
XLA Modules:
  0.0 183.3 jit_solution(6338959863698555061)
XLA Ops:
  0.6 6.3 %pool.1 = bf16[4,64,16,128]{3,2,1,0:T(8,128)(2,1)} custom-call(s32[1,4,8192]{2,1,0:T(4,128)} %index_ref.3, s32[1,8192]{1,0:T(1,128)} %length_ref.3, bf16[1,64,256]{2,1,0:T(8,128)(2,1)} %bitcast.56), custom_call_target="tpu_custom_call" | custom-call | tf_op jit(solution)/shard_map/pool/pallas_call | solution.py:104
  7.0 14.7 %all-to-all-start = ((bf16[256,16,128]{2,1,0:T(8,128)(2,1)}), bf16[256,16,128]{2,1,0:T(8,128)(2,1)S(1)}, u32[]{:S(2)}, u32[]{:S(2)}) async-start(bf16[256,16,128]{2,1,0:T(8,128)(2,1)} %bitcast.52), calls=%async_computation | async-start | bytes 2097152 | tf_op jit(solution)/shard_map/all_to_all | solution.py:467
  22.7 29.1 %all-to-all-done = bf16[256,16,128]{2,1,0:T(8,128)(2,1)S(1)} async-done(((bf16[256,16,128]{2,1,0:T(8,128)(2,1)}), bf16[256,16,128]{2,1,0:T(8,128)(2,1)S(1)}, u32[]{:S(2)}, u32[]{:S(2)}) %all-to-all-start) | async-done | bytes 1048608 | tf_op jit(solution)/shard_map/all_to_all | solution.py:467
  51.9 2.9 %interact.1 = (bf16[32,2432]{1,0:T(8,128)(2,1)}, bf16[16,64,512]{2,1,0:T(8,128)(2,1)}) custom-call(s32[64]{0:T(128)S(1)} %copy-done.3, bf16[4,64,16,128]{3,2,1,0:T(8,128)(2,1)S(1)} %bitcast.48, f32[32,256]{1,0:T(8,128)S(1)} %get-tuple-element.48.mine_ref, f32[32,128]{1,0:T(8,128)S(1)} %broadcast_in_dim.17.label_ref), custom_call_target="tpu_custom_call" | custom-call | tf_op jit(solution)/shard_map/interact/pallas_call | solution.py:172
  54.8 1.5 collective-permute-start.2
  56.5 1.9 %collective-permute-start = (bf16[32,2432]{1,0:T(8,128)(2,1)}, bf16[32,2432]{1,0:T(8,128)(2,1)S(1)}, u32[]{:S(2)}, u32[]{:S(2)}) collective-permute-start(bf16[32,2432]{1,0:T(8,128)(2,1)} %get-tuple-element.20.f0), channel_id=1, source_target_pairs={{0,64},{64,128},{128,192},{192,8},{8,72},{72,136},{136,200},{200,0... | collective-permute-start | bytes 466952 | tf_op jit(solution)/shard_map/ppermute | solution.py:462
  58.4 0.7 reshape.82
  59.1 5.0 %collective-permute-done.2.f3 = bf16[32,2432]{1,0:T(8,128)(2,1)S(1)} collective-permute-done((bf16[32,2432]{1,0:T(8,128)(2,1)}, bf16[32,2432]{1,0:T(8,128)(2,1)S(1)}, u32[]{:S(2)}, u32[]{:S(2)}) %collective-permute-start.2) | collective-permute-done | bytes 155680 | tf_op jit(solution)/shard_map/ppermute | solution.py:462
  64.2 2.3 %collective-permute-done.f1 = bf16[32,2432]{1,0:T(8,128)(2,1)S(1)} collective-permute-done((bf16[32,2432]{1,0:T(8,128)(2,1)}, bf16[32,2432]{1,0:T(8,128)(2,1)S(1)}, u32[]{:S(2)}, u32[]{:S(2)}) %collective-permute-start) | collective-permute-done | bytes 155680 | tf_op jit(solution)/shard_map/ppermute | solution.py:462
  66.5 3.0 %top.1 = (bf16[128,2432]{1,0:T(8,128)(2,1)}, bf16[32,2432]{1,0:T(8,128)(2,1)}, bf16[32,2432]{1,0:T(8,128)(2,1)S(1)}, bf16[32,2432]{1,0:T(8,128)(2,1)S(1)}, bf16[...) custom-call(bf16[32,2432]{1,0:T(8,128)(2,1)} %get-tuple-element.20.f0, ...), custom_call_target="tpu_custom_call" | custom-call | tf_op jit(solution)/shard_map/top/pallas_call | solution.py:216
  69.5 3.0 %collective-permute-start.9 = (f32[8,128]{1,0:T(8,128)S(1)}, f32[8,128]{1,0:T(8,128)S(1)}, u32[]{:S(2)}, u32[]{:S(2)}) collective-permute-start(f32[8,128]{1,0:T(8,128)S(1)} %get-tuple-element.25.p0), channel_id=1, source_target_pairs={{0,128},{64,192},{128,8},{192,72},{8,136},{72,200},{136,0},{200,64... | collective-permute-start | bytes 12296 | tf_op jit(solution)/shard_map/ppermute | solution.py:462
  72.4 1.2 collective-permute-start.8
  73.6 2.2 %collective-permute-start.7 = (f32[8,128]{1,0:T(8,128)S(1)}, f32[8,128]{1,0:T(8,128)S(1)}, u32[]{:S(2)}, u32[]{:S(2)}) collective-permute-start(f32[8,128]{1,0:T(8,128)S(1)} %get-tuple-element.25.p0), channel_id=1, source_target_pairs={{0,64},{64,128},{128,192},{192,8},{8,72},{72,136},{136,200},{200,0... | collective-permute-start | bytes 12296 | tf_op jit(solution)/shard_map/ppermute | solution.py:462
  75.8 1.1 collective-permute-start.6
  76.9 1.5 collective-permute-done.7.p2
  78.4 1.0 collective-permute-done.6.p1
  79.4 3.9 %weight_grad.1 = (bf16[16,16,2432]{2,1,0:T(8,128)(2,1)}, bf16[16,16,2432]{2,1,0:T(8,128)(2,1)}) custom-call(s32[2]{0:T(128)S(1)} %pad_add_fusion.place_ref, f32[8,128]{1,0:T(8,128)S(1)} %get-tuple-element.25.p0, f32[8,128]{1,0:T(8,128)S(1)} %collective-permute-done.6.p1, f32[8,128]{1,0:T(8,128)S(1)} %collective-permute-done.7.p2, ...), custom_call_target="tpu_custom_call" | custom-call | tf_op jit(solution)/shard_map/weight_grad/pallas_call | solution.py:284
  83.2 2.3 %collective-permute-start.3 = (bf16[32,2432]{1,0:T(8,128)(2,1)S(1)}, bf16[32,2432]{1,0:T(8,128)(2,1)S(1)}, u32[]{:S(2)}, u32[]{:S(2)}) collective-permute-start(bf16[32,2432]{1,0:T(8,128)(2,1)S(1)} %get-tuple-element.22), channel_id=1, source_target_pairs={{0,200},{64,0},{128,64},{192,128},{8,192},{72,8},{136,72},{200,136... | collective-permute-start | bytes 466952 | tf_op jit(solution)/shard_map/ppermute | solution.py:462
  85.5 1.5 collective-permute-start.5
  87.1 5.9 %collective-permute-done.3.z1 = bf16[32,2432]{1,0:T(8,128)(2,1)S(1)} collective-permute-done((bf16[32,2432]{1,0:T(8,128)(2,1)S(1)}, bf16[32,2432]{1,0:T(8,128)(2,1)S(1)}, u32[]{:S(2)}, u32[]{:S(2)}) %collective-permute-start.3) | collective-permute-done | bytes 155680 | tf_op jit(solution)/shard_map/ppermute | solution.py:462
  93.0 0.6 collective-permute-done.4.z2
  93.6 0.9 copy-done.2
  94.5 5.0 %spread.1 = (bf16[4,64,16,128]{3,2,1,0:T(8,128)(2,1)}, f32[16,256]{1,0:T(8,128)S(1)}, f32[8,128]{1,0:T(8,128)S(1)}) custom-call(s32[64]{0:T(128)S(1)} %copy-done.3, s32[2]{0:T(128)S(1)} %pad_add_fusion.place_ref, bf16[32,2432]{1,0:T(8,128)(2,1)S(1)} %copy-done.2, bf16[32,2432]{1,0:T(8,128)(2,1)S(1)} %collective-permute-done.3.z1, ...), custom_call_target="tpu_custom_call" | custom-call | tf_op jit(solution)/shard_map/spread/pallas_call | solution.py:384
  99.7 1.1 collective-permute-done.10
  100.8 1.1 collective-permute-start.13
  101.9 0.9 collective-permute-start.12
  102.8 1.5 collective-permute-start.11
  104.7 1.8 collective-permute-start.16
  106.5 0.7 collective-permute-start.18
  107.2 2.8 %collective-permute-start.17 = (bf16[64,2432]{1,0:T(8,128)(2,1)S(1)}, bf16[64,2432]{1,0:T(8,128)(2,1)S(1)}, u32[]{:S(2)}, u32[]{:S(2)}) collective-permute-start(bf16[64,2432]{1,0:T(8,128)(2,1)S(1)} %get-tuple-element.41), channel_id=1, source_target_pairs={{0,32},{16,48},{32,0},{48,16},{1,33},{17,49},{33,1},{49,17},{2,34}... | collective-permute-start | bytes 933896 | tf_op jit(solution)/shard_map/ppermute | solution.py:454
  110.1 4.7 %collective-permute-done.16 = bf16[64,2432]{1,0:T(8,128)(2,1)S(1)} collective-permute-done((bf16[64,2432]{1,0:T(8,128)(2,1)S(1)}, bf16[64,2432]{1,0:T(8,128)(2,1)S(1)}, u32[]{:S(2)}, u32[]{:S(2)}) %collective-permute-start.16) | collective-permute-done | bytes 311328 | tf_op jit(solution)/shard_map/ppermute | solution.py:454
  114.8 1.9 %collective-permute-done.18 = bf16[64,2432]{1,0:T(8,128)(2,1)S(1)} collective-permute-done((bf16[64,2432]{1,0:T(8,128)(2,1)S(1)}, bf16[64,2432]{1,0:T(8,128)(2,1)S(1)}, u32[]{:S(2)}, u32[]{:S(2)}) %collective-permute-start.18) | collective-permute-done | bytes 311328 | tf_op jit(solution)/shard_map/ppermute | solution.py:454
  116.7 5.1 %collective-permute-done.17 = bf16[64,2432]{1,0:T(8,128)(2,1)S(1)} collective-permute-done((bf16[64,2432]{1,0:T(8,128)(2,1)S(1)}, bf16[64,2432]{1,0:T(8,128)(2,1)S(1)}, u32[]{:S(2)}, u32[]{:S(2)}) %collective-permute-start.17) | collective-permute-done | bytes 311328 | tf_op jit(solution)/shard_map/ppermute | solution.py:454
  122.0 0.7 collective-permute-start.20
  122.8 2.6 %collective-permute-start.21 = (bf16[16,2944]{1,0:T(8,128)(2,1)S(1)}, bf16[16,2944]{1,0:T(8,128)(2,1)S(1)}, u32[]{:S(2)}, u32[]{:S(2)}) collective-permute-start(bf16[16,2944]{1,0:T(8,128)(2,1)S(1)} %get-tuple-element.50), channel_id=1, source_target_pairs={{0,6},{2,0},{4,2},{6,4},{1,7},{3,1},{5,3},{7,5},{8,14},{10,8},{12,... | collective-permute-start | bytes 282632 | tf_op jit(solution)/shard_map/ppermute | solution.py:454
  125.6 3.3 %collective-permute-done.20 = bf16[16,2944]{1,0:T(8,128)(2,1)S(1)} collective-permute-done((bf16[16,2944]{1,0:T(8,128)(2,1)S(1)}, bf16[16,2944]{1,0:T(8,128)(2,1)S(1)}, u32[]{:S(2)}, u32[]{:S(2)}) %collective-permute-start.20) | collective-permute-done | bytes 94240 | tf_op jit(solution)/shard_map/ppermute | solution.py:454
  129.0 2.5 %collective-permute-done.19 = bf16[16,2944]{1,0:T(8,128)(2,1)S(1)} collective-permute-done((bf16[16,2944]{1,0:T(8,128)(2,1)S(1)}, bf16[16,2944]{1,0:T(8,128)(2,1)S(1)}, u32[]{:S(2)}, u32[]{:S(2)}) %collective-permute-start.19) | collective-permute-done | bytes 94240 | tf_op jit(solution)/shard_map/ppermute | solution.py:454
  131.6 4.3 %collective-permute-start.22 = (bf16[8,3456]{1,0:T(8,128)(2,1)S(1)}, bf16[8,3456]{1,0:T(8,128)(2,1)S(1)}, u32[]{:S(2)}, u32[]{:S(2)}) collective-permute-start(bf16[8,3456]{1,0:T(8,128)(2,1)S(1)} %constant_dynamic-update-slice_fusion), channel_id=1, source_target_pairs={{0,8},{8,0},{1,9},{9,1},{2,10},{10,2},{3,11},{11,3},{4,12},{12,4},... | collective-permute-start | bytes 165896 | tf_op jit(solution)/shard_map/ppermute | solution.py:454
  136.0 10.3 %all-to-all-start.1 = ((bf16[256,16,128]{2,1,0:T(8,128)(2,1)}), bf16[256,16,128]{2,1,0:T(8,128)(2,1)S(1)}, u32[]{:S(2)}, u32[]{:S(2)}) async-start(bf16[256,16,128]{2,1,0:T(8,128)(2,1)} %bitcast.23), calls=%async_computation.1 | async-start | bytes 2097152 | tf_op jit(solution)/shard_map/all_to_all | solution.py:467
  146.4 4.0 %collective-permute-start.25 = (f32[16,256]{1,0:T(8,128)S(1)}, f32[16,256]{1,0:T(8,128)S(1)}, u32[]{:S(2)}, u32[]{:S(2)}) collective-permute-start(f32[16,256]{1,0:T(8,128)S(1)} %fusion.13), channel_id=1, source_target_pairs={{0,192},{64,0},{128,64},{192,128},{1,193},{65,1},{129,65},{193,129... | collective-permute-start | bytes 49160 | tf_op jit(solution)/shard_map/ppermute | solution.py:454
  150.3 0.9 collective-permute-start.23
  151.2 0.6 slice_bitcast_fusion
  151.8 0.7 fusion.16
  152.5 17.7 %collective-permute-done.25 = f32[16,256]{1,0:T(8,128)S(1)} collective-permute-done((f32[16,256]{1,0:T(8,128)S(1)}, f32[16,256]{1,0:T(8,128)S(1)}, u32[]{:S(2)}, u32[]{:S(2)}) %collective-permute-start.25) | collective-permute-done | bytes 16416 | tf_op jit(solution)/shard_map/ppermute | solution.py:454
  170.2 1.2 collective-permute-done.24
  171.6 0.6 reshape.79
  172.2 4.6 %all-to-all-done.1 = bf16[256,16,128]{2,1,0:T(8,128)(2,1)S(1)} async-done(((bf16[256,16,128]{2,1,0:T(8,128)(2,1)}), bf16[256,16,128]{2,1,0:T(8,128)(2,1)S(1)}, u32[]{:S(2)}, u32[]{:S(2)}) %all-to-all-start.1) | async-done | bytes 1048608 | tf_op jit(solution)/shard_map/all_to_all | solution.py:467
  176.8 6.4 %row_grad.1 = f32[1,64,256]{2,1,0:T(8,128)} custom-call(s32[1,4,8192]{2,1,0:T(4,128)} %index_ref.3, s32[1,8192]{1,0:T(1,128)} %length_ref.3, bf16[4,64,16,128]{3,2,1,0:T(8,128)(2,1)S(1)} %bitcast.47), custom_call_target="tpu_custom_call" | custom-call | tf_op jit(solution)/shard_map/row_grad/pallas_call | solution.py:432
  (81 shorter events, 2.8 us)
Async XLA Ops:
  0.6 21.5 %copy-start = (bf16[13,256]{1,0:T(8,128)(2,1)S(1)}, bf16[13,256]{1,0:T(8,128)(2,1)}, u32[]{:S(2)}) copy-start(bf16[13,256]{1,0:T(8,128)(2,1)} %param.14) | copy-start | bytes 19972
  7.0 14.7 %copy-start.9 = (s32[128]{0:T(128)S(1)}, s32[128]{0:T(128)}, u32[]{:S(2)}) copy-start(s32[128]{0:T(128)} %param.17) | copy-start | bytes 1540
  7.0 14.9 %copy-start.8 = (bf16[128,13]{0,1:T(8,128)(2,1)S(1)}, bf16[128,13]{0,1:T(8,128)(2,1)}, u32[]{:S(2)}) copy-start(bf16[128,13]{0,1:T(8,128)(2,1)} %param.13) | copy-start | bytes 9988
  7.0 45.0 %copy-start.3 = (s32[64]{0:T(128)S(1)}, s32[64]{0:T(128)}, u32[]{:S(2)}) copy-start(s32[64]{0:T(128)} %slot_ref.3) | copy-start | bytes 772
  7.0 59.5 %copy-start.1 = (bf16[2336,512]{1,0:T(8,128)(2,1)S(1)}, bf16[2336,512]{1,0:T(8,128)(2,1)}, u32[]{:S(2)}) copy-start(bf16[2336,512]{1,0:T(8,128)(2,1)} %weight_ref.1) | copy-start | bytes 7176196
  7.0 44.9 %all-to-all-start = ((bf16[256,16,128]{2,1,0:T(8,128)(2,1)}), bf16[256,16,128]{2,1,0:T(8,128)(2,1)S(1)}, u32[]{:S(2)}, u32[]{:S(2)}) async-start(bf16[256,16,128]{2,1,0:T(8,128)(2,1)} %bitcast.52), calls=%async_computation | async-start | bytes 2097152 | tf_op jit(solution)/shard_map/all_to_all | solution.py:467
  22.1 0.6 copy-start.5
  54.8 9.3 %collective-permute-start.2 = (bf16[32,2432]{1,0:T(8,128)(2,1)}, bf16[32,2432]{1,0:T(8,128)(2,1)S(1)}, u32[]{:S(2)}, u32[]{:S(2)}) collective-permute-start(bf16[32,2432]{1,0:T(8,128)(2,1)} %get-tuple-element.20.f0), channel_id=1, source_target_pairs={{0,128},{64,200},{128,8},{192,64},{8,136},{72,192},{136,0},{200,72... | collective-permute-start | bytes 466952 | tf_op jit(solution)/shard_map/ppermute | solution.py:462
  56.3 7.8 %collective-permute-start.1 = (bf16[32,2432]{1,0:T(8,128)(2,1)}, bf16[32,2432]{1,0:T(8,128)(2,1)S(1)}, u32[]{:S(2)}, u32[]{:S(2)}) collective-permute-start(bf16[32,2432]{1,0:T(8,128)(2,1)} %get-tuple-element.20.f0), channel_id=1, source_target_pairs={{0,200},{64,0},{128,64},{192,128},{8,192},{72,8},{136,72},{200,136... | collective-permute-start | bytes 466952 | tf_op jit(solution)/shard_map/ppermute | solution.py:462
  56.5 10.0 %collective-permute-start = (bf16[32,2432]{1,0:T(8,128)(2,1)}, bf16[32,2432]{1,0:T(8,128)(2,1)S(1)}, u32[]{:S(2)}, u32[]{:S(2)}) collective-permute-start(bf16[32,2432]{1,0:T(8,128)(2,1)} %get-tuple-element.20.f0), channel_id=1, source_target_pairs={{0,64},{64,128},{128,192},{192,8},{8,72},{72,136},{136,200},{200,0... | collective-permute-start | bytes 466952 | tf_op jit(solution)/shard_map/ppermute | solution.py:462
  66.4 20.6 %copy-start.6 = (bf16[2,1,16,13]{3,2,0,1:T(8,128)(2,1)S(1)}, bf16[2,1,16,13]{3,2,0,1:T(8,128)(2,1)}, u32[]{:S(2)}) copy-start(bf16[2,1,16,13]{3,2,0,1:T(8,128)(2,1)} %copy-done.5) | copy-start | bytes 2500
  69.5 7.5 %collective-permute-start.14 = (f32[8,128]{1,0:T(8,128)S(1)}, f32[8,128]{1,0:T(8,128)S(1)}, u32[]{:S(2)}, u32[]{:S(2)}) collective-permute-start(f32[8,128]{1,0:T(8,128)S(1)} %get-tuple-element.25.p0), channel_id=1, source_target_pairs={{0,72},{64,8},{128,200},{192,136},{8,64},{72,0},{136,192},{200,128... | collective-permute-start | bytes 12296 | tf_op jit(solution)/shard_map/ppermute | solution.py:462
  69.5 7.5 %collective-permute-start.9 = (f32[8,128]{1,0:T(8,128)S(1)}, f32[8,128]{1,0:T(8,128)S(1)}, u32[]{:S(2)}, u32[]{:S(2)}) collective-permute-start(f32[8,128]{1,0:T(8,128)S(1)} %get-tuple-element.25.p0), channel_id=1, source_target_pairs={{0,128},{64,192},{128,8},{192,72},{8,136},{72,200},{136,0},{200,64... | collective-permute-start | bytes 12296 | tf_op jit(solution)/shard_map/ppermute | solution.py:462
  72.4 4.5 %collective-permute-start.8 = (f32[8,128]{1,0:T(8,128)S(1)}, f32[8,128]{1,0:T(8,128)S(1)}, u32[]{:S(2)}, u32[]{:S(2)}) collective-permute-start(f32[8,128]{1,0:T(8,128)S(1)} %get-tuple-element.25.p0), channel_id=1, source_target_pairs={{0,136},{64,200},{128,0},{192,64},{8,128},{72,192},{136,8},{200,72... | collective-permute-start | bytes 12296 | tf_op jit(solution)/shard_map/ppermute | solution.py:462
  73.6 4.8 %collective-permute-start.7 = (f32[8,128]{1,0:T(8,128)S(1)}, f32[8,128]{1,0:T(8,128)S(1)}, u32[]{:S(2)}, u32[]{:S(2)}) collective-permute-start(f32[8,128]{1,0:T(8,128)S(1)} %get-tuple-element.25.p0), channel_id=1, source_target_pairs={{0,64},{64,128},{128,192},{192,8},{8,72},{72,136},{136,200},{200,0... | collective-permute-start | bytes 12296 | tf_op jit(solution)/shard_map/ppermute | solution.py:462
  75.8 3.6 %collective-permute-start.6 = (f32[8,128]{1,0:T(8,128)S(1)}, f32[8,128]{1,0:T(8,128)S(1)}, u32[]{:S(2)}, u32[]{:S(2)}) collective-permute-start(f32[8,128]{1,0:T(8,128)S(1)} %get-tuple-element.25.p0), channel_id=1, source_target_pairs={{0,200},{64,0},{128,64},{192,128},{8,192},{72,8},{136,72},{200,136... | collective-permute-start | bytes 12296 | tf_op jit(solution)/shard_map/ppermute | solution.py:462
  83.2 21.1 %collective-permute-start.15 = (bf16[16,16,2432]{2,1,0:T(8,128)(2,1)}, bf16[16,16,2432]{2,1,0:T(8,128)(2,1)S(1)}, u32[]{:S(2)}, u32[]{:S(2)}) collective-permute-start(bf16[16,16,2432]{2,1,0:T(8,128)(2,1)} %get-tuple-element.33), channel_id=1, source_target_pairs={{0,1},{1,0},{2,3},{3,2},{4,5},{5,4},{6,7},{7,6},{8,9},{9,8},{10,11... | collective-permute-start | bytes 3735560 | tf_op jit(solution)/shard_map/ppermute | solution.py:454
  83.2 9.8 %collective-permute-start.3 = (bf16[32,2432]{1,0:T(8,128)(2,1)S(1)}, bf16[32,2432]{1,0:T(8,128)(2,1)S(1)}, u32[]{:S(2)}, u32[]{:S(2)}) collective-permute-start(bf16[32,2432]{1,0:T(8,128)(2,1)S(1)} %get-tuple-element.22), channel_id=1, source_target_pairs={{0,200},{64,0},{128,64},{192,128},{8,192},{72,8},{136,72},{200,136... | collective-permute-start | bytes 466952 | tf_op jit(solution)/shard_map/ppermute | solution.py:462
  85.5 8.1 %collective-permute-start.4 = (bf16[32,2432]{1,0:T(8,128)(2,1)S(1)}, bf16[32,2432]{1,0:T(8,128)(2,1)S(1)}, u32[]{:S(2)}, u32[]{:S(2)}) collective-permute-start(bf16[32,2432]{1,0:T(8,128)(2,1)S(1)} %get-tuple-element.23), channel_id=1, source_target_pairs={{0,64},{64,128},{128,192},{192,8},{8,72},{72,136},{136,200},{200,0... | collective-permute-start | bytes 466952 | tf_op jit(solution)/shard_map/ppermute | solution.py:462
  85.5 8.1 %collective-permute-start.5 = (bf16[32,2432]{1,0:T(8,128)(2,1)S(1)}, bf16[32,2432]{1,0:T(8,128)(2,1)S(1)}, u32[]{:S(2)}, u32[]{:S(2)}) collective-permute-start(bf16[32,2432]{1,0:T(8,128)(2,1)S(1)} %get-tuple-element.24), channel_id=1, source_target_pairs={{0,136},{64,192},{128,0},{192,72},{8,128},{72,200},{136,8},{200,64... | collective-permute-start | bytes 466952 | tf_op jit(solution)/shard_map/ppermute | solution.py:462
  93.6 0.9 copy-start.2
  94.5 9.8 %copy-start.4 = (bf16[16,16,2432]{2,1,0:T(8,128)(2,1)S(1)}, bf16[16,16,2432]{2,1,0:T(8,128)(2,1)}, u32[]{:S(2)}) copy-start(bf16[16,16,2432]{2,1,0:T(8,128)(2,1)} %get-tuple-element.32) | copy-start | bytes 3735556
  99.6 1.2 collective-permute-start.10
  100.8 6.4 %collective-permute-start.13 = (f32[16,256]{1,0:T(8,128)S(1)}, f32[16,256]{1,0:T(8,128)S(1)}, u32[]{:S(2)}, u32[]{:S(2)}) collective-permute-start(f32[16,256]{1,0:T(8,128)S(1)} %add.185), channel_id=1, source_target_pairs={{0,48},{16,0},{32,16},{48,32},{1,49},{17,1},{33,17},{49,33},{2,50}... | collective-permute-start | bytes 49160 | tf_op jit(solution)/shard_map/ppermute | solution.py:454
  101.9 8.1 %collective-permute-start.12 = (f32[16,256]{1,0:T(8,128)S(1)}, f32[16,256]{1,0:T(8,128)S(1)}, u32[]{:S(2)}, u32[]{:S(2)}) collective-permute-start(f32[16,256]{1,0:T(8,128)S(1)} %add.185), channel_id=1, source_target_pairs={{0,16},{16,32},{32,48},{48,0},{1,17},{17,33},{33,49},{49,1},{2,18}... | collective-permute-start | bytes 49160 | tf_op jit(solution)/shard_map/ppermute | solution.py:454
  102.8 7.2 %collective-permute-start.11 = (f32[16,256]{1,0:T(8,128)S(1)}, f32[16,256]{1,0:T(8,128)S(1)}, u32[]{:S(2)}, u32[]{:S(2)}) collective-permute-start(f32[16,256]{1,0:T(8,128)S(1)} %add.185), channel_id=1, source_target_pairs={{0,32},{16,48},{32,0},{48,16},{1,33},{17,49},{33,1},{49,17},{2,34}... | collective-permute-start | bytes 49160 | tf_op jit(solution)/shard_map/ppermute | solution.py:454
  104.7 10.1 %collective-permute-start.16 = (bf16[64,2432]{1,0:T(8,128)(2,1)S(1)}, bf16[64,2432]{1,0:T(8,128)(2,1)S(1)}, u32[]{:S(2)}, u32[]{:S(2)}) collective-permute-start(bf16[64,2432]{1,0:T(8,128)(2,1)S(1)} %get-tuple-element.39), channel_id=1, source_target_pairs={{0,16},{16,32},{32,48},{48,0},{1,17},{17,33},{33,49},{49,1},{2,18}... | collective-permute-start | bytes 933896 | tf_op jit(solution)/shard_map/ppermute | solution.py:454
  106.5 10.2 %collective-permute-start.18 = (bf16[64,2432]{1,0:T(8,128)(2,1)S(1)}, bf16[64,2432]{1,0:T(8,128)(2,1)S(1)}, u32[]{:S(2)}, u32[]{:S(2)}) collective-permute-start(bf16[64,2432]{1,0:T(8,128)(2,1)S(1)} %get-tuple-element.40), channel_id=1, source_target_pairs={{0,48},{16,0},{32,16},{48,32},{1,49},{17,1},{33,17},{49,33},{2,50}... | collective-permute-start | bytes 933896 | tf_op jit(solution)/shard_map/ppermute | solution.py:454
  107.2 14.6 %collective-permute-start.17 = (bf16[64,2432]{1,0:T(8,128)(2,1)S(1)}, bf16[64,2432]{1,0:T(8,128)(2,1)S(1)}, u32[]{:S(2)}, u32[]{:S(2)}) collective-permute-start(bf16[64,2432]{1,0:T(8,128)(2,1)S(1)} %get-tuple-element.41), channel_id=1, source_target_pairs={{0,32},{16,48},{32,0},{48,16},{1,33},{17,49},{33,1},{49,17},{2,34}... | collective-permute-start | bytes 933896 | tf_op jit(solution)/shard_map/ppermute | solution.py:454
  122.0 6.9 %collective-permute-start.20 = (bf16[16,2944]{1,0:T(8,128)(2,1)S(1)}, bf16[16,2944]{1,0:T(8,128)(2,1)S(1)}, u32[]{:S(2)}, u32[]{:S(2)}) collective-permute-start(bf16[16,2944]{1,0:T(8,128)(2,1)S(1)} %get-tuple-element.49), channel_id=1, source_target_pairs={{0,2},{2,4},{4,6},{6,0},{1,3},{3,5},{5,7},{7,1},{8,10},{10,12},{12... | collective-permute-start | bytes 282632 | tf_op jit(solution)/shard_map/ppermute | solution.py:454
  122.8 6.2 %collective-permute-start.21 = (bf16[16,2944]{1,0:T(8,128)(2,1)S(1)}, bf16[16,2944]{1,0:T(8,128)(2,1)S(1)}, u32[]{:S(2)}, u32[]{:S(2)}) collective-permute-start(bf16[16,2944]{1,0:T(8,128)(2,1)S(1)} %get-tuple-element.50), channel_id=1, source_target_pairs={{0,6},{2,0},{4,2},{6,4},{1,7},{3,1},{5,3},{7,5},{8,14},{10,8},{12,... | collective-permute-start | bytes 282632 | tf_op jit(solution)/shard_map/ppermute | solution.py:454
  125.4 6.1 %collective-permute-start.19 = (bf16[16,2944]{1,0:T(8,128)(2,1)S(1)}, bf16[16,2944]{1,0:T(8,128)(2,1)S(1)}, u32[]{:S(2)}, u32[]{:S(2)}) collective-permute-start(bf16[16,2944]{1,0:T(8,128)(2,1)S(1)} %get-tuple-element.51), channel_id=1, source_target_pairs={{0,4},{2,6},{4,0},{6,2},{1,5},{3,7},{5,1},{7,3},{8,12},{10,14},{12... | collective-permute-start | bytes 282632 | tf_op jit(solution)/shard_map/ppermute | solution.py:454
  131.6 14.6 %collective-permute-start.22 = (bf16[8,3456]{1,0:T(8,128)(2,1)S(1)}, bf16[8,3456]{1,0:T(8,128)(2,1)S(1)}, u32[]{:S(2)}, u32[]{:S(2)}) collective-permute-start(bf16[8,3456]{1,0:T(8,128)(2,1)S(1)} %constant_dynamic-update-slice_fusion), channel_id=1, source_target_pairs={{0,8},{8,0},{1,9},{9,1},{2,10},{10,2},{3,11},{11,3},{4,12},{12,4},... | collective-permute-start | bytes 165896 | tf_op jit(solution)/shard_map/ppermute | solution.py:454
  136.0 40.9 %all-to-all-start.1 = ((bf16[256,16,128]{2,1,0:T(8,128)(2,1)}), bf16[256,16,128]{2,1,0:T(8,128)(2,1)S(1)}, u32[]{:S(2)}, u32[]{:S(2)}) async-start(bf16[256,16,128]{2,1,0:T(8,128)(2,1)} %bitcast.23), calls=%async_computation.1 | async-start | bytes 2097152 | tf_op jit(solution)/shard_map/all_to_all | solution.py:467
  146.4 23.9 %collective-permute-start.25 = (f32[16,256]{1,0:T(8,128)S(1)}, f32[16,256]{1,0:T(8,128)S(1)}, u32[]{:S(2)}, u32[]{:S(2)}) collective-permute-start(f32[16,256]{1,0:T(8,128)S(1)} %fusion.13), channel_id=1, source_target_pairs={{0,192},{64,0},{128,64},{192,128},{1,193},{65,1},{129,65},{193,129... | collective-permute-start | bytes 49160 | tf_op jit(solution)/shard_map/ppermute | solution.py:454
  150.3 21.1 %collective-permute-start.24 = (f32[16,256]{1,0:T(8,128)S(1)}, f32[16,256]{1,0:T(8,128)S(1)}, u32[]{:S(2)}, u32[]{:S(2)}) collective-permute-start(f32[16,256]{1,0:T(8,128)S(1)} %fusion.13), channel_id=1, source_target_pairs={{0,64},{64,128},{128,192},{192,0},{1,65},{65,129},{129,193},{193,1... | collective-permute-start | bytes 49160 | tf_op jit(solution)/shard_map/ppermute | solution.py:454
  150.3 21.1 %collective-permute-start.23 = (f32[16,256]{1,0:T(8,128)S(1)}, f32[16,256]{1,0:T(8,128)S(1)}, u32[]{:S(2)}, u32[]{:S(2)}) collective-permute-start(f32[16,256]{1,0:T(8,128)S(1)} %fusion.13), channel_id=1, source_target_pairs={{0,128},{64,192},{128,0},{192,64},{1,129},{65,193},{129,1},{193,65... | collective-permute-start | bytes 49160 | tf_op jit(solution)/shard_map/ppermute | solution.py:454
  171.5 11.8 %copy-start.7 = (f32[16,256]{1,0:T(8,128)}, f32[16,256]{1,0:T(8,128)S(1)}, u32[]{:S(2)}) copy-start(f32[16,256]{1,0:T(8,128)S(1)} %add_add_fusion) | copy-start | bytes 49156

commit v5 on v4

--- a/solution.py
+++ b/solution.py
@@ -20,6 +20,7 @@
 FEAT = 2336
 WIDE = 2432
 STEP = 8
+GRAD_STEP = 16
 LABEL_LANE = 36
 
 
@@ -137,15 +138,15 @@
     lax.fori_loop(0, TAB, place, 0, unroll=8)
     bottom = packed_bottom(mine_ref)
     low = jnp.concatenate([low_lanes(TAB)] * 4, axis=1)
+    first = jnp.where(low, 1.0, 0.0).astype(BF16)
+    second = jnp.where(low, 0.0, 1.0).astype(BF16)
     for row in range(ROWS):
         vectors = jnp.concatenate(
             [spaced[part, pl.ds(row, TAB, stride=ROWS), :] for part in range(4)], axis=1
         )
         narrow = vectors.astype(BF16)
         vectors_ref[row] = narrow
-        right = jnp.concatenate(
-            [jnp.where(low, vectors, 0.0), jnp.where(low, 0.0, vectors)], axis=0
-        ).astype(BF16)
+        right = jnp.concatenate([narrow * first, narrow * second], axis=0)
         extra = jnp.broadcast_to(bottom[row : row + 1], (ROWS, 512)).astype(BF16)
         product = dot_t(jnp.concatenate([narrow, extra], axis=0), right)
         gram[pl.ds(row, TAB, stride=ROWS), :] = product[0:TAB]
@@ -205,7 +206,9 @@
     delta = (out_weight * slope).astype(BF16)
     hidden_ref[...] = hidden
     delta_ref[...] = delta
-    partial_ref[...] = dot_t(jnp.broadcast_to(out_weight, (16, 512)).astype(BF16), hidden)[0:8]
+    partial = dot_t(jnp.broadcast_to(out_weight, (16, 512)).astype(BF16), hidden)[0:8]
+    for place in range(8):
+        partial_ref[place] = partial
     z = dot_t(delta, weight).astype(BF16)
     for part, ref in enumerate((z0, z1, z2, z3)):
         ref[:, 0:FEAT] = z[part * 32 : (part + 1) * 32]
@@ -220,7 +223,7 @@
         out_shape=[hbm((128, WIDE), BF16), hbm((32, WIDE), BF16)]
         + [jax.ShapeDtypeStruct((32, WIDE), BF16)] * 3
         + [
-            jax.ShapeDtypeStruct((8, LANES), F32),
+            jax.ShapeDtypeStruct((8, 8, LANES), F32),
             hbm((128, 512), BF16),
             hbm((128, 512), BF16),
         ],
@@ -234,10 +237,10 @@
 
 
 def weight_grad_kernel(
-    place_ref, p0, p1, p2, p3, p4, p5, all_ref, delta_ref, hidden_ref, own_ref, other_ref, grad,
+    place_ref, partial_ref, all_ref, delta_ref, hidden_ref, own_ref, other_ref, grad,
 ):
     even = place_ref[1] == 0
-    r0, up1, down1, up2, down2, far = (p[...] for p in (p0, p1, p2, p3, p4, p5))
+    r0, up1, down1, up2, down2, far = (partial_ref[place_ref[2 + i]] for i in range(6))
 
     def at(x, slot, to):
         return turned(x, 32 * (to - slot))
@@ -283,7 +286,7 @@
 def weight_grad(place, partials, features, delta, hidden):
     return pl.pallas_call(
         weight_grad_kernel,
-        in_specs=[pl.BlockSpec(memory_space=pltpu.SMEM)] + vmem_specs(9),
+        in_specs=[pl.BlockSpec(memory_space=pltpu.SMEM)] + vmem_specs(4),
         out_specs=vmem_specs(2),
         out_shape=[
             hbm((16, 16, WIDE), BF16),
@@ -292,14 +295,14 @@
         scratch_shapes=[pltpu.VMEM((512, WIDE), F32)],
         compiler_params=pltpu.CompilerParams(vmem_limit_bytes=32 << 20),
         name="weight_grad",
-    )(place, *partials, *in_hbm(features, delta, hidden))
+    )(place, partials, *in_hbm(features, delta, hidden))
 
 
 def spread_kernel(
-    slot_ref, place_ref, z0, z1, z2, z3, p0, p1, p2, p3, p4, label_ref, vectors_ref, mine_ref,
-    slope_ref, dense_ref, back_ref, bottom_ref, logit_ref, dfeat, upper, edge, right, dvec, dedge,
+    slot_ref, place_ref, z0, z1, z2, z3, partial_ref, label_ref, vectors_ref, mine_ref,
+    slope_ref, dense_ref, back_ref, bottom_ref, logit_ref, dfeat, upper, edge, rights, dvec, dedge,
 ):
-    logits = own_logits(place_ref[1] == 0, p0[...], p1[...], p2[...], p3[...], p4[...])
+    logits = own_logits(place_ref[1] == 0, *(partial_ref[place_ref[2 + i]] for i in range(5)))
     logit_ref[...] = logits
     labels = jnp.sum(jnp.where(lane_iota(32) == LABEL_LANE, label_ref[...], 0.0), axis=1, keepdims=True)
     column = (jax.nn.sigmoid(logits.T[0:32, 0:1]) - labels) * (1.0 / 128.0)
@@ -321,10 +324,12 @@
         else:
             upper[row * ROWS : (row + 1) * ROWS, :] = filled
     upper[(TAB - 1) * ROWS :, :] = jnp.zeros((ROWS, LANES), F32)
-    right[...] = jnp.zeros_like(right)
+    rights[...] = jnp.zeros_like(rights)
     bottom = packed_bottom(mine_ref)
     low = low_lanes(TAB)
     low_wide = jnp.concatenate([low] * 4, axis=1)
+    low_factor = jnp.where(low_wide, 1.0, 0.0).astype(BF16)
+    high_factor = jnp.where(low_wide, 0.0, 1.0).astype(BF16)
     low_few = jnp.concatenate([low_lanes(16)] * 4, axis=1)
     top_row = lax.broadcasted_iota(jnp.int32, (16, 512), 0) == 0
     for row in range(ROWS):
@@ -341,9 +346,9 @@
             ],
             axis=0,
         ).astype(BF16)
-        vectors = vectors_ref[row].astype(F32)
-        right[0:TAB, :] = jnp.where(low_wide, vectors, 0.0).astype(BF16)
-        right[TAB : 2 * TAB, :] = jnp.where(low_wide, 0.0, vectors).astype(BF16)
+        right = rights.at[row % 2]
+        right[0:TAB, :] = vectors_ref[row] * low_factor
+        right[TAB : 2 * TAB, :] = vectors_ref[row] * high_factor
         own = jnp.broadcast_to(bottom[row : row + 1], (16, 512))
         right[128:144, :] = jnp.where(top_row & ~low_few, own, 0.0).astype(BF16)
         right[192:208, :] = jnp.where(top_row & low_few, own, 0.0).astype(BF16)
@@ -383,7 +388,7 @@
 def spread(table_slot, place, zs, partials, labels, vectors, mine, slope, dense):
     return pl.pallas_call(
         spread_kernel,
-        in_specs=[pl.BlockSpec(memory_space=pltpu.SMEM)] * 2 + vmem_specs(14),
+        in_specs=[pl.BlockSpec(memory_space=pltpu.SMEM)] * 2 + vmem_specs(10),
         out_specs=vmem_specs(3),
         out_shape=[
             hbm((4, TAB, ROWS, LANES), BF16),
@@ -394,33 +399,79 @@
             pltpu.VMEM((2 * ROWS, WIDE), F32),
             pltpu.VMEM((TAB * ROWS, LANES), F32),
             pltpu.VMEM((ROWS, LANES), F32),
-            pltpu.VMEM((256, 512), BF16),
+            pltpu.VMEM((2, 256, 512), BF16),
             pltpu.VMEM((4, TAB * ROWS, LANES), F32),
             pltpu.VMEM((ROWS, 512), F32),
         ],
         compiler_params=pltpu.CompilerParams(vmem_limit_bytes=16 << 20),
         name="spread",
-    )(table_slot, place, *zs, *partials, labels, *in_hbm(vectors), mine, slope, dense)
-
-
-def row_grad_kernel(index_ref, length_ref, back_ref, out_ref, total, counted, moved):
+    )(table_slot, place, *zs, partials, labels, *in_hbm(vectors), mine, slope, dense)
+
+
+def pack_kernel(place_ref, own_ref, other_ref, bottom_ref, keep_ref, s1, s2, s3, bottom_own_ref):
+    high = bottom_ref[...].astype(BF16)
+    low = (bottom_ref[...] - high.astype(F32)).astype(BF16)
+    bottom_own_ref[...] = high.astype(F32) + low.astype(F32)
+    tile = jnp.concatenate([v[:, p : p + LANES] for v in (high, low) for p in (0, LANES)], axis=0)
+    for away, ref in enumerate((keep_ref, s1, s2, s3)):
+        first = ((place_ref[8] + away) & 3) * 4
+        for y in range(4):
+            rows = slice(y * 16, (y + 1) * 16)
+            total = own_ref[first + y].astype(F32) + other_ref[first + y].astype(F32)
+            ref[rows, 0:WIDE] = total.astype(ref.dtype)
+        if away:
+            ref[:, WIDE:] = tile
+
+
+def pack(place, own, other, bottom):
+    return pl.pallas_call(
+        pack_kernel,
+        in_specs=[pl.BlockSpec(memory_space=pltpu.SMEM)] + vmem_specs(3),
+        out_specs=vmem_specs(5),
+        out_shape=[hbm((64, WIDE), F32)]
+        + [jax.ShapeDtypeStruct((64, WIDE + LANES), BF16)] * 3
+        + [jax.ShapeDtypeStruct((16, EMB), F32)],
+        compiler_params=pltpu.CompilerParams(vmem_limit_bytes=16 << 20),
+        name="pack",
+    )(place, *in_hbm(own), other, bottom)
+
+
+def count_kernel(index_ref, length_ref, out_ref):
+    values = row_values()
+    for group in range(STEP):
+        out_ref[:, group * LANES : (group + 1) * LANES] = counts_of(index_ref, length_ref, group, values)
+
+
+def count(pool_index, bag_length):
+    return pl.pallas_call(
+        count_kernel,
+        grid=(TAB // STEP,),
+        in_specs=[
+            pl.BlockSpec((1, 4, STEP * LANES), lambda i: (0, 0, i)),
+            pl.BlockSpec((1, STEP * LANES), lambda i: (0, i)),
+        ],
+        out_specs=pl.BlockSpec((256, STEP * LANES), lambda i: (0, i)),
+        out_shape=hbm((256, TAB * LANES), BF16),
+        compiler_params=pltpu.CompilerParams(vmem_limit_bytes=12 << 20),
+        name="count",
+    )(*in_hbm(pool_index, bag_length))
+
+
+def row_grad_kernel(count_ref, back_ref, out_ref, total, moved):
     step = pl.program_id(0)
 
     @pl.when(step == 0)
     def _():
         total[...] = jnp.zeros_like(total)
 
-    values = row_values()
     low = low_lanes(HALF)
     first = jnp.where(low, 1.0, 0.0).astype(BF16)
     second = jnp.where(low, 0.0, 1.0).astype(BF16)
-    for group in range(STEP):
-        lanes = slice(group * LANES, (group + 1) * LANES)
-        counted[:, lanes] = counts_of(index_ref, length_ref, group, values)
+    for group in range(GRAD_STEP):
         rows = jnp.concatenate([back_ref[peer, group] for peer in range(4)], axis=0)
         moved[group * LANES : group * LANES + HALF, :] = rows * first
         moved[group * LANES + HALF : (group + 1) * LANES, :] = rows * second
-    total[...] += jnp.dot(counted[...], moved[...], preferred_element_type=F32)
+    total[...] += jnp.dot(count_ref[...], moved[...], preferred_element_type=F32)
 
     @pl.when(step == pl.num_programs(0) - 1)
     def _():
@@ -428,25 +479,23 @@
         out_ref[0] = flipped[0:HALF] + flipped[HALF:LANES]
 
 
-def row_grad(pool_index, bag_length, back):
+def row_grad(counts, back):
     return pl.pallas_call(
         row_grad_kernel,
-        grid=(TAB // STEP,),
+        grid=(TAB // GRAD_STEP,),
         in_specs=[
-            pl.BlockSpec((1, 4, STEP * LANES), lambda i: (0, 0, i)),
-            pl.BlockSpec((1, STEP * LANES), lambda i: (0, i)),
-            pl.BlockSpec((4, STEP, ROWS, LANES), lambda i: (0, i, 0, 0)),
+            pl.BlockSpec((256, GRAD_STEP * LANES), lambda i: (0, i)),
+            pl.BlockSpec((4, GRAD_STEP, ROWS, LANES), lambda i: (0, i, 0, 0)),
         ],
         out_specs=pl.BlockSpec((1, HALF, 256), lambda i: (0, 0, 0)),
         out_shape=jax.ShapeDtypeStruct((1, HALF, 256), F32),
         scratch_shapes=[
             pltpu.VMEM((256, LANES), F32),
-            pltpu.VMEM((256, STEP * LANES), BF16),
-            pltpu.VMEM((STEP * LANES, LANES), BF16),
-        ],
-        compiler_params=pltpu.CompilerParams(vmem_limit_bytes=12 << 20),
+            pltpu.VMEM((GRAD_STEP * LANES, LANES), BF16),
+        ],
+        compiler_params=pltpu.CompilerParams(vmem_limit_bytes=16 << 20),
         name="row_grad",
-    )(*in_hbm(pool_index, bag_length), back)
+    )(*in_hbm(counts), back)
 
 
 def shifted(x, axis, shift):
@@ -538,9 +587,13 @@
     dense_wide = jnp.pad(dense_mine.astype(F32), ((0, 0), (0, 16 - dense_mine.shape[1])))
     labels_mine = lax.dynamic_index_in_dim(labels.reshape(2, 4, ROWS), me, 1, keepdims=False)
     labels_mine = jnp.broadcast_to(labels_mine.astype(F32).reshape(2 * ROWS, 1), (2 * ROWS, LANES))
-    place = jnp.stack([core, me % 2]).astype(jnp.int32)
+    spot = lax.axis_index("grp_1") * 4 + me
+    near = [spot, spot + 1, spot - 1, spot + 2, spot - 2, jnp.where(me % 2 == 0, spot - 3, spot + 3)]
+    near = [p % 4 * 2 + p % 8 // 4 for p in near]
+    place = jnp.stack([core, me % 2, *near, lax.axis_index("grp_0")]).astype(jnp.int32)
     out_weight_row = out_weight.astype(F32).reshape(1, -1)
 
+    counts = count(pool_index, bag_length)
     part, vectors = interact(table_slot, arrived, mine, labels_mine)
     parts = [
         part,
@@ -555,26 +608,24 @@
         ring_sent(zs[2], lambda p: 1),
         ring_sent(zs[3], lambda p: 2 if p % 2 else -2),
     ]
-    partials = [
-        partial,
-        ring_sent(partial, lambda p: -1),
-        ring_sent(partial, lambda p: 1),
-        ring_sent(partial, lambda p: -2),
-        ring_sent(partial, lambda p: 2),
-        ring_sent(partial, lambda p: 3 if p % 2 else -3),
-    ]
+    partials = lax.all_to_all(partial, ("col", "grp_1"), split_axis=0, concat_axis=0, tiled=True)
     own, other = weight_grad(place, partials, features, delta, hidden)
     back, bottom, logits_mine = spread(
-        table_slot, place, zs, partials[:5], labels_mine, vectors, mine, mine_slope, dense_wide
+        table_slot, place, zs, partials, labels_mine, vectors, mine, mine_slope, dense_wide
     )
     returned = exchange_all(back)
-    grad_rows = jnp.transpose(row_grad(pool_index, bag_length, returned), (0, 2, 1))
+    grad_rows = jnp.transpose(row_grad(counts, returned), (0, 2, 1))
 
     other = shifted(other, "grp_3", 1)
-    grad = (own.astype(F32) + other.astype(F32)).astype(BF16).reshape(4, 64, WIDE)
-    grad = reduced_to(grad, "grp_0").reshape(4, 16, WIDE)
-    for axis in ("grp_3", "grp_0"):
-        bottom = summed_over(bottom, axis)
+    grad, *blocks, bottom = pack(place, own, other, bottom)
+    sums = []
+    for away in (1, 2, 3):
+        block = shifted(blocks[away - 1], "grp_0", away).astype(F32)
+        grad = grad + block[:, 0:WIDE]
+        tile = block[0:32, WIDE:] + block[32:64, WIDE:]
+        sums.append(jnp.concatenate([tile[0:16], tile[16:32]], axis=1))
+    grad = grad.reshape(4, 16, WIDE)
+    bottom = summed_over((bottom + sums[1]) + (sums[0] + sums[2]), "grp_3")
     grad, bottom = reduced_to(grad, "grp_2", bottom)
     grad, bottom = reduced_to(grad.reshape(2, 8, WIDE), "grp_1", bottom)
     grad_top = jnp.transpose(grad[:, 0:FEAT])

time: 186 us -> 182 us (0.978)
  starting transfers between devices: 61.2 us -> 50.9 us
  Pallas kernels: 27.6 us -> 33.2 us
  waiting for transfers between devices: 87.7 us -> 90.5 us
    ppermute x11 -> x6, starting transfers between devices: 14.7 us -> 6.44 us  [ring_sent(): return lax.ppermute(x, ('col', 'grp_1'), pairs)]
    ppermute x15 -> x12, starting transfers between devices: 21.5 us -> 13.6 us  [shifted(): return lax.ppermute(x, axis, [(i, (i + shift) % size) for i in range(size)])]
    all_to_all x0 -> x1, waiting for transfers between devices: none -> 7.2 us  [step(): lax.all_to_all(partial, ('col', 'grp_1'), split_axis=0, concat_axis=0, ti...]
    pallas_call x1 -> x3, Pallas kernels: 6.44 us -> 13 us  [the longest x1 5.96 us: count(): pl.pallas_call(count_kernel, grid=(TAB // STEP,), in_specs=[pl.BlockSpec(...]
    all_to_all x0 -> x1, starting transfers between devices: none -> 3.47 us  [step(): lax.all_to_all(partial, ('col', 'grp_1'), split_axis=0, concat_axis=0, ti...]
    ppermute x15 -> x12, waiting for transfers between devices: 37.5 us -> 34.1 us  [shifted(): return lax.ppermute(x, axis, [(i, (i + shift) % size) for i in range(size)])]
    all_to_all x2, starting transfers between devices: 24.9 us -> 27.4 us  [exchange_all(): lax.all_to_all(flat, COL_GRP, split_axis=0, concat_axis=0, tiled=True)]
    ppermute x11 -> x6, waiting for transfers between devices: 16.4 us -> 15 us  [ring_sent(): return lax.ppermute(x, ('col', 'grp_1'), pairs)]
  transfers between devices with their start and end apart: 28 -> 21, of which waited for: 17 -> 18; matrix products, arithmetic and copies ran while one was open for 2% -> 2% of each run, Pallas kernels for 3% -> 6%
where the time goes in v5:
time: 182 us; the launch traced here: 179 us
  waiting for transfers between devices  90.5 us (50%)
  starting transfers between devices  50.9 us (28%)
  Pallas kernels  33.2 us (18%)
  local copies, waits for them, and re-layouts  2.11 us (1%)
    all_to_all x2, waiting for transfers between devices, exchange_all(): lax.all_to_all(flat, COL_GRP, split_axis=0, concat_axis=0, tiled=True)  34.2 us
    ppermute x12, waiting for transfers between devices, shifted(): return lax.ppermute(x, axis, [(i, (i + shift) % size) for i in range(size)])  34.1 us
    all_to_all x2, starting transfers between devices, exchange_all(): lax.all_to_all(flat, COL_GRP, split_axis=0, concat_axis=0, tiled=True)  27.4 us
    ppermute x6, waiting for transfers between devices, ring_sent(): return lax.ppermute(x, ('col', 'grp_1'), pairs)  15 us
    ppermute x12, starting transfers between devices, shifted(): return lax.ppermute(x, axis, [(i, (i + shift) % size) for i in range(size)])  13.6 us
    all_to_all x1, waiting for transfers between devices, step(): lax.all_to_all(partial, ('col', 'grp_1'), split_axis=0, concat_axis=0, ti...  7.2 us
    ppermute x6, starting transfers between devices, ring_sent(): return lax.ppermute(x, ('col', 'grp_1'), pairs)  6.44 us
    pallas_call x1, Pallas kernels, pool(): pl.pallas_call(pool_kernel, grid=(TAB // STEP,), in_specs=[pl.BlockSpec((...  6.37 us
  transfers between devices with their start and end apart: 21, of which 18 were waited for; matrix products, arithmetic and copies ran while one was open for 2% of the time, Pallas kernels for 6%

profile of v5, /device:TPU:4, one launch (start us, length us, event | category | flops | bytes accessed | tf_op | source)
XLA Modules:
  0.0 179.4 jit_solution(5788312847504184419)
XLA Ops:
  0.6 6.4 %pool.1 = bf16[4,64,16,128]{3,2,1,0:T(8,128)(2,1)} custom-call(s32[1,4,8192]{2,1,0:T(4,128)} %index_ref.3, s32[1,8192]{1,0:T(1,128)} %length_ref.3, bf16[1,64,256]{2,1,0:T(8,128)(2,1)} %bitcast.51), custom_call_target="tpu_custom_call" | custom-call | tf_op jit(solution)/shard_map/pool/pallas_call | solution.py:105
  7.1 14.7 %all-to-all-start = ((bf16[256,16,128]{2,1,0:T(8,128)(2,1)}), bf16[256,16,128]{2,1,0:T(8,128)(2,1)S(1)}, u32[]{:S(2)}, u32[]{:S(2)}) async-start(bf16[256,16,128]{2,1,0:T(8,128)(2,1)} %bitcast.47), calls=%async_computation | async-start | bytes 2097152 | tf_op jit(solution)/shard_map/all_to_all | solution.py:516
  22.1 0.1 copy.18
  22.2 0.1 add_multiply_fusion
  22.3 29.6 %all-to-all-done = bf16[256,16,128]{2,1,0:T(8,128)(2,1)S(1)} async-done(((bf16[256,16,128]{2,1,0:T(8,128)(2,1)}), bf16[256,16,128]{2,1,0:T(8,128)(2,1)S(1)}, u32[]{:S(2)}, u32[]{:S(2)}) %all-to-all-start) | async-done | bytes 1048608 | tf_op jit(solution)/shard_map/all_to_all | solution.py:516
  52.0 2.9 %interact.1 = (bf16[32,2432]{1,0:T(8,128)(2,1)S(1)}, bf16[16,64,512]{2,1,0:T(8,128)(2,1)}) custom-call(s32[64]{0:T(128)S(1)} %copy-done.3, bf16[4,64,16,128]{3,2,1,0:T(8,128)(2,1)S(1)} %bitcast.44, f32[32,256]{1,0:T(8,128)S(1)} %get-tuple-element.55.mine_ref, f32[32,128]{1,0:T(8,128)S(1)} %broadcast_in_dim.17.label_ref), custom_call_target="tpu_custom_call" | custom-call | tf_op jit(solution)/shard_map/interact/pallas_call | solution.py:173
  54.8 1.5 collective-permute-start.2
  56.4 0.1 collective-permute-start.1
  56.5 1.9 %collective-permute-start = (bf16[32,2432]{1,0:T(8,128)(2,1)S(1)}, bf16[32,2432]{1,0:T(8,128)(2,1)S(1)}, u32[]{:S(2)}, u32[]{:S(2)}) collective-permute-start(bf16[32,2432]{1,0:T(8,128)(2,1)S(1)} %get-tuple-element.25.f0), channel_id=1, source_target_pairs={{0,64},{64,128},{128,192},{192,8},{8,72},{72,136},{136,200},{200,0... | collective-permute-start | bytes 466952 | tf_op jit(solution)/shard_map/ppermute | solution.py:511
  58.4 5.5 %collective-permute-done.2.f3 = bf16[32,2432]{1,0:T(8,128)(2,1)S(1)} collective-permute-done((bf16[32,2432]{1,0:T(8,128)(2,1)S(1)}, bf16[32,2432]{1,0:T(8,128)(2,1)S(1)}, u32[]{:S(2)}, u32[]{:S(2)}) %collective-permute-start.2) | collective-permute-done | bytes 155680 | tf_op jit(solution)/shard_map/ppermute | solution.py:511
  64.0 2.3 %collective-permute-done.f1 = bf16[32,2432]{1,0:T(8,128)(2,1)S(1)} collective-permute-done((bf16[32,2432]{1,0:T(8,128)(2,1)S(1)}, bf16[32,2432]{1,0:T(8,128)(2,1)S(1)}, u32[]{:S(2)}, u32[]{:S(2)}) %collective-permute-start) | collective-permute-done | bytes 155680 | tf_op jit(solution)/shard_map/ppermute | solution.py:511
  66.2 2.0 %top.1 = (bf16[128,2432]{1,0:T(8,128)(2,1)}, bf16[32,2432]{1,0:T(8,128)(2,1)}, bf16[32,2432]{1,0:T(8,128)(2,1)S(1)}, bf16[32,2432]{1,0:T(8,128)(2,1)S(1)}, bf16[...) custom-call(bf16[32,2432]{1,0:T(8,128)(2,1)S(1)} %get-tuple-element.25.f0, ...), custom_call_target="tpu_custom_call" | custom-call | tf_op jit(solution)/shard_map/top/pallas_call | solution.py:219
  68.3 3.5 %all-to-all-start.1 = ((f32[8,8,128]{2,1,0:T(8,128)}), f32[8,8,128]{2,1,0:T(8,128)S(1)}, u32[]{:S(2)}, u32[]{:S(2)}) async-start(f32[8,8,128]{2,1,0:T(8,128)} %get-tuple-element.30), calls=%async_computation.1 | async-start | bytes 65536 | tf_op jit(solution)/shard_map/all_to_all | solution.py:611
  72.2 7.2 %all-to-all-done.1.partial_ref = f32[8,8,128]{2,1,0:T(8,128)S(1)} async-done(((f32[8,8,128]{2,1,0:T(8,128)}), f32[8,8,128]{2,1,0:T(8,128)S(1)}, u32[]{:S(2)}, u32[]{:S(2)}) %all-to-all-start.1) | async-done | bytes 32800 | tf_op jit(solution)/shard_map/all_to_all | solution.py:611
  79.4 3.9 %weight_grad.1 = (bf16[16,16,2432]{2,1,0:T(8,128)(2,1)}, bf16[16,16,2432]{2,1,0:T(8,128)(2,1)}) custom-call(s32[9]{0:T(128)S(1)} %stack.39.place_ref, f32[8,8,128]{2,1,0:T(8,128)S(1)} %all-to-all-done.1.partial_ref, bf16[128,2432]{1,0:T(8,128)(2,1)} %get-tuple-element.33.all_ref, bf16[128,512]{1,0:T(8,128)(2,1)} %get-tuple-element.34.delta_ref, ...), custom_call_target="tpu_custom_call" | custom-call | tf_op jit(solution)/shard_map/weight_grad/pallas_call | solution.py:287
  83.3 0.7 collective-permute-start.3
  84.0 1.3 collective-permute-start.4
  85.3 0.9 collective-permute-start.5
  86.2 3.7 %collective-permute-done.3.z1 = bf16[32,2432]{1,0:T(8,128)(2,1)S(1)} collective-permute-done((bf16[32,2432]{1,0:T(8,128)(2,1)S(1)}, bf16[32,2432]{1,0:T(8,128)(2,1)S(1)}, u32[]{:S(2)}, u32[]{:S(2)}) %collective-permute-start.3) | collective-permute-done | bytes 155680 | tf_op jit(solution)/shard_map/ppermute | solution.py:511
  89.9 2.2 %collective-permute-done.4.z2 = bf16[32,2432]{1,0:T(8,128)(2,1)S(1)} collective-permute-done((bf16[32,2432]{1,0:T(8,128)(2,1)S(1)}, bf16[32,2432]{1,0:T(8,128)(2,1)S(1)}, u32[]{:S(2)}, u32[]{:S(2)}) %collective-permute-start.4) | collective-permute-done | bytes 155680 | tf_op jit(solution)/shard_map/ppermute | solution.py:511
  92.1 1.2 collective-permute-done.5.z3
  93.3 5.0 %spread.1 = (bf16[4,64,16,128]{3,2,1,0:T(8,128)(2,1)}, f32[16,256]{1,0:T(8,128)S(1)}, f32[8,128]{1,0:T(8,128)S(1)}) custom-call(s32[64]{0:T(128)S(1)} %copy-done.3, s32[9]{0:T(128)S(1)} %stack.39.place_ref, bf16[32,2432]{1,0:T(8,128)(2,1)S(1)} %copy-done.2, bf16[32,2432]{1,0:T(8,128)(2,1)S(1)} %collective-permute-done.3.z1, ...), custom_call_target="tpu_custom_call" | custom-call | tf_op jit(solution)/shard_map/spread/pallas_call | solution.py:389
  98.3 2.4 %pack.1 = (f32[64,2432]{1,0:T(8,128)}, bf16[64,2560]{1,0:T(8,128)(2,1)S(1)}, bf16[64,2560]{1,0:T(8,128)(2,1)S(1)}, bf16[64,2560]{1,0:T(8,128)(2,1)S(1)}, f32[16,256]{1,0:T(8,128)S(1)}) custom-call(s32[9]{0:T(128)S(1)} %stack.39.place_ref, bf16[16,16,2432]{2,1,0:T(8,128)(2,1)} %get-tuple-element.36.own_ref, ...), custom_call_target="tpu_custom_call" | custom-call | tf_op jit(solution)/shard_map/pack/pallas_call | solution.py:427
  100.7 1.7 collective-permute-start.7
  102.4 6.0 %count.1.count_ref = bf16[256,8192]{1,0:T(8,128)(2,1)} custom-call(s32[1,4,8192]{2,1,0:T(4,128)} %index_ref.3, s32[1,8192]{1,0:T(1,128)} %length_ref.3), custom_call_target="tpu_custom_call" | custom-call | tf_op jit(solution)/shard_map/count/pallas_call | solution.py:446
  108.4 1.6 collective-permute-start.8
  110.0 0.5 collective-permute-start.9
  110.5 1.6 collective-permute-done.7
  112.2 6.3 %collective-permute-done.8 = bf16[64,2560]{1,0:T(8,128)(2,1)S(1)} collective-permute-done((bf16[64,2560]{1,0:T(8,128)(2,1)S(1)}, bf16[64,2560]{1,0:T(8,128)(2,1)S(1)}, u32[]{:S(2)}, u32[]{:S(2)}) %collective-permute-start.8) | collective-permute-done | bytes 327712 | tf_op jit(solution)/shard_map/ppermute | solution.py:503
  118.6 0.1 collective-permute-done.9
  118.7 0.1 slice_add_fusion
  119.1 1.1 collective-permute-done.10
  120.2 0.5 collective-permute-start.12
  120.7 2.9 %collective-permute-start.13 = (bf16[16,2944]{1,0:T(8,128)(2,1)S(1)}, bf16[16,2944]{1,0:T(8,128)(2,1)S(1)}, u32[]{:S(2)}, u32[]{:S(2)}) collective-permute-start(bf16[16,2944]{1,0:T(8,128)(2,1)S(1)} %get-tuple-element.57), channel_id=1, source_target_pairs={{0,6},{2,0},{4,2},{6,4},{1,7},{3,1},{5,3},{7,5},{8,14},{10,8},{12,... | collective-permute-start | bytes 282632 | tf_op jit(solution)/shard_map/ppermute | solution.py:503
  123.5 2.7 %collective-permute-done.12 = bf16[16,2944]{1,0:T(8,128)(2,1)S(1)} collective-permute-done((bf16[16,2944]{1,0:T(8,128)(2,1)S(1)}, bf16[16,2944]{1,0:T(8,128)(2,1)S(1)}, u32[]{:S(2)}, u32[]{:S(2)}) %collective-permute-start.12) | collective-permute-done | bytes 94240 | tf_op jit(solution)/shard_map/ppermute | solution.py:503
  126.3 1.3 collective-permute-done.13
  127.6 2.0 %collective-permute-done.11 = bf16[16,2944]{1,0:T(8,128)(2,1)S(1)} collective-permute-done((bf16[16,2944]{1,0:T(8,128)(2,1)S(1)}, bf16[16,2944]{1,0:T(8,128)(2,1)S(1)}, u32[]{:S(2)}, u32[]{:S(2)}) %collective-permute-start.11) | collective-permute-done | bytes 94240 | tf_op jit(solution)/shard_map/ppermute | solution.py:503
  129.8 1.6 collective-permute-start.14
  131.4 12.7 %all-to-all-start.2 = ((bf16[256,16,128]{2,1,0:T(8,128)(2,1)}), bf16[256,16,128]{2,1,0:T(8,128)(2,1)S(1)}, u32[]{:S(2)}, u32[]{:S(2)}) async-start(bf16[256,16,128]{2,1,0:T(8,128)(2,1)} %bitcast.25), calls=%async_computation.2 | async-start | bytes 2097152 | tf_op jit(solution)/shard_map/all_to_all | solution.py:516
  144.3 4.0 %collective-permute-start.17 = (f32[16,256]{1,0:T(8,128)S(1)}, f32[16,256]{1,0:T(8,128)S(1)}, u32[]{:S(2)}, u32[]{:S(2)}) collective-permute-start(f32[16,256]{1,0:T(8,128)S(1)} %fusion.11), channel_id=1, source_target_pairs={{0,192},{64,0},{128,64},{192,128},{1,193},{65,1},{129,65},{193,129... | collective-permute-start | bytes 49160 | tf_op jit(solution)/shard_map/ppermute | solution.py:503
  148.3 0.9 collective-permute-start.15
  149.1 0.6 slice_bitcast_fusion
  149.8 0.7 fusion.15
  150.5 17.7 %collective-permute-done.17 = f32[16,256]{1,0:T(8,128)S(1)} collective-permute-done((f32[16,256]{1,0:T(8,128)S(1)}, f32[16,256]{1,0:T(8,128)S(1)}, u32[]{:S(2)}, u32[]{:S(2)}) %collective-permute-start.17) | collective-permute-done | bytes 16416 | tf_op jit(solution)/shard_map/ppermute | solution.py:503
  168.2 1.2 collective-permute-done.16
  169.5 0.6 reshape.73
  170.1 4.6 %all-to-all-done.2 = bf16[256,16,128]{2,1,0:T(8,128)(2,1)S(1)} async-done(((bf16[256,16,128]{2,1,0:T(8,128)(2,1)}), bf16[256,16,128]{2,1,0:T(8,128)(2,1)S(1)}, u32[]{:S(2)}, u32[]{:S(2)}) %all-to-all-start.2) | async-done | bytes 1048608 | tf_op jit(solution)/shard_map/all_to_all | solution.py:516
  174.8 4.7 %row_grad.1 = f32[1,64,256]{2,1,0:T(8,128)} custom-call(bf16[256,8192]{1,0:T(8,128)(2,1)} %count.1.count_ref, bf16[4,64,16,128]{3,2,1,0:T(8,128)(2,1)S(1)} %bitcast.45), custom_call_target="tpu_custom_call" | custom-call | tf_op jit(solution)/shard_map/row_grad/pallas_call | solution.py:483
  (72 shorter events, 1.4 us)
Async XLA Ops:
  0.6 21.5 %copy-start = (bf16[13,256]{1,0:T(8,128)(2,1)S(1)}, bf16[13,256]{1,0:T(8,128)(2,1)}, u32[]{:S(2)}) copy-start(bf16[13,256]{1,0:T(8,128)(2,1)} %param.14) | copy-start | bytes 19972
  7.0 14.7 %copy-start.8 = (s32[128]{0:T(128)S(1)}, s32[128]{0:T(128)}, u32[]{:S(2)}) copy-start(s32[128]{0:T(128)} %param.17) | copy-start | bytes 1540
  7.0 14.9 %copy-start.6 = (bf16[128,13]{0,1:T(8,128)(2,1)S(1)}, bf16[128,13]{0,1:T(8,128)(2,1)}, u32[]{:S(2)}) copy-start(bf16[128,13]{0,1:T(8,128)(2,1)} %param.13) | copy-start | bytes 9988
  7.0 45.0 %copy-start.3 = (s32[64]{0:T(128)S(1)}, s32[64]{0:T(128)}, u32[]{:S(2)}) copy-start(s32[64]{0:T(128)} %slot_ref.3) | copy-start | bytes 772
  7.0 51.4 %copy-start.7 = (bf16[512]{0:T(512)(128)(2,1)S(1)}, bf16[512]{0:T(512)(128)(2,1)}, u32[]{:S(2)}) copy-start(bf16[512]{0:T(512)(128)(2,1)} %param.16) | copy-start | bytes 3076
  7.0 59.2 %copy-start.1 = (bf16[2336,512]{1,0:T(8,128)(2,1)S(1)}, bf16[2336,512]{1,0:T(8,128)(2,1)}, u32[]{:S(2)}) copy-start(bf16[2336,512]{1,0:T(8,128)(2,1)} %weight_ref.1) | copy-start | bytes 7176196
  7.1 44.9 %all-to-all-start = ((bf16[256,16,128]{2,1,0:T(8,128)(2,1)}), bf16[256,16,128]{2,1,0:T(8,128)(2,1)S(1)}, u32[]{:S(2)}, u32[]{:S(2)}) async-start(bf16[256,16,128]{2,1,0:T(8,128)(2,1)} %bitcast.47), calls=%async_computation | async-start | bytes 2097152 | tf_op jit(solution)/shard_map/all_to_all | solution.py:516
  54.8 9.1 %collective-permute-start.2 = (bf16[32,2432]{1,0:T(8,128)(2,1)S(1)}, bf16[32,2432]{1,0:T(8,128)(2,1)S(1)}, u32[]{:S(2)}, u32[]{:S(2)}) collective-permute-start(bf16[32,2432]{1,0:T(8,128)(2,1)S(1)} %get-tuple-element.25.f0), channel_id=1, source_target_pairs={{0,128},{64,200},{128,8},{192,64},{8,136},{72,192},{136,0},{200,72... | collective-permute-start | bytes 466952 | tf_op jit(solution)/shard_map/ppermute | solution.py:511
  56.4 7.6 %collective-permute-start.1 = (bf16[32,2432]{1,0:T(8,128)(2,1)S(1)}, bf16[32,2432]{1,0:T(8,128)(2,1)S(1)}, u32[]{:S(2)}, u32[]{:S(2)}) collective-permute-start(bf16[32,2432]{1,0:T(8,128)(2,1)S(1)} %get-tuple-element.25.f0), channel_id=1, source_target_pairs={{0,200},{64,0},{128,64},{192,128},{8,192},{72,8},{136,72},{200,136... | collective-permute-start | bytes 466952 | tf_op jit(solution)/shard_map/ppermute | solution.py:511
  56.5 9.8 %collective-permute-start = (bf16[32,2432]{1,0:T(8,128)(2,1)S(1)}, bf16[32,2432]{1,0:T(8,128)(2,1)S(1)}, u32[]{:S(2)}, u32[]{:S(2)}) collective-permute-start(bf16[32,2432]{1,0:T(8,128)(2,1)S(1)} %get-tuple-element.25.f0), channel_id=1, source_target_pairs={{0,64},{64,128},{128,192},{192,8},{8,72},{72,136},{136,200},{200,0... | collective-permute-start | bytes 466952 | tf_op jit(solution)/shard_map/ppermute | solution.py:511
  68.3 25.0 %copy-start.2 = (bf16[32,2432]{1,0:T(8,128)(2,1)S(1)}, bf16[32,2432]{1,0:T(8,128)(2,1)}, u32[]{:S(2)}) copy-start(bf16[32,2432]{1,0:T(8,128)(2,1)} %get-tuple-element.26.z0) | copy-start | bytes 466948
  68.3 11.1 %all-to-all-start.1 = ((f32[8,8,128]{2,1,0:T(8,128)}), f32[8,8,128]{2,1,0:T(8,128)S(1)}, u32[]{:S(2)}, u32[]{:S(2)}) async-start(f32[8,8,128]{2,1,0:T(8,128)} %get-tuple-element.30), calls=%async_computation.1 | async-start | bytes 65536 | tf_op jit(solution)/shard_map/all_to_all | solution.py:611
  83.3 15.1 %collective-permute-start.6 = (bf16[16,16,2432]{2,1,0:T(8,128)(2,1)}, bf16[16,16,2432]{2,1,0:T(8,128)(2,1)S(1)}, u32[]{:S(2)}, u32[]{:S(2)}) collective-permute-start(bf16[16,16,2432]{2,1,0:T(8,128)(2,1)} %get-tuple-element.37), channel_id=1, source_target_pairs={{0,1},{1,0},{2,3},{3,2},{4,5},{5,4},{6,7},{7,6},{8,9},{9,8},{10,11... | collective-permute-start | bytes 3735560 | tf_op jit(solution)/shard_map/ppermute | solution.py:503
  83.3 6.6 %collective-permute-start.3 = (bf16[32,2432]{1,0:T(8,128)(2,1)S(1)}, bf16[32,2432]{1,0:T(8,128)(2,1)S(1)}, u32[]{:S(2)}, u32[]{:S(2)}) collective-permute-start(bf16[32,2432]{1,0:T(8,128)(2,1)S(1)} %get-tuple-element.27), channel_id=1, source_target_pairs={{0,200},{64,0},{128,64},{192,128},{8,192},{72,8},{136,72},{200,136... | collective-permute-start | bytes 466952 | tf_op jit(solution)/shard_map/ppermute | solution.py:511
  84.0 8.1 %collective-permute-start.4 = (bf16[32,2432]{1,0:T(8,128)(2,1)S(1)}, bf16[32,2432]{1,0:T(8,128)(2,1)S(1)}, u32[]{:S(2)}, u32[]{:S(2)}) collective-permute-start(bf16[32,2432]{1,0:T(8,128)(2,1)S(1)} %get-tuple-element.28), channel_id=1, source_target_pairs={{0,64},{64,128},{128,192},{192,8},{8,72},{72,136},{136,200},{200,0... | collective-permute-start | bytes 466952 | tf_op jit(solution)/shard_map/ppermute | solution.py:511
  85.3 8.0 %collective-permute-start.5 = (bf16[32,2432]{1,0:T(8,128)(2,1)S(1)}, bf16[32,2432]{1,0:T(8,128)(2,1)S(1)}, u32[]{:S(2)}, u32[]{:S(2)}) collective-permute-start(bf16[32,2432]{1,0:T(8,128)(2,1)S(1)} %get-tuple-element.29), channel_id=1, source_target_pairs={{0,136},{64,192},{128,0},{192,72},{8,128},{72,200},{136,8},{200,64... | collective-permute-start | bytes 466952 | tf_op jit(solution)/shard_map/ppermute | solution.py:511
  100.7 11.5 %collective-permute-start.7 = (bf16[64,2560]{1,0:T(8,128)(2,1)S(1)}, bf16[64,2560]{1,0:T(8,128)(2,1)S(1)}, u32[]{:S(2)}, u32[]{:S(2)}) collective-permute-start(bf16[64,2560]{1,0:T(8,128)(2,1)S(1)} %get-tuple-element.40), channel_id=1, source_target_pairs={{0,32},{16,48},{32,0},{48,16},{1,33},{17,49},{33,1},{49,17},{2,34}... | collective-permute-start | bytes 983048 | tf_op jit(solution)/shard_map/ppermute | solution.py:503
  108.4 10.1 %collective-permute-start.8 = (bf16[64,2560]{1,0:T(8,128)(2,1)S(1)}, bf16[64,2560]{1,0:T(8,128)(2,1)S(1)}, u32[]{:S(2)}, u32[]{:S(2)}) collective-permute-start(bf16[64,2560]{1,0:T(8,128)(2,1)S(1)} %get-tuple-element.41), channel_id=1, source_target_pairs={{0,16},{16,32},{32,48},{48,0},{1,17},{17,33},{33,49},{49,1},{2,18}... | collective-permute-start | bytes 983048 | tf_op jit(solution)/shard_map/ppermute | solution.py:503
  110.0 8.7 %collective-permute-start.9 = (bf16[64,2560]{1,0:T(8,128)(2,1)S(1)}, bf16[64,2560]{1,0:T(8,128)(2,1)S(1)}, u32[]{:S(2)}, u32[]{:S(2)}) collective-permute-start(bf16[64,2560]{1,0:T(8,128)(2,1)S(1)} %get-tuple-element.42), channel_id=1, source_target_pairs={{0,48},{16,0},{32,16},{48,32},{1,49},{17,1},{33,17},{49,33},{2,50}... | collective-permute-start | bytes 983048 | tf_op jit(solution)/shard_map/ppermute | solution.py:503
  112.2 6.5 %copy-start.4 = (f32[64,2432]{1,0:T(8,128)S(1)}, f32[64,2432]{1,0:T(8,128)}, u32[]{:S(2)}) copy-start(f32[64,2432]{1,0:T(8,128)} %get-tuple-element.43) | copy-start | bytes 1867780
  118.9 1.3 collective-permute-start.10
  120.2 6.1 %collective-permute-start.12 = (bf16[16,2944]{1,0:T(8,128)(2,1)S(1)}, bf16[16,2944]{1,0:T(8,128)(2,1)S(1)}, u32[]{:S(2)}, u32[]{:S(2)}) collective-permute-start(bf16[16,2944]{1,0:T(8,128)(2,1)S(1)} %get-tuple-element.56), channel_id=1, source_target_pairs={{0,2},{2,4},{4,6},{6,0},{1,3},{3,5},{5,7},{7,1},{8,10},{10,12},{12... | collective-permute-start | bytes 282632 | tf_op jit(solution)/shard_map/ppermute | solution.py:503
  120.7 6.9 %collective-permute-start.13 = (bf16[16,2944]{1,0:T(8,128)(2,1)S(1)}, bf16[16,2944]{1,0:T(8,128)(2,1)S(1)}, u32[]{:S(2)}, u32[]{:S(2)}) collective-permute-start(bf16[16,2944]{1,0:T(8,128)(2,1)S(1)} %get-tuple-element.57), channel_id=1, source_target_pairs={{0,6},{2,0},{4,2},{6,4},{1,7},{3,1},{5,3},{7,5},{8,14},{10,8},{12,... | collective-permute-start | bytes 282632 | tf_op jit(solution)/shard_map/ppermute | solution.py:503
  123.5 6.1 %collective-permute-start.11 = (bf16[16,2944]{1,0:T(8,128)(2,1)S(1)}, bf16[16,2944]{1,0:T(8,128)(2,1)S(1)}, u32[]{:S(2)}, u32[]{:S(2)}) collective-permute-start(bf16[16,2944]{1,0:T(8,128)(2,1)S(1)} %get-tuple-element.58), channel_id=1, source_target_pairs={{0,4},{2,6},{4,0},{6,2},{1,5},{3,7},{5,1},{7,3},{8,12},{10,14},{12... | collective-permute-start | bytes 282632 | tf_op jit(solution)/shard_map/ppermute | solution.py:503
  129.8 14.4 %collective-permute-start.14 = (bf16[8,3456]{1,0:T(8,128)(2,1)S(1)}, bf16[8,3456]{1,0:T(8,128)(2,1)S(1)}, u32[]{:S(2)}, u32[]{:S(2)}) collective-permute-start(bf16[8,3456]{1,0:T(8,128)(2,1)S(1)} %constant_dynamic-update-slice_fusion), channel_id=1, source_target_pairs={{0,8},{8,0},{1,9},{9,1},{2,10},{10,2},{3,11},{11,3},{4,12},{12,4},... | collective-permute-start | bytes 165896 | tf_op jit(solution)/shard_map/ppermute | solution.py:503
  131.4 43.3 %all-to-all-start.2 = ((bf16[256,16,128]{2,1,0:T(8,128)(2,1)}), bf16[256,16,128]{2,1,0:T(8,128)(2,1)S(1)}, u32[]{:S(2)}, u32[]{:S(2)}) async-start(bf16[256,16,128]{2,1,0:T(8,128)(2,1)} %bitcast.25), calls=%async_computation.2 | async-start | bytes 2097152 | tf_op jit(solution)/shard_map/all_to_all | solution.py:516
  144.3 23.9 %collective-permute-start.17 = (f32[16,256]{1,0:T(8,128)S(1)}, f32[16,256]{1,0:T(8,128)S(1)}, u32[]{:S(2)}, u32[]{:S(2)}) collective-permute-start(f32[16,256]{1,0:T(8,128)S(1)} %fusion.11), channel_id=1, source_target_pairs={{0,192},{64,0},{128,64},{192,128},{1,193},{65,1},{129,65},{193,129... | collective-permute-start | bytes 49160 | tf_op jit(solution)/shard_map/ppermute | solution.py:503
  148.3 21.1 %collective-permute-start.16 = (f32[16,256]{1,0:T(8,128)S(1)}, f32[16,256]{1,0:T(8,128)S(1)}, u32[]{:S(2)}, u32[]{:S(2)}) collective-permute-start(f32[16,256]{1,0:T(8,128)S(1)} %fusion.11), channel_id=1, source_target_pairs={{0,64},{64,128},{128,192},{192,0},{1,65},{65,129},{129,193},{193,1... | collective-permute-start | bytes 49160 | tf_op jit(solution)/shard_map/ppermute | solution.py:503
  148.3 21.1 %collective-permute-start.15 = (f32[16,256]{1,0:T(8,128)S(1)}, f32[16,256]{1,0:T(8,128)S(1)}, u32[]{:S(2)}, u32[]{:S(2)}) collective-permute-start(f32[16,256]{1,0:T(8,128)S(1)} %fusion.11), channel_id=1, source_target_pairs={{0,128},{64,192},{128,0},{192,64},{1,129},{65,193},{129,1},{193,65... | collective-permute-start | bytes 49160 | tf_op jit(solution)/shard_map/ppermute | solution.py:503
  169.4 10.1 %copy-start.5 = (f32[16,256]{1,0:T(8,128)}, f32[16,256]{1,0:T(8,128)S(1)}, u32[]{:S(2)}) copy-start(f32[16,256]{1,0:T(8,128)S(1)} %add_add_fusion) | copy-start | bytes 49156

commit v6 on v5

--- a/solution.py
+++ b/solution.py
@@ -14,12 +14,13 @@
 
 TAB = 64
 ROWS = 16
+APART = 24
 LANES = 128
 HALF = 64
 EMB = 256
 FEAT = 2336
 WIDE = 2432
-STEP = 8
+STEP = 16
 GRAD_STEP = 16
 LABEL_LANE = 36
 
@@ -130,7 +131,7 @@
 
 def interact_kernel(slot_ref, arrived_ref, mine_ref, label_ref, out_ref, vectors_ref, spaced, gram, edge):
     def place(table, carry):
-        start = pl.multiple_of(slot_ref[table] * ROWS, ROWS)
+        start = pl.multiple_of(slot_ref[table] * APART, 8)
         for part in range(4):
             spaced[part, pl.ds(start, ROWS), :] = arrived_ref[part, table].astype(F32)
         return carry
@@ -142,14 +143,14 @@
     second = jnp.where(low, 0.0, 1.0).astype(BF16)
     for row in range(ROWS):
         vectors = jnp.concatenate(
-            [spaced[part, pl.ds(row, TAB, stride=ROWS), :] for part in range(4)], axis=1
+            [spaced[part, pl.ds(row, TAB, stride=APART), :] for part in range(4)], axis=1
         )
         narrow = vectors.astype(BF16)
         vectors_ref[row] = narrow
         right = jnp.concatenate([narrow * first, narrow * second], axis=0)
         extra = jnp.broadcast_to(bottom[row : row + 1], (ROWS, 512)).astype(BF16)
         product = dot_t(jnp.concatenate([narrow, extra], axis=0), right)
-        gram[pl.ds(row, TAB, stride=ROWS), :] = product[0:TAB]
+        gram[pl.ds(row, TAB, stride=APART), :] = product[0:TAB]
         edge[row : row + 1, :] = product[TAB : TAB + 1]
 
     lane = lane_iota(ROWS)
@@ -158,14 +159,14 @@
         out_ref[where, 0:EMB] = mine_ref[where, :].astype(BF16)
         tile, filled = EMB // LANES, jnp.zeros((ROWS, LANES), F32)
         for row, start, count, spot in pieces():
-            source = edge[...] if row < 0 else gram[row * ROWS : (row + 1) * ROWS, :]
+            source = edge[...] if row < 0 else gram[row * APART : row * APART + ROWS, :]
             moved = turned(source, spot - start - half * HALF)
-            for at, first, end in parts_of(spot, count):
+            for at, first, _ in parts_of(spot, count):
                 if at != tile:
                     out_ref[where, tile * LANES : (tile + 1) * LANES] = filled.astype(BF16)
-                    tile, filled = at, jnp.zeros((ROWS, LANES), F32)
-                filled = jnp.where((lane >= first) & (lane < end), moved, filled)
-        filled = jnp.where(lane == LABEL_LANE, label_ref[where, :], filled)
+                    tile, filled = at, moved
+                filled = moved if first == 0 else jnp.where(lane >= first, moved, filled)
+        filled = jnp.where(lane < FEAT % LANES, filled, jnp.where(lane == LABEL_LANE, label_ref[where, :], 0.0))
         out_ref[where, tile * LANES : (tile + 1) * LANES] = filled.astype(BF16)
 
 
@@ -182,8 +183,8 @@
             hbm((ROWS, TAB, 512), BF16),
         ],
         scratch_shapes=[
-            pltpu.VMEM((4, TAB * ROWS, LANES), F32),
-            pltpu.VMEM((TAB * ROWS, LANES), F32),
+            pltpu.VMEM((4, TAB * APART, LANES), F32),
+            pltpu.VMEM((TAB * APART, LANES), F32),
             pltpu.VMEM((ROWS, LANES), F32),
         ],
         compiler_params=pltpu.CompilerParams(vmem_limit_bytes=16 << 20),
@@ -300,31 +301,33 @@
 
 def spread_kernel(
     slot_ref, place_ref, z0, z1, z2, z3, partial_ref, label_ref, vectors_ref, mine_ref,
-    slope_ref, dense_ref, back_ref, bottom_ref, logit_ref, dfeat, upper, edge, rights, dvec, dedge,
+    slope_ref, dense_ref, back_ref, bottom_ref, logit_ref, dfeat, dpairs, upper, edge, dvec, dedge,
 ):
     logits = own_logits(place_ref[1] == 0, *(partial_ref[place_ref[2 + i]] for i in range(5)))
     logit_ref[...] = logits
     labels = jnp.sum(jnp.where(lane_iota(32) == LABEL_LANE, label_ref[...], 0.0), axis=1, keepdims=True)
     column = (jax.nn.sigmoid(logits.T[0:32, 0:1]) - labels) * (1.0 / 128.0)
     summed = z0[...].astype(F32) + z1[...].astype(F32) + z2[...].astype(F32) + z3[...].astype(F32)
-    dfeat[...] = summed * column
+    summed = summed * column
+    dfeat[...] = summed[:, 0:EMB]
+    dpairs[...] = summed.astype(BF16).astype(F32)
     lane = lane_iota(ROWS)
+    none = jnp.zeros((ROWS, LANES), F32)
     for row, start, count, spot in pieces():
-        filled = jnp.zeros((ROWS, LANES), F32)
+        filled = none
         for half in range(2):
-            for at, first, end in parts_of(spot, count):
-                source = dfeat[half * ROWS : (half + 1) * ROWS, at * LANES : (at + 1) * LANES]
+            for at, first, _ in parts_of(spot, count):
+                source = dpairs[half * ROWS : (half + 1) * ROWS, at * LANES : (at + 1) * LANES]
                 moved = turned(source, start + half * HALF - spot)
-                shift = start + half * HALF - spot + at * LANES
-                inside = (lane >= first + shift) & (lane < end + shift)
-                filled = jnp.where(inside, moved, filled)
-        filled = filled.astype(BF16).astype(F32)
+                begin = first + start + half * HALF - spot + at * LANES
+                filled = jnp.where(lane >= begin, moved, filled)
+            if half == 0 and row >= 0:
+                filled = jnp.where(lane >= HALF, 0.0, filled)
         if row < 0:
             edge[...] = filled
         else:
-            upper[row * ROWS : (row + 1) * ROWS, :] = filled
-    upper[(TAB - 1) * ROWS :, :] = jnp.zeros((ROWS, LANES), F32)
-    rights[...] = jnp.zeros_like(rights)
+            upper[row * APART : row * APART + ROWS, :] = filled
+    upper[(TAB - 1) * APART : (TAB - 1) * APART + ROWS, :] = jnp.zeros((ROWS, LANES), F32)
     bottom = packed_bottom(mine_ref)
     low = low_lanes(TAB)
     low_wide = jnp.concatenate([low] * 4, axis=1)
@@ -332,8 +335,11 @@
     high_factor = jnp.where(low_wide, 0.0, 1.0).astype(BF16)
     low_few = jnp.concatenate([low_lanes(16)] * 4, axis=1)
     top_row = lax.broadcasted_iota(jnp.int32, (16, 512), 0) == 0
+    low_own = jnp.where(top_row & low_few, 1.0, 0.0).astype(BF16)
+    high_own = jnp.where(top_row & ~low_few, 1.0, 0.0).astype(BF16)
+    empty = jnp.zeros((48, 512), BF16)
     for row in range(ROWS):
-        half = upper[pl.ds(row, TAB, stride=ROWS), :]
+        half = upper[pl.ds(row, TAB, stride=APART), :]
         zeroth = jnp.broadcast_to(edge[row : row + 1, :], (TAB, LANES))
         flipped = jnp.concatenate([half, zeroth], axis=0).T
         first, second = flipped[0:TAB], turned(flipped[TAB : 2 * TAB], HALF)
@@ -346,20 +352,19 @@
             ],
             axis=0,
         ).astype(BF16)
-        right = rights.at[row % 2]
-        right[0:TAB, :] = vectors_ref[row] * low_factor
-        right[TAB : 2 * TAB, :] = vectors_ref[row] * high_factor
-        own = jnp.broadcast_to(bottom[row : row + 1], (16, 512))
-        right[128:144, :] = jnp.where(top_row & ~low_few, own, 0.0).astype(BF16)
-        right[192:208, :] = jnp.where(top_row & low_few, own, 0.0).astype(BF16)
-        product = jnp.dot(left, right[...], preferred_element_type=F32)
+        vectors = vectors_ref[row]
+        own = jnp.broadcast_to(bottom[row : row + 1], (16, 512)).astype(BF16)
+        right = jnp.concatenate(
+            [vectors * low_factor, vectors * high_factor, own * high_own, empty, own * low_own, empty], axis=0
+        )
+        product = jnp.dot(left, right, preferred_element_type=F32)
         for part in range(4):
             lanes = slice(part * LANES, (part + 1) * LANES)
-            dvec[part, pl.ds(row, TAB, stride=ROWS), :] = product[0:TAB, lanes]
+            dvec[part, pl.ds(row, TAB, stride=APART), :] = product[0:TAB, lanes]
         dedge[row : row + 1, :] = product[TAB : TAB + 1]
 
     def place(table, carry):
-        start = pl.multiple_of(slot_ref[table] * ROWS, ROWS)
+        start = pl.multiple_of(slot_ref[table] * APART, 8)
         for part in range(4):
             back_ref[part, table] = dvec[part, pl.ds(start, ROWS), :].astype(BF16)
         return carry
@@ -375,7 +380,7 @@
             [jnp.where(low, turned(tiles[2 * p], HALF), tiles[2 * p + 1]) for p in range(2)], axis=1
         ),
     ]
-    dbottom = (dfeat[:, 0:EMB] + jnp.concatenate(own_rows, axis=0)) * slope_ref[...]
+    dbottom = (dfeat[...] + jnp.concatenate(own_rows, axis=0)) * slope_ref[...]
     bottom_ref[...] = lax.dot_general(
         dense_ref[...],
         dbottom,
@@ -396,11 +401,11 @@
             jax.ShapeDtypeStruct((8, LANES), F32),
         ],
         scratch_shapes=[
+            pltpu.VMEM((2 * ROWS, EMB), F32),
             pltpu.VMEM((2 * ROWS, WIDE), F32),
-            pltpu.VMEM((TAB * ROWS, LANES), F32),
+            pltpu.VMEM((TAB * APART, LANES), F32),
             pltpu.VMEM((ROWS, LANES), F32),
-            pltpu.VMEM((2, 256, 512), BF16),
-            pltpu.VMEM((4, TAB * ROWS, LANES), F32),
+            pltpu.VMEM((4, TAB * APART, LANES), F32),
             pltpu.VMEM((ROWS, 512), F32),
         ],
         compiler_params=pltpu.CompilerParams(vmem_limit_bytes=16 << 20),

time: 182 us -> 178 us (0.978)
  Pallas kernels: 33.2 us -> 29.3 us
  transfers between devices with their start and end apart: 21 -> 21, of which waited for: 18 -> 17; matrix products, arithmetic and copies ran while one was open for 2% -> 2% of each run, Pallas kernels for 6% -> 5%
where the time goes in v6:
time: 178 us; the launch traced here: 176 us
  waiting for transfers between devices  91.7 us (52%)
  starting transfers between devices  49.9 us (28%)
  Pallas kernels  29.3 us (16%)
  local copies, waits for them, and re-layouts  2.11 us (1%)
    ppermute x12, waiting for transfers between devices, shifted(): return lax.ppermute(x, axis, [(i, (i + shift) % size) for i in range(size)])  35.2 us
    all_to_all x2, waiting for transfers between devices, exchange_all(): lax.all_to_all(flat, COL_GRP, split_axis=0, concat_axis=0, tiled=True)  34.2 us
    all_to_all x2, starting transfers between devices, exchange_all(): lax.all_to_all(flat, COL_GRP, split_axis=0, concat_axis=0, tiled=True)  26.4 us
    ppermute x6, waiting for transfers between devices, ring_sent(): return lax.ppermute(x, ('col', 'grp_1'), pairs)  15 us
    ppermute x12, starting transfers between devices, shifted(): return lax.ppermute(x, axis, [(i, (i + shift) % size) for i in range(size)])  13.6 us
    all_to_all x1, waiting for transfers between devices, step(): lax.all_to_all(partial, ('col', 'grp_1'), split_axis=0, concat_axis=0, ti...  7.2 us
    ppermute x6, starting transfers between devices, ring_sent(): return lax.ppermute(x, ('col', 'grp_1'), pairs)  6.43 us
    pallas_call x1, Pallas kernels, pool(): pl.pallas_call(pool_kernel, grid=(TAB // STEP,), in_specs=[pl.BlockSpec((...  4.79 us
  transfers between devices with their start and end apart: 21, of which 17 were waited for; matrix products, arithmetic and copies ran while one was open for 2% of the time, Pallas kernels for 5%

profile of v6, /device:TPU:4, one launch (start us, length us, event | category | flops | bytes accessed | tf_op | source)
XLA Modules:
  0.0 175.7 jit_solution(6490965409938937415)
XLA Ops:
  0.6 4.8 %pool.1 = bf16[4,64,16,128]{3,2,1,0:T(8,128)(2,1)} custom-call(s32[1,4,8192]{2,1,0:T(4,128)} %index_ref.3, s32[1,8192]{1,0:T(1,128)} %length_ref.3, bf16[1,64,256]{2,1,0:T(8,128)(2,1)} %bitcast.51), custom_call_target="tpu_custom_call" | custom-call | tf_op jit(solution)/shard_map/pool/pallas_call | solution.py:106
  5.5 14.7 %all-to-all-start = ((bf16[256,16,128]{2,1,0:T(8,128)(2,1)}), bf16[256,16,128]{2,1,0:T(8,128)(2,1)S(1)}, u32[]{:S(2)}, u32[]{:S(2)}) async-start(bf16[256,16,128]{2,1,0:T(8,128)(2,1)} %bitcast.47), calls=%async_computation | async-start | bytes 2097152 | tf_op jit(solution)/shard_map/all_to_all | solution.py:521
  20.5 0.1 copy.18
  20.6 0.1 add_multiply_fusion
  20.7 29.6 %all-to-all-done = bf16[256,16,128]{2,1,0:T(8,128)(2,1)S(1)} async-done(((bf16[256,16,128]{2,1,0:T(8,128)(2,1)}), bf16[256,16,128]{2,1,0:T(8,128)(2,1)S(1)}, u32[]{:S(2)}, u32[]{:S(2)}) %all-to-all-start) | async-done | bytes 1048608 | tf_op jit(solution)/shard_map/all_to_all | solution.py:521
  50.4 2.7 %interact.1 = (bf16[32,2432]{1,0:T(8,128)(2,1)S(1)}, bf16[16,64,512]{2,1,0:T(8,128)(2,1)}) custom-call(s32[64]{0:T(128)S(1)} %copy-done.3, bf16[4,64,16,128]{3,2,1,0:T(8,128)(2,1)S(1)} %bitcast.44, f32[32,256]{1,0:T(8,128)S(1)} %get-tuple-element.55.mine_ref, f32[32,128]{1,0:T(8,128)S(1)} %broadcast_in_dim.17.label_ref), custom_call_target="tpu_custom_call" | custom-call | tf_op jit(solution)/shard_map/interact/pallas_call | solution.py:174
  53.1 1.5 collective-permute-start.2
  54.6 0.1 collective-permute-start.1
  54.8 1.9 %collective-permute-start = (bf16[32,2432]{1,0:T(8,128)(2,1)S(1)}, bf16[32,2432]{1,0:T(8,128)(2,1)S(1)}, u32[]{:S(2)}, u32[]{:S(2)}) collective-permute-start(bf16[32,2432]{1,0:T(8,128)(2,1)S(1)} %get-tuple-element.25.f0), channel_id=1, source_target_pairs={{0,64},{64,128},{128,192},{192,8},{8,72},{72,136},{136,200},{200,0... | collective-permute-start | bytes 466952 | tf_op jit(solution)/shard_map/ppermute | solution.py:516
  56.7 5.5 %collective-permute-done.2.f3 = bf16[32,2432]{1,0:T(8,128)(2,1)S(1)} collective-permute-done((bf16[32,2432]{1,0:T(8,128)(2,1)S(1)}, bf16[32,2432]{1,0:T(8,128)(2,1)S(1)}, u32[]{:S(2)}, u32[]{:S(2)}) %collective-permute-start.2) | collective-permute-done | bytes 155680 | tf_op jit(solution)/shard_map/ppermute | solution.py:516
  62.2 0.1 collective-permute-done.1.f2
  62.3 2.3 %collective-permute-done.f1 = bf16[32,2432]{1,0:T(8,128)(2,1)S(1)} collective-permute-done((bf16[32,2432]{1,0:T(8,128)(2,1)S(1)}, bf16[32,2432]{1,0:T(8,128)(2,1)S(1)}, u32[]{:S(2)}, u32[]{:S(2)}) %collective-permute-start) | collective-permute-done | bytes 155680 | tf_op jit(solution)/shard_map/ppermute | solution.py:516
  64.5 2.0 %top.1 = (bf16[128,2432]{1,0:T(8,128)(2,1)}, bf16[32,2432]{1,0:T(8,128)(2,1)}, bf16[32,2432]{1,0:T(8,128)(2,1)S(1)}, bf16[32,2432]{1,0:T(8,128)(2,1)S(1)}, bf16[...) custom-call(bf16[32,2432]{1,0:T(8,128)(2,1)S(1)} %get-tuple-element.25.f0, ...), custom_call_target="tpu_custom_call" | custom-call | tf_op jit(solution)/shard_map/top/pallas_call | solution.py:220
  66.5 3.5 %all-to-all-start.1 = ((f32[8,8,128]{2,1,0:T(8,128)}), f32[8,8,128]{2,1,0:T(8,128)S(1)}, u32[]{:S(2)}, u32[]{:S(2)}) async-start(f32[8,8,128]{2,1,0:T(8,128)} %get-tuple-element.30), calls=%async_computation.1 | async-start | bytes 65536 | tf_op jit(solution)/shard_map/all_to_all | solution.py:616
  70.4 7.2 %all-to-all-done.1.partial_ref = f32[8,8,128]{2,1,0:T(8,128)S(1)} async-done(((f32[8,8,128]{2,1,0:T(8,128)}), f32[8,8,128]{2,1,0:T(8,128)S(1)}, u32[]{:S(2)}, u32[]{:S(2)}) %all-to-all-start.1) | async-done | bytes 32800 | tf_op jit(solution)/shard_map/all_to_all | solution.py:616
  77.6 3.9 %weight_grad.1 = (bf16[16,16,2432]{2,1,0:T(8,128)(2,1)}, bf16[16,16,2432]{2,1,0:T(8,128)(2,1)}) custom-call(s32[9]{0:T(128)S(1)} %stack.39.place_ref, f32[8,8,128]{2,1,0:T(8,128)S(1)} %all-to-all-done.1.partial_ref, bf16[128,2432]{1,0:T(8,128)(2,1)} %get-tuple-element.33.all_ref, bf16[128,512]{1,0:T(8,128)(2,1)} %get-tuple-element.34.delta_ref, ...), custom_call_target="tpu_custom_call" | custom-call | tf_op jit(solution)/shard_map/weight_grad/pallas_call | solution.py:288
  81.5 0.7 collective-permute-start.3
  82.2 1.3 collective-permute-start.4
  83.6 0.9 collective-permute-start.5
  84.4 3.7 %collective-permute-done.3.z1 = bf16[32,2432]{1,0:T(8,128)(2,1)S(1)} collective-permute-done((bf16[32,2432]{1,0:T(8,128)(2,1)S(1)}, bf16[32,2432]{1,0:T(8,128)(2,1)S(1)}, u32[]{:S(2)}, u32[]{:S(2)}) %collective-permute-start.3) | collective-permute-done | bytes 155680 | tf_op jit(solution)/shard_map/ppermute | solution.py:516
  88.2 2.2 %collective-permute-done.4.z2 = bf16[32,2432]{1,0:T(8,128)(2,1)S(1)} collective-permute-done((bf16[32,2432]{1,0:T(8,128)(2,1)S(1)}, bf16[32,2432]{1,0:T(8,128)(2,1)S(1)}, u32[]{:S(2)}, u32[]{:S(2)}) %collective-permute-start.4) | collective-permute-done | bytes 155680 | tf_op jit(solution)/shard_map/ppermute | solution.py:516
  90.3 1.2 collective-permute-done.5.z3
  91.6 4.1 %spread.1 = (bf16[4,64,16,128]{3,2,1,0:T(8,128)(2,1)}, f32[16,256]{1,0:T(8,128)S(1)}, f32[8,128]{1,0:T(8,128)S(1)}) custom-call(s32[64]{0:T(128)S(1)} %copy-done.3, s32[9]{0:T(128)S(1)} %stack.39.place_ref, bf16[32,2432]{1,0:T(8,128)(2,1)S(1)} %copy-done.2, bf16[32,2432]{1,0:T(8,128)(2,1)S(1)} %collective-permute-done.3.z1, ...), custom_call_target="tpu_custom_call" | custom-call | tf_op jit(solution)/shard_map/spread/pallas_call | solution.py:394
  95.7 2.4 %pack.1 = (f32[64,2432]{1,0:T(8,128)}, bf16[64,2560]{1,0:T(8,128)(2,1)S(1)}, bf16[64,2560]{1,0:T(8,128)(2,1)S(1)}, bf16[64,2560]{1,0:T(8,128)(2,1)S(1)}, f32[16,256]{1,0:T(8,128)S(1)}) custom-call(s32[9]{0:T(128)S(1)} %stack.39.place_ref, bf16[16,16,2432]{2,1,0:T(8,128)(2,1)} %get-tuple-element.36.own_ref, ...), custom_call_target="tpu_custom_call" | custom-call | tf_op jit(solution)/shard_map/pack/pallas_call | solution.py:432
  98.0 1.7 collective-permute-start.7
  99.8 4.7 %count.1.count_ref = bf16[256,8192]{1,0:T(8,128)(2,1)} custom-call(s32[1,4,8192]{2,1,0:T(4,128)} %index_ref.3, s32[1,8192]{1,0:T(1,128)} %length_ref.3), custom_call_target="tpu_custom_call" | custom-call | tf_op jit(solution)/shard_map/count/pallas_call | solution.py:451
  104.5 1.5 collective-permute-start.8
  106.0 0.6 collective-permute-start.9
  106.6 3.6 %collective-permute-done.7 = bf16[64,2560]{1,0:T(8,128)(2,1)S(1)} collective-permute-done((bf16[64,2560]{1,0:T(8,128)(2,1)S(1)}, bf16[64,2560]{1,0:T(8,128)(2,1)S(1)}, u32[]{:S(2)}, u32[]{:S(2)}) %collective-permute-start.7) | collective-permute-done | bytes 327712 | tf_op jit(solution)/shard_map/ppermute | solution.py:508
  110.2 5.6 %collective-permute-done.8 = bf16[64,2560]{1,0:T(8,128)(2,1)S(1)} collective-permute-done((bf16[64,2560]{1,0:T(8,128)(2,1)S(1)}, bf16[64,2560]{1,0:T(8,128)(2,1)S(1)}, u32[]{:S(2)}, u32[]{:S(2)}) %collective-permute-start.8) | collective-permute-done | bytes 327712 | tf_op jit(solution)/shard_map/ppermute | solution.py:508
  116.0 0.1 slice_add_fusion
  116.3 1.1 collective-permute-done.10
  117.5 0.6 collective-permute-start.12
  118.0 2.8 %collective-permute-start.13 = (bf16[16,2944]{1,0:T(8,128)(2,1)S(1)}, bf16[16,2944]{1,0:T(8,128)(2,1)S(1)}, u32[]{:S(2)}, u32[]{:S(2)}) collective-permute-start(bf16[16,2944]{1,0:T(8,128)(2,1)S(1)} %get-tuple-element.57), channel_id=1, source_target_pairs={{0,6},{2,0},{4,2},{6,4},{1,7},{3,1},{5,3},{7,5},{8,14},{10,8},{12,... | collective-permute-start | bytes 282632 | tf_op jit(solution)/shard_map/ppermute | solution.py:508
  120.8 2.7 %collective-permute-done.12 = bf16[16,2944]{1,0:T(8,128)(2,1)S(1)} collective-permute-done((bf16[16,2944]{1,0:T(8,128)(2,1)S(1)}, bf16[16,2944]{1,0:T(8,128)(2,1)S(1)}, u32[]{:S(2)}, u32[]{:S(2)}) %collective-permute-start.12) | collective-permute-done | bytes 94240 | tf_op jit(solution)/shard_map/ppermute | solution.py:508
  123.5 1.3 collective-permute-done.13
  124.9 2.0 %collective-permute-done.11 = bf16[16,2944]{1,0:T(8,128)(2,1)S(1)} collective-permute-done((bf16[16,2944]{1,0:T(8,128)(2,1)S(1)}, bf16[16,2944]{1,0:T(8,128)(2,1)S(1)}, u32[]{:S(2)}, u32[]{:S(2)}) %collective-permute-start.11) | collective-permute-done | bytes 94240 | tf_op jit(solution)/shard_map/ppermute | solution.py:508
  127.0 1.6 collective-permute-start.14
  128.7 11.7 %all-to-all-start.2 = ((bf16[256,16,128]{2,1,0:T(8,128)(2,1)}), bf16[256,16,128]{2,1,0:T(8,128)(2,1)S(1)}, u32[]{:S(2)}, u32[]{:S(2)}) async-start(bf16[256,16,128]{2,1,0:T(8,128)(2,1)} %bitcast.25), calls=%async_computation.2 | async-start | bytes 2097152 | tf_op jit(solution)/shard_map/all_to_all | solution.py:521
  140.5 4.0 %collective-permute-start.17 = (f32[16,256]{1,0:T(8,128)S(1)}, f32[16,256]{1,0:T(8,128)S(1)}, u32[]{:S(2)}, u32[]{:S(2)}) collective-permute-start(f32[16,256]{1,0:T(8,128)S(1)} %fusion.11), channel_id=1, source_target_pairs={{0,192},{64,0},{128,64},{192,128},{1,193},{65,1},{129,65},{193,129... | collective-permute-start | bytes 49160 | tf_op jit(solution)/shard_map/ppermute | solution.py:508
  144.5 0.9 collective-permute-start.15
  145.4 0.6 slice_bitcast_fusion
  146.0 0.7 fusion.15
  146.7 17.7 %collective-permute-done.17 = f32[16,256]{1,0:T(8,128)S(1)} collective-permute-done((f32[16,256]{1,0:T(8,128)S(1)}, f32[16,256]{1,0:T(8,128)S(1)}, u32[]{:S(2)}, u32[]{:S(2)}) %collective-permute-start.17) | collective-permute-done | bytes 16416 | tf_op jit(solution)/shard_map/ppermute | solution.py:508
  164.4 1.2 collective-permute-done.16
  165.8 0.6 reshape.73
  166.4 4.6 %all-to-all-done.2 = bf16[256,16,128]{2,1,0:T(8,128)(2,1)S(1)} async-done(((bf16[256,16,128]{2,1,0:T(8,128)(2,1)}), bf16[256,16,128]{2,1,0:T(8,128)(2,1)S(1)}, u32[]{:S(2)}, u32[]{:S(2)}) %all-to-all-start.2) | async-done | bytes 1048608 | tf_op jit(solution)/shard_map/all_to_all | solution.py:521
  171.0 4.7 %row_grad.1 = f32[1,64,256]{2,1,0:T(8,128)} custom-call(bf16[256,8192]{1,0:T(8,128)(2,1)} %count.1.count_ref, bf16[4,64,16,128]{3,2,1,0:T(8,128)(2,1)S(1)} %bitcast.45), custom_call_target="tpu_custom_call" | custom-call | tf_op jit(solution)/shard_map/row_grad/pallas_call | solution.py:488
  (72 shorter events, 1.3 us)
Async XLA Ops:
  0.6 20.0 %copy-start = (bf16[13,256]{1,0:T(8,128)(2,1)S(1)}, bf16[13,256]{1,0:T(8,128)(2,1)}, u32[]{:S(2)}) copy-start(bf16[13,256]{1,0:T(8,128)(2,1)} %param.14) | copy-start | bytes 19972
  5.4 14.7 %copy-start.8 = (s32[128]{0:T(128)S(1)}, s32[128]{0:T(128)}, u32[]{:S(2)}) copy-start(s32[128]{0:T(128)} %param.17) | copy-start | bytes 1540
  5.4 14.9 %copy-start.6 = (bf16[128,13]{0,1:T(8,128)(2,1)S(1)}, bf16[128,13]{0,1:T(8,128)(2,1)}, u32[]{:S(2)}) copy-start(bf16[128,13]{0,1:T(8,128)(2,1)} %param.13) | copy-start | bytes 9988
  5.4 45.0 %copy-start.3 = (s32[64]{0:T(128)S(1)}, s32[64]{0:T(128)}, u32[]{:S(2)}) copy-start(s32[64]{0:T(128)} %slot_ref.3) | copy-start | bytes 772
  5.5 51.2 %copy-start.7 = (bf16[512]{0:T(512)(128)(2,1)S(1)}, bf16[512]{0:T(512)(128)(2,1)}, u32[]{:S(2)}) copy-start(bf16[512]{0:T(512)(128)(2,1)} %param.16) | copy-start | bytes 3076
  5.5 59.1 %copy-start.1 = (bf16[2336,512]{1,0:T(8,128)(2,1)S(1)}, bf16[2336,512]{1,0:T(8,128)(2,1)}, u32[]{:S(2)}) copy-start(bf16[2336,512]{1,0:T(8,128)(2,1)} %weight_ref.1) | copy-start | bytes 7176196
  5.5 44.9 %all-to-all-start = ((bf16[256,16,128]{2,1,0:T(8,128)(2,1)}), bf16[256,16,128]{2,1,0:T(8,128)(2,1)S(1)}, u32[]{:S(2)}, u32[]{:S(2)}) async-start(bf16[256,16,128]{2,1,0:T(8,128)(2,1)} %bitcast.47), calls=%async_computation | async-start | bytes 2097152 | tf_op jit(solution)/shard_map/all_to_all | solution.py:521
  53.1 9.1 %collective-permute-start.2 = (bf16[32,2432]{1,0:T(8,128)(2,1)S(1)}, bf16[32,2432]{1,0:T(8,128)(2,1)S(1)}, u32[]{:S(2)}, u32[]{:S(2)}) collective-permute-start(bf16[32,2432]{1,0:T(8,128)(2,1)S(1)} %get-tuple-element.25.f0), channel_id=1, source_target_pairs={{0,128},{64,200},{128,8},{192,64},{8,136},{72,192},{136,0},{200,72... | collective-permute-start | bytes 466952 | tf_op jit(solution)/shard_map/ppermute | solution.py:516
  54.6 7.6 %collective-permute-start.1 = (bf16[32,2432]{1,0:T(8,128)(2,1)S(1)}, bf16[32,2432]{1,0:T(8,128)(2,1)S(1)}, u32[]{:S(2)}, u32[]{:S(2)}) collective-permute-start(bf16[32,2432]{1,0:T(8,128)(2,1)S(1)} %get-tuple-element.25.f0), channel_id=1, source_target_pairs={{0,200},{64,0},{128,64},{192,128},{8,192},{72,8},{136,72},{200,136... | collective-permute-start | bytes 466952 | tf_op jit(solution)/shard_map/ppermute | solution.py:516
  54.8 9.8 %collective-permute-start = (bf16[32,2432]{1,0:T(8,128)(2,1)S(1)}, bf16[32,2432]{1,0:T(8,128)(2,1)S(1)}, u32[]{:S(2)}, u32[]{:S(2)}) collective-permute-start(bf16[32,2432]{1,0:T(8,128)(2,1)S(1)} %get-tuple-element.25.f0), channel_id=1, source_target_pairs={{0,64},{64,128},{128,192},{192,8},{8,72},{72,136},{136,200},{200,0... | collective-permute-start | bytes 466952 | tf_op jit(solution)/shard_map/ppermute | solution.py:516
  66.5 25.0 %copy-start.2 = (bf16[32,2432]{1,0:T(8,128)(2,1)S(1)}, bf16[32,2432]{1,0:T(8,128)(2,1)}, u32[]{:S(2)}) copy-start(bf16[32,2432]{1,0:T(8,128)(2,1)} %get-tuple-element.26.z0) | copy-start | bytes 466948
  66.5 11.1 %all-to-all-start.1 = ((f32[8,8,128]{2,1,0:T(8,128)}), f32[8,8,128]{2,1,0:T(8,128)S(1)}, u32[]{:S(2)}, u32[]{:S(2)}) async-start(f32[8,8,128]{2,1,0:T(8,128)} %get-tuple-element.30), calls=%async_computation.1 | async-start | bytes 65536 | tf_op jit(solution)/shard_map/all_to_all | solution.py:616
  81.5 14.1 %collective-permute-start.6 = (bf16[16,16,2432]{2,1,0:T(8,128)(2,1)}, bf16[16,16,2432]{2,1,0:T(8,128)(2,1)S(1)}, u32[]{:S(2)}, u32[]{:S(2)}) collective-permute-start(bf16[16,16,2432]{2,1,0:T(8,128)(2,1)} %get-tuple-element.37), channel_id=1, source_target_pairs={{0,1},{1,0},{2,3},{3,2},{4,5},{5,4},{6,7},{7,6},{8,9},{9,8},{10,11... | collective-permute-start | bytes 3735560 | tf_op jit(solution)/shard_map/ppermute | solution.py:508
  81.5 6.6 %collective-permute-start.3 = (bf16[32,2432]{1,0:T(8,128)(2,1)S(1)}, bf16[32,2432]{1,0:T(8,128)(2,1)S(1)}, u32[]{:S(2)}, u32[]{:S(2)}) collective-permute-start(bf16[32,2432]{1,0:T(8,128)(2,1)S(1)} %get-tuple-element.27), channel_id=1, source_target_pairs={{0,200},{64,0},{128,64},{192,128},{8,192},{72,8},{136,72},{200,136... | collective-permute-start | bytes 466952 | tf_op jit(solution)/shard_map/ppermute | solution.py:516
  82.2 8.1 %collective-permute-start.4 = (bf16[32,2432]{1,0:T(8,128)(2,1)S(1)}, bf16[32,2432]{1,0:T(8,128)(2,1)S(1)}, u32[]{:S(2)}, u32[]{:S(2)}) collective-permute-start(bf16[32,2432]{1,0:T(8,128)(2,1)S(1)} %get-tuple-element.28), channel_id=1, source_target_pairs={{0,64},{64,128},{128,192},{192,8},{8,72},{72,136},{136,200},{200,0... | collective-permute-start | bytes 466952 | tf_op jit(solution)/shard_map/ppermute | solution.py:516
  83.6 8.0 %collective-permute-start.5 = (bf16[32,2432]{1,0:T(8,128)(2,1)S(1)}, bf16[32,2432]{1,0:T(8,128)(2,1)S(1)}, u32[]{:S(2)}, u32[]{:S(2)}) collective-permute-start(bf16[32,2432]{1,0:T(8,128)(2,1)S(1)} %get-tuple-element.29), channel_id=1, source_target_pairs={{0,136},{64,192},{128,0},{192,72},{8,128},{72,200},{136,8},{200,64... | collective-permute-start | bytes 466952 | tf_op jit(solution)/shard_map/ppermute | solution.py:516
  98.0 12.1 %collective-permute-start.7 = (bf16[64,2560]{1,0:T(8,128)(2,1)S(1)}, bf16[64,2560]{1,0:T(8,128)(2,1)S(1)}, u32[]{:S(2)}, u32[]{:S(2)}) collective-permute-start(bf16[64,2560]{1,0:T(8,128)(2,1)S(1)} %get-tuple-element.40), channel_id=1, source_target_pairs={{0,32},{16,48},{32,0},{48,16},{1,33},{17,49},{33,1},{49,17},{2,34}... | collective-permute-start | bytes 983048 | tf_op jit(solution)/shard_map/ppermute | solution.py:508
  104.5 11.4 %collective-permute-start.8 = (bf16[64,2560]{1,0:T(8,128)(2,1)S(1)}, bf16[64,2560]{1,0:T(8,128)(2,1)S(1)}, u32[]{:S(2)}, u32[]{:S(2)}) collective-permute-start(bf16[64,2560]{1,0:T(8,128)(2,1)S(1)} %get-tuple-element.41), channel_id=1, source_target_pairs={{0,16},{16,32},{32,48},{48,0},{1,17},{17,33},{33,49},{49,1},{2,18}... | collective-permute-start | bytes 983048 | tf_op jit(solution)/shard_map/ppermute | solution.py:508
  106.0 9.9 %collective-permute-start.9 = (bf16[64,2560]{1,0:T(8,128)(2,1)S(1)}, bf16[64,2560]{1,0:T(8,128)(2,1)S(1)}, u32[]{:S(2)}, u32[]{:S(2)}) collective-permute-start(bf16[64,2560]{1,0:T(8,128)(2,1)S(1)} %get-tuple-element.42), channel_id=1, source_target_pairs={{0,48},{16,0},{32,16},{48,32},{1,49},{17,1},{33,17},{49,33},{2,50}... | collective-permute-start | bytes 983048 | tf_op jit(solution)/shard_map/ppermute | solution.py:508
  110.2 5.8 %copy-start.4 = (f32[64,2432]{1,0:T(8,128)S(1)}, f32[64,2432]{1,0:T(8,128)}, u32[]{:S(2)}) copy-start(f32[64,2432]{1,0:T(8,128)} %get-tuple-element.43) | copy-start | bytes 1867780
  116.2 1.3 collective-permute-start.10
  117.5 6.1 %collective-permute-start.12 = (bf16[16,2944]{1,0:T(8,128)(2,1)S(1)}, bf16[16,2944]{1,0:T(8,128)(2,1)S(1)}, u32[]{:S(2)}, u32[]{:S(2)}) collective-permute-start(bf16[16,2944]{1,0:T(8,128)(2,1)S(1)} %get-tuple-element.56), channel_id=1, source_target_pairs={{0,2},{2,4},{4,6},{6,0},{1,3},{3,5},{5,7},{7,1},{8,10},{10,12},{12... | collective-permute-start | bytes 282632 | tf_op jit(solution)/shard_map/ppermute | solution.py:508
  118.0 6.8 %collective-permute-start.13 = (bf16[16,2944]{1,0:T(8,128)(2,1)S(1)}, bf16[16,2944]{1,0:T(8,128)(2,1)S(1)}, u32[]{:S(2)}, u32[]{:S(2)}) collective-permute-start(bf16[16,2944]{1,0:T(8,128)(2,1)S(1)} %get-tuple-element.57), channel_id=1, source_target_pairs={{0,6},{2,0},{4,2},{6,4},{1,7},{3,1},{5,3},{7,5},{8,14},{10,8},{12,... | collective-permute-start | bytes 282632 | tf_op jit(solution)/shard_map/ppermute | solution.py:508
  120.8 6.1 %collective-permute-start.11 = (bf16[16,2944]{1,0:T(8,128)(2,1)S(1)}, bf16[16,2944]{1,0:T(8,128)(2,1)S(1)}, u32[]{:S(2)}, u32[]{:S(2)}) collective-permute-start(bf16[16,2944]{1,0:T(8,128)(2,1)S(1)} %get-tuple-element.58), channel_id=1, source_target_pairs={{0,4},{2,6},{4,0},{6,2},{1,5},{3,7},{5,1},{7,3},{8,12},{10,14},{12... | collective-permute-start | bytes 282632 | tf_op jit(solution)/shard_map/ppermute | solution.py:508
  127.0 13.4 %collective-permute-start.14 = (bf16[8,3456]{1,0:T(8,128)(2,1)S(1)}, bf16[8,3456]{1,0:T(8,128)(2,1)S(1)}, u32[]{:S(2)}, u32[]{:S(2)}) collective-permute-start(bf16[8,3456]{1,0:T(8,128)(2,1)S(1)} %constant_dynamic-update-slice_fusion), channel_id=1, source_target_pairs={{0,8},{8,0},{1,9},{9,1},{2,10},{10,2},{3,11},{11,3},{4,12},{12,4},... | collective-permute-start | bytes 165896 | tf_op jit(solution)/shard_map/ppermute | solution.py:508
  128.7 42.3 %all-to-all-start.2 = ((bf16[256,16,128]{2,1,0:T(8,128)(2,1)}), bf16[256,16,128]{2,1,0:T(8,128)(2,1)S(1)}, u32[]{:S(2)}, u32[]{:S(2)}) async-start(bf16[256,16,128]{2,1,0:T(8,128)(2,1)} %bitcast.25), calls=%async_computation.2 | async-start | bytes 2097152 | tf_op jit(solution)/shard_map/all_to_all | solution.py:521
  140.5 23.9 %collective-permute-start.17 = (f32[16,256]{1,0:T(8,128)S(1)}, f32[16,256]{1,0:T(8,128)S(1)}, u32[]{:S(2)}, u32[]{:S(2)}) collective-permute-start(f32[16,256]{1,0:T(8,128)S(1)} %fusion.11), channel_id=1, source_target_pairs={{0,192},{64,0},{128,64},{192,128},{1,193},{65,1},{129,65},{193,129... | collective-permute-start | bytes 49160 | tf_op jit(solution)/shard_map/ppermute | solution.py:508
  144.5 21.1 %collective-permute-start.16 = (f32[16,256]{1,0:T(8,128)S(1)}, f32[16,256]{1,0:T(8,128)S(1)}, u32[]{:S(2)}, u32[]{:S(2)}) collective-permute-start(f32[16,256]{1,0:T(8,128)S(1)} %fusion.11), channel_id=1, source_target_pairs={{0,64},{64,128},{128,192},{192,0},{1,65},{65,129},{129,193},{193,1... | collective-permute-start | bytes 49160 | tf_op jit(solution)/shard_map/ppermute | solution.py:508
  144.5 21.1 %collective-permute-start.15 = (f32[16,256]{1,0:T(8,128)S(1)}, f32[16,256]{1,0:T(8,128)S(1)}, u32[]{:S(2)}, u32[]{:S(2)}) collective-permute-start(f32[16,256]{1,0:T(8,128)S(1)} %fusion.11), channel_id=1, source_target_pairs={{0,128},{64,192},{128,0},{192,64},{1,129},{65,193},{129,1},{193,65... | collective-permute-start | bytes 49160 | tf_op jit(solution)/shard_map/ppermute | solution.py:508
  165.6 10.1 %copy-start.5 = (f32[16,256]{1,0:T(8,128)}, f32[16,256]{1,0:T(8,128)S(1)}, u32[]{:S(2)}) copy-start(f32[16,256]{1,0:T(8,128)S(1)} %add_add_fusion) | copy-start | bytes 49156

commit v7 on v6

--- a/solution.py
+++ b/solution.py
@@ -20,7 +20,7 @@
 EMB = 256
 FEAT = 2336
 WIDE = 2432
-STEP = 16
+STEP = 32
 GRAD_STEP = 16
 LABEL_LANE = 36
 
@@ -291,7 +291,7 @@
         out_specs=vmem_specs(2),
         out_shape=[
             hbm((16, 16, WIDE), BF16),
-            hbm((16, 16, WIDE), BF16),
+            jax.ShapeDtypeStruct((16, 16, WIDE), BF16),
         ],
         scratch_shapes=[pltpu.VMEM((512, WIDE), F32)],
         compiler_params=pltpu.CompilerParams(vmem_limit_bytes=32 << 20),
@@ -433,7 +433,7 @@
         pack_kernel,
         in_specs=[pl.BlockSpec(memory_space=pltpu.SMEM)] + vmem_specs(3),
         out_specs=vmem_specs(5),
-        out_shape=[hbm((64, WIDE), F32)]
+        out_shape=[hbm((64, WIDE), BF16)]
         + [jax.ShapeDtypeStruct((64, WIDE + LANES), BF16)] * 3
         + [jax.ShapeDtypeStruct((16, EMB), F32)],
         compiler_params=pltpu.CompilerParams(vmem_limit_bytes=16 << 20),
@@ -462,7 +462,7 @@
     )(*in_hbm(pool_index, bag_length))
 
 
-def row_grad_kernel(count_ref, back_ref, out_ref, total, moved):
+def row_grad_kernel(count_ref, back_ref, out_ref, total):
     step = pl.program_id(0)
 
     @pl.when(step == 0)
@@ -472,11 +472,11 @@
     low = low_lanes(HALF)
     first = jnp.where(low, 1.0, 0.0).astype(BF16)
     second = jnp.where(low, 0.0, 1.0).astype(BF16)
+    moved = []
     for group in range(GRAD_STEP):
         rows = jnp.concatenate([back_ref[peer, group] for peer in range(4)], axis=0)
-        moved[group * LANES : group * LANES + HALF, :] = rows * first
-        moved[group * LANES + HALF : (group + 1) * LANES, :] = rows * second
-    total[...] += jnp.dot(count_ref[...], moved[...], preferred_element_type=F32)
+        moved += [rows * first, rows * second]
+    total[...] += jnp.dot(count_ref[...], jnp.concatenate(moved, axis=0), preferred_element_type=F32)
 
     @pl.when(step == pl.num_programs(0) - 1)
     def _():
@@ -496,7 +496,6 @@
         out_shape=jax.ShapeDtypeStruct((1, HALF, 256), F32),
         scratch_shapes=[
             pltpu.VMEM((256, LANES), F32),
-            pltpu.VMEM((GRAD_STEP * LANES, LANES), BF16),
         ],
         compiler_params=pltpu.CompilerParams(vmem_limit_bytes=16 << 20),
         name="row_grad",
@@ -623,6 +622,7 @@
 
     other = shifted(other, "grp_3", 1)
     grad, *blocks, bottom = pack(place, own, other, bottom)
+    grad = grad.astype(F32)
     sums = []
     for away in (1, 2, 3):
         block = shifted(blocks[away - 1], "grp_0", away).astype(F32)

time: 178 us -> 179 us (level)
  local copies, waits for them, and re-layouts: 2.11 us -> 4.12 us
    unnamed x23 -> x35, local copies, waits for them, and re-layouts: 0.18 us -> 2.18 us
where the time goes in v7:
time: 179 us; the launch traced here: 177 us
  waiting for transfers between devices  92 us (51%)
  starting transfers between devices  49.9 us (28%)
  Pallas kernels  28 us (16%)
  local copies, waits for them, and re-layouts  4.12 us (2%)
    ppermute x12, waiting for transfers between devices, shifted(): return lax.ppermute(x, axis, [(i, (i + shift) % size) for i in range(size)])  35.6 us
    all_to_all x2, waiting for transfers between devices, exchange_all(): lax.all_to_all(flat, COL_GRP, split_axis=0, concat_axis=0, tiled=True)  34.2 us
    all_to_all x2, starting transfers between devices, exchange_all(): lax.all_to_all(flat, COL_GRP, split_axis=0, concat_axis=0, tiled=True)  26.4 us
    ppermute x6, waiting for transfers between devices, ring_sent(): return lax.ppermute(x, ('col', 'grp_1'), pairs)  15 us
    ppermute x12, starting transfers between devices, shifted(): return lax.ppermute(x, axis, [(i, (i + shift) % size) for i in range(size)])  13.6 us
    all_to_all x1, waiting for transfers between devices, step(): lax.all_to_all(partial, ('col', 'grp_1'), split_axis=0, concat_axis=0, ti...  7.2 us
    ppermute x6, starting transfers between devices, ring_sent(): return lax.ppermute(x, ('col', 'grp_1'), pairs)  6.43 us
    pallas_call x1, Pallas kernels, row_grad(): pl.pallas_call(row_grad_kernel, grid=(TAB // GRAD_STEP,), in_specs=[pl.Bl...  4.58 us
  transfers between devices with their start and end apart: 21, of which 17 were waited for; matrix products, arithmetic and copies ran while one was open for 2% of the time, Pallas kernels for 5%

profile of v7, /device:TPU:4, one launch (start us, length us, event | category | flops | bytes accessed | tf_op | source)
XLA Modules:
  0.0 176.8 jit_solution(14096739550192767300)
XLA Ops:
  0.6 4.5 %pool.1 = bf16[4,64,16,128]{3,2,1,0:T(8,128)(2,1)} custom-call(s32[1,4,8192]{2,1,0:T(4,128)} %index_ref.3, s32[1,8192]{1,0:T(1,128)} %length_ref.3, bf16[1,64,256]{2,1,0:T(8,128)(2,1)} %bitcast.51), custom_call_target="tpu_custom_call" | custom-call | tf_op jit(solution)/shard_map/pool/pallas_call | solution.py:106
  5.2 14.7 %all-to-all-start = ((bf16[256,16,128]{2,1,0:T(8,128)(2,1)}), bf16[256,16,128]{2,1,0:T(8,128)(2,1)S(1)}, u32[]{:S(2)}, u32[]{:S(2)}) async-start(bf16[256,16,128]{2,1,0:T(8,128)(2,1)} %bitcast.47), calls=%async_computation | async-start | bytes 2097152 | tf_op jit(solution)/shard_map/all_to_all | solution.py:520
  20.4 0.1 add_multiply_fusion
  20.5 29.6 %all-to-all-done = bf16[256,16,128]{2,1,0:T(8,128)(2,1)S(1)} async-done(((bf16[256,16,128]{2,1,0:T(8,128)(2,1)}), bf16[256,16,128]{2,1,0:T(8,128)(2,1)S(1)}, u32[]{:S(2)}, u32[]{:S(2)}) %all-to-all-start) | async-done | bytes 1048608 | tf_op jit(solution)/shard_map/all_to_all | solution.py:520
  50.2 2.7 %interact.1 = (bf16[32,2432]{1,0:T(8,128)(2,1)S(1)}, bf16[16,64,512]{2,1,0:T(8,128)(2,1)}) custom-call(s32[64]{0:T(128)S(1)} %copy-done.3, bf16[4,64,16,128]{3,2,1,0:T(8,128)(2,1)S(1)} %bitcast.44, f32[32,256]{1,0:T(8,128)S(1)} %get-tuple-element.55.mine_ref, f32[32,128]{1,0:T(8,128)S(1)} %broadcast_in_dim.17.label_ref), custom_call_target="tpu_custom_call" | custom-call | tf_op jit(solution)/shard_map/interact/pallas_call | solution.py:174
  52.9 1.5 collective-permute-start.2
  54.5 1.9 %collective-permute-start = (bf16[32,2432]{1,0:T(8,128)(2,1)S(1)}, bf16[32,2432]{1,0:T(8,128)(2,1)S(1)}, u32[]{:S(2)}, u32[]{:S(2)}) collective-permute-start(bf16[32,2432]{1,0:T(8,128)(2,1)S(1)} %get-tuple-element.25.f0), channel_id=1, source_target_pairs={{0,64},{64,128},{128,192},{192,8},{8,72},{72,136},{136,200},{200,0... | collective-permute-start | bytes 466952 | tf_op jit(solution)/shard_map/ppermute | solution.py:515
  56.4 5.5 %collective-permute-done.2.f3 = bf16[32,2432]{1,0:T(8,128)(2,1)S(1)} collective-permute-done((bf16[32,2432]{1,0:T(8,128)(2,1)S(1)}, bf16[32,2432]{1,0:T(8,128)(2,1)S(1)}, u32[]{:S(2)}, u32[]{:S(2)}) %collective-permute-start.2) | collective-permute-done | bytes 155680 | tf_op jit(solution)/shard_map/ppermute | solution.py:515
  62.0 2.3 %collective-permute-done.f1 = bf16[32,2432]{1,0:T(8,128)(2,1)S(1)} collective-permute-done((bf16[32,2432]{1,0:T(8,128)(2,1)S(1)}, bf16[32,2432]{1,0:T(8,128)(2,1)S(1)}, u32[]{:S(2)}, u32[]{:S(2)}) %collective-permute-start) | collective-permute-done | bytes 155680 | tf_op jit(solution)/shard_map/ppermute | solution.py:515
  64.3 2.0 %top.1 = (bf16[128,2432]{1,0:T(8,128)(2,1)}, bf16[32,2432]{1,0:T(8,128)(2,1)}, bf16[32,2432]{1,0:T(8,128)(2,1)S(1)}, bf16[32,2432]{1,0:T(8,128)(2,1)S(1)}, bf16[...) custom-call(bf16[32,2432]{1,0:T(8,128)(2,1)S(1)} %get-tuple-element.25.f0, ...), custom_call_target="tpu_custom_call" | custom-call | tf_op jit(solution)/shard_map/top/pallas_call | solution.py:220
  66.3 0.7 copy-done.4
  67.0 0.7 copy-done.6
  67.6 0.7 copy-done.8
  68.3 3.5 %all-to-all-start.1 = ((f32[8,8,128]{2,1,0:T(8,128)}), f32[8,8,128]{2,1,0:T(8,128)S(1)}, u32[]{:S(2)}, u32[]{:S(2)}) async-start(f32[8,8,128]{2,1,0:T(8,128)} %get-tuple-element.30), calls=%async_computation.1 | async-start | bytes 65536 | tf_op jit(solution)/shard_map/all_to_all | solution.py:615
  72.2 7.2 %all-to-all-done.1.partial_ref = f32[8,8,128]{2,1,0:T(8,128)S(1)} async-done(((f32[8,8,128]{2,1,0:T(8,128)}), f32[8,8,128]{2,1,0:T(8,128)S(1)}, u32[]{:S(2)}, u32[]{:S(2)}) %all-to-all-start.1) | async-done | bytes 32800 | tf_op jit(solution)/shard_map/all_to_all | solution.py:615
  79.4 3.6 %weight_grad.1 = (bf16[16,16,2432]{2,1,0:T(8,128)(2,1)}, bf16[16,16,2432]{2,1,0:T(8,128)(2,1)S(1)}) custom-call(s32[9]{0:T(128)S(1)} %stack.39.place_ref, f32[8,8,128]{2,1,0:T(8,128)S(1)} %all-to-all-done.1.partial_ref, bf16[128,2432]{1,0:T(8,128)(2,1)} %get-tuple-element.33.all_ref, bf16[128,512]{1,0:T(8,128)(2,1)} %get-tuple-element.34.delta_ref, ...), custom_call_target="tpu_custom_call" | custom-call | tf_op jit(solution)/shard_map/weight_grad/pallas_call | solution.py:288
  83.0 0.7 collective-permute-start.3
  83.7 1.3 collective-permute-start.4
  85.0 0.9 collective-permute-start.5
  85.9 3.7 %collective-permute-done.3.z1 = bf16[32,2432]{1,0:T(8,128)(2,1)S(1)} collective-permute-done((bf16[32,2432]{1,0:T(8,128)(2,1)S(1)}, bf16[32,2432]{1,0:T(8,128)(2,1)S(1)}, u32[]{:S(2)}, u32[]{:S(2)}) %collective-permute-start.3) | collective-permute-done | bytes 155680 | tf_op jit(solution)/shard_map/ppermute | solution.py:515
  89.6 2.2 %collective-permute-done.4.z2 = bf16[32,2432]{1,0:T(8,128)(2,1)S(1)} collective-permute-done((bf16[32,2432]{1,0:T(8,128)(2,1)S(1)}, bf16[32,2432]{1,0:T(8,128)(2,1)S(1)}, u32[]{:S(2)}, u32[]{:S(2)}) %collective-permute-start.4) | collective-permute-done | bytes 155680 | tf_op jit(solution)/shard_map/ppermute | solution.py:515
  91.8 1.2 collective-permute-done.5.z3
  93.1 4.1 %spread.1 = (bf16[4,64,16,128]{3,2,1,0:T(8,128)(2,1)}, f32[16,256]{1,0:T(8,128)S(1)}, f32[8,128]{1,0:T(8,128)S(1)}) custom-call(s32[64]{0:T(128)S(1)} %copy-done.3, s32[9]{0:T(128)S(1)} %stack.39.place_ref, bf16[32,2432]{1,0:T(8,128)(2,1)S(1)} %copy-done.2, bf16[32,2432]{1,0:T(8,128)(2,1)S(1)} %collective-permute-done.3.z1, ...), custom_call_target="tpu_custom_call" | custom-call | tf_op jit(solution)/shard_map/spread/pallas_call | solution.py:394
  97.1 2.1 %pack.1 = (bf16[64,2432]{1,0:T(8,128)(2,1)}, bf16[64,2560]{1,0:T(8,128)(2,1)S(1)}, bf16[64,2560]{1,0:T(8,128)(2,1)S(1)}, bf16[64,2560]{1,0:T(8,128)(2,1)S(1)}, f32[16,256]{1,0:T(8,128)S(1)}) custom-call(s32[9]{0:T(128)S(1)} %stack.39.place_ref, bf16[16,16,2432]{2,1,0:T(8,128)(2,1)} %get-tuple-element.36.own_ref, ...), custom_call_target="tpu_custom_call" | custom-call | tf_op jit(solution)/shard_map/pack/pallas_call | solution.py:432
  99.3 1.7 collective-permute-start.7
  101.0 4.3 %count.1.count_ref = bf16[256,8192]{1,0:T(8,128)(2,1)} custom-call(s32[1,4,8192]{2,1,0:T(4,128)} %index_ref.3, s32[1,8192]{1,0:T(1,128)} %length_ref.3), custom_call_target="tpu_custom_call" | custom-call | tf_op jit(solution)/shard_map/count/pallas_call | solution.py:451
  105.3 1.6 collective-permute-start.8
  106.9 0.5 collective-permute-start.9
  107.4 3.9 %collective-permute-done.7 = bf16[64,2560]{1,0:T(8,128)(2,1)S(1)} collective-permute-done((bf16[64,2560]{1,0:T(8,128)(2,1)S(1)}, bf16[64,2560]{1,0:T(8,128)(2,1)S(1)}, u32[]{:S(2)}, u32[]{:S(2)}) %collective-permute-start.7) | collective-permute-done | bytes 327712 | tf_op jit(solution)/shard_map/ppermute | solution.py:507
  111.4 5.6 %collective-permute-done.8 = bf16[64,2560]{1,0:T(8,128)(2,1)S(1)} collective-permute-done((bf16[64,2560]{1,0:T(8,128)(2,1)S(1)}, bf16[64,2560]{1,0:T(8,128)(2,1)S(1)}, u32[]{:S(2)}, u32[]{:S(2)}) %collective-permute-start.8) | collective-permute-done | bytes 327712 | tf_op jit(solution)/shard_map/ppermute | solution.py:507
  117.2 0.1 slice_add_fusion
  117.5 1.1 collective-permute-done.10
  118.7 0.6 collective-permute-start.12
  119.2 2.8 %collective-permute-start.13 = (bf16[16,2944]{1,0:T(8,128)(2,1)S(1)}, bf16[16,2944]{1,0:T(8,128)(2,1)S(1)}, u32[]{:S(2)}, u32[]{:S(2)}) collective-permute-start(bf16[16,2944]{1,0:T(8,128)(2,1)S(1)} %get-tuple-element.57), channel_id=1, source_target_pairs={{0,6},{2,0},{4,2},{6,4},{1,7},{3,1},{5,3},{7,5},{8,14},{10,8},{12,... | collective-permute-start | bytes 282632 | tf_op jit(solution)/shard_map/ppermute | solution.py:507
  122.0 2.7 %collective-permute-done.12 = bf16[16,2944]{1,0:T(8,128)(2,1)S(1)} collective-permute-done((bf16[16,2944]{1,0:T(8,128)(2,1)S(1)}, bf16[16,2944]{1,0:T(8,128)(2,1)S(1)}, u32[]{:S(2)}, u32[]{:S(2)}) %collective-permute-start.12) | collective-permute-done | bytes 94240 | tf_op jit(solution)/shard_map/ppermute | solution.py:507
  124.8 1.3 collective-permute-done.13
  126.1 2.0 %collective-permute-done.11 = bf16[16,2944]{1,0:T(8,128)(2,1)S(1)} collective-permute-done((bf16[16,2944]{1,0:T(8,128)(2,1)S(1)}, bf16[16,2944]{1,0:T(8,128)(2,1)S(1)}, u32[]{:S(2)}, u32[]{:S(2)}) %collective-permute-start.11) | collective-permute-done | bytes 94240 | tf_op jit(solution)/shard_map/ppermute | solution.py:507
  128.2 1.6 collective-permute-start.14
  129.9 11.7 %all-to-all-start.2 = ((bf16[256,16,128]{2,1,0:T(8,128)(2,1)}), bf16[256,16,128]{2,1,0:T(8,128)(2,1)S(1)}, u32[]{:S(2)}, u32[]{:S(2)}) async-start(bf16[256,16,128]{2,1,0:T(8,128)(2,1)} %bitcast.25), calls=%async_computation.2 | async-start | bytes 2097152 | tf_op jit(solution)/shard_map/all_to_all | solution.py:520
  141.7 4.0 %collective-permute-start.17 = (f32[16,256]{1,0:T(8,128)S(1)}, f32[16,256]{1,0:T(8,128)S(1)}, u32[]{:S(2)}, u32[]{:S(2)}) collective-permute-start(f32[16,256]{1,0:T(8,128)S(1)} %fusion.11), channel_id=1, source_target_pairs={{0,192},{64,0},{128,64},{192,128},{1,193},{65,1},{129,65},{193,129... | collective-permute-start | bytes 49160 | tf_op jit(solution)/shard_map/ppermute | solution.py:507
  145.7 0.9 collective-permute-start.15
  146.6 0.6 slice_bitcast_fusion
  147.2 0.7 fusion.15
  147.9 17.7 %collective-permute-done.17 = f32[16,256]{1,0:T(8,128)S(1)} collective-permute-done((f32[16,256]{1,0:T(8,128)S(1)}, f32[16,256]{1,0:T(8,128)S(1)}, u32[]{:S(2)}, u32[]{:S(2)}) %collective-permute-start.17) | collective-permute-done | bytes 16416 | tf_op jit(solution)/shard_map/ppermute | solution.py:507
  165.6 1.2 collective-permute-done.16
  167.0 0.6 reshape.73
  167.6 4.6 %all-to-all-done.2 = bf16[256,16,128]{2,1,0:T(8,128)(2,1)S(1)} async-done(((bf16[256,16,128]{2,1,0:T(8,128)(2,1)}), bf16[256,16,128]{2,1,0:T(8,128)(2,1)S(1)}, u32[]{:S(2)}, u32[]{:S(2)}) %all-to-all-start.2) | async-done | bytes 1048608 | tf_op jit(solution)/shard_map/all_to_all | solution.py:520
  172.2 4.6 %row_grad.1 = f32[1,64,256]{2,1,0:T(8,128)} custom-call(bf16[256,8192]{1,0:T(8,128)(2,1)} %count.1.count_ref, bf16[4,64,16,128]{3,2,1,0:T(8,128)(2,1)S(1)} %bitcast.45), custom_call_target="tpu_custom_call" | custom-call | tf_op jit(solution)/shard_map/row_grad/pallas_call | solution.py:488
  (84 shorter events, 1.7 us)
Async XLA Ops:
  0.6 19.7 %copy-start = (bf16[13,256]{1,0:T(8,128)(2,1)S(1)}, bf16[13,256]{1,0:T(8,128)(2,1)}, u32[]{:S(2)}) copy-start(bf16[13,256]{1,0:T(8,128)(2,1)} %param.14) | copy-start | bytes 19972
  5.2 14.7 %copy-start.14 = (s32[128]{0:T(128)S(1)}, s32[128]{0:T(128)}, u32[]{:S(2)}) copy-start(s32[128]{0:T(128)} %param.17) | copy-start | bytes 1540
  5.2 14.9 %copy-start.12 = (bf16[128,13]{0,1:T(8,128)(2,1)S(1)}, bf16[128,13]{0,1:T(8,128)(2,1)}, u32[]{:S(2)}) copy-start(bf16[128,13]{0,1:T(8,128)(2,1)} %param.13) | copy-start | bytes 9988
  5.2 45.0 %copy-start.3 = (s32[64]{0:T(128)S(1)}, s32[64]{0:T(128)}, u32[]{:S(2)}) copy-start(s32[64]{0:T(128)} %slot_ref.3) | copy-start | bytes 772
  5.2 51.2 %copy-start.13 = (bf16[512]{0:T(512)(128)(2,1)S(1)}, bf16[512]{0:T(512)(128)(2,1)}, u32[]{:S(2)}) copy-start(bf16[512]{0:T(512)(128)(2,1)} %param.16) | copy-start | bytes 3076
  5.2 59.1 %copy-start.1 = (bf16[2336,512]{1,0:T(8,128)(2,1)S(1)}, bf16[2336,512]{1,0:T(8,128)(2,1)}, u32[]{:S(2)}) copy-start(bf16[2336,512]{1,0:T(8,128)(2,1)} %weight_ref.1) | copy-start | bytes 7176196
  5.2 44.9 %all-to-all-start = ((bf16[256,16,128]{2,1,0:T(8,128)(2,1)}), bf16[256,16,128]{2,1,0:T(8,128)(2,1)S(1)}, u32[]{:S(2)}, u32[]{:S(2)}) async-start(bf16[256,16,128]{2,1,0:T(8,128)(2,1)} %bitcast.47), calls=%async_computation | async-start | bytes 2097152 | tf_op jit(solution)/shard_map/all_to_all | solution.py:520
  52.9 9.1 %collective-permute-start.2 = (bf16[32,2432]{1,0:T(8,128)(2,1)S(1)}, bf16[32,2432]{1,0:T(8,128)(2,1)S(1)}, u32[]{:S(2)}, u32[]{:S(2)}) collective-permute-start(bf16[32,2432]{1,0:T(8,128)(2,1)S(1)} %get-tuple-element.25.f0), channel_id=1, source_target_pairs={{0,128},{64,200},{128,8},{192,64},{8,136},{72,192},{136,0},{200,72... | collective-permute-start | bytes 466952 | tf_op jit(solution)/shard_map/ppermute | solution.py:515
  54.4 7.6 %collective-permute-start.1 = (bf16[32,2432]{1,0:T(8,128)(2,1)S(1)}, bf16[32,2432]{1,0:T(8,128)(2,1)S(1)}, u32[]{:S(2)}, u32[]{:S(2)}) collective-permute-start(bf16[32,2432]{1,0:T(8,128)(2,1)S(1)} %get-tuple-element.25.f0), channel_id=1, source_target_pairs={{0,200},{64,0},{128,64},{192,128},{8,192},{72,8},{136,72},{200,136... | collective-permute-start | bytes 466952 | tf_op jit(solution)/shard_map/ppermute | solution.py:515
  54.5 9.8 %collective-permute-start = (bf16[32,2432]{1,0:T(8,128)(2,1)S(1)}, bf16[32,2432]{1,0:T(8,128)(2,1)S(1)}, u32[]{:S(2)}, u32[]{:S(2)}) collective-permute-start(bf16[32,2432]{1,0:T(8,128)(2,1)S(1)} %get-tuple-element.25.f0), channel_id=1, source_target_pairs={{0,64},{64,128},{128,192},{192,8},{8,72},{72,136},{136,200},{200,0... | collective-permute-start | bytes 466952 | tf_op jit(solution)/shard_map/ppermute | solution.py:515
  66.3 0.7 copy-start.4
  67.0 0.7 copy-start.6
  67.6 0.7 copy-start.8
  68.3 24.8 %copy-start.2 = (bf16[32,2432]{1,0:T(8,128)(2,1)S(1)}, bf16[32,2432]{1,0:T(8,128)(2,1)}, u32[]{:S(2)}) copy-start(bf16[32,2432]{1,0:T(8,128)(2,1)} %get-tuple-element.26.z0) | copy-start | bytes 466948
  68.3 14.7 %copy-start.9 = (bf16[32,2432]{1,0:T(8,128)(2,1)S(1)}, bf16[32,2432]{1,0:T(8,128)(2,1)}, u32[]{:S(2)}) copy-start(bf16[32,2432]{1,0:T(8,128)(2,1)} %copy-done.8) | copy-start | bytes 466948
  68.3 15.4 %copy-start.7 = (bf16[32,2432]{1,0:T(8,128)(2,1)S(1)}, bf16[32,2432]{1,0:T(8,128)(2,1)}, u32[]{:S(2)}) copy-start(bf16[32,2432]{1,0:T(8,128)(2,1)} %copy-done.6) | copy-start | bytes 466948
  68.3 16.7 %copy-start.5 = (bf16[32,2432]{1,0:T(8,128)(2,1)S(1)}, bf16[32,2432]{1,0:T(8,128)(2,1)}, u32[]{:S(2)}) copy-start(bf16[32,2432]{1,0:T(8,128)(2,1)} %copy-done.4) | copy-start | bytes 466948
  68.3 11.1 %all-to-all-start.1 = ((f32[8,8,128]{2,1,0:T(8,128)}), f32[8,8,128]{2,1,0:T(8,128)S(1)}, u32[]{:S(2)}, u32[]{:S(2)}) async-start(f32[8,8,128]{2,1,0:T(8,128)} %get-tuple-element.30), calls=%async_computation.1 | async-start | bytes 65536 | tf_op jit(solution)/shard_map/all_to_all | solution.py:615
  83.0 14.1 %collective-permute-start.6 = (bf16[16,16,2432]{2,1,0:T(8,128)(2,1)S(1)}, bf16[16,16,2432]{2,1,0:T(8,128)(2,1)S(1)}, u32[]{:S(2)}, u32[]{:S(2)}) collective-permute-start(bf16[16,16,2432]{2,1,0:T(8,128)(2,1)S(1)} %get-tuple-element.37), channel_id=1, source_target_pairs={{0,1},{1,0},{2,3},{3,2},{4,5},{5,4},{6,7},{7,6},{8,9},{9,8},{10,11... | collective-permute-start | bytes 3735560 | tf_op jit(solution)/shard_map/ppermute | solution.py:507
  83.0 6.6 %collective-permute-start.3 = (bf16[32,2432]{1,0:T(8,128)(2,1)S(1)}, bf16[32,2432]{1,0:T(8,128)(2,1)S(1)}, u32[]{:S(2)}, u32[]{:S(2)}) collective-permute-start(bf16[32,2432]{1,0:T(8,128)(2,1)S(1)} %copy-done.9), channel_id=1, source_target_pairs={{0,200},{64,0},{128,64},{192,128},{8,192},{72,8},{136,72},{200,136... | collective-permute-start | bytes 466952 | tf_op jit(solution)/shard_map/ppermute | solution.py:515
  83.7 8.1 %collective-permute-start.4 = (bf16[32,2432]{1,0:T(8,128)(2,1)S(1)}, bf16[32,2432]{1,0:T(8,128)(2,1)S(1)}, u32[]{:S(2)}, u32[]{:S(2)}) collective-permute-start(bf16[32,2432]{1,0:T(8,128)(2,1)S(1)} %copy-done.7), channel_id=1, source_target_pairs={{0,64},{64,128},{128,192},{192,8},{8,72},{72,136},{136,200},{200,0... | collective-permute-start | bytes 466952 | tf_op jit(solution)/shard_map/ppermute | solution.py:515
  85.0 8.0 %collective-permute-start.5 = (bf16[32,2432]{1,0:T(8,128)(2,1)S(1)}, bf16[32,2432]{1,0:T(8,128)(2,1)S(1)}, u32[]{:S(2)}, u32[]{:S(2)}) collective-permute-start(bf16[32,2432]{1,0:T(8,128)(2,1)S(1)} %copy-done.5), channel_id=1, source_target_pairs={{0,136},{64,192},{128,0},{192,72},{8,128},{72,200},{136,8},{200,64... | collective-permute-start | bytes 466952 | tf_op jit(solution)/shard_map/ppermute | solution.py:515
  99.3 12.1 %collective-permute-start.7 = (bf16[64,2560]{1,0:T(8,128)(2,1)S(1)}, bf16[64,2560]{1,0:T(8,128)(2,1)S(1)}, u32[]{:S(2)}, u32[]{:S(2)}) collective-permute-start(bf16[64,2560]{1,0:T(8,128)(2,1)S(1)} %get-tuple-element.40), channel_id=1, source_target_pairs={{0,32},{16,48},{32,0},{48,16},{1,33},{17,49},{33,1},{49,17},{2,34}... | collective-permute-start | bytes 983048 | tf_op jit(solution)/shard_map/ppermute | solution.py:507
  105.3 11.7 %collective-permute-start.8 = (bf16[64,2560]{1,0:T(8,128)(2,1)S(1)}, bf16[64,2560]{1,0:T(8,128)(2,1)S(1)}, u32[]{:S(2)}, u32[]{:S(2)}) collective-permute-start(bf16[64,2560]{1,0:T(8,128)(2,1)S(1)} %get-tuple-element.41), channel_id=1, source_target_pairs={{0,16},{16,32},{32,48},{48,0},{1,17},{17,33},{33,49},{49,1},{2,18}... | collective-permute-start | bytes 983048 | tf_op jit(solution)/shard_map/ppermute | solution.py:507
  106.9 10.2 %collective-permute-start.9 = (bf16[64,2560]{1,0:T(8,128)(2,1)S(1)}, bf16[64,2560]{1,0:T(8,128)(2,1)S(1)}, u32[]{:S(2)}, u32[]{:S(2)}) collective-permute-start(bf16[64,2560]{1,0:T(8,128)(2,1)S(1)} %get-tuple-element.42), channel_id=1, source_target_pairs={{0,48},{16,0},{32,16},{48,32},{1,49},{17,1},{33,17},{49,33},{2,50}... | collective-permute-start | bytes 983048 | tf_op jit(solution)/shard_map/ppermute | solution.py:507
  111.4 5.8 %copy-start.10 = (bf16[64,2432]{1,0:T(8,128)(2,1)S(1)}, bf16[64,2432]{1,0:T(8,128)(2,1)}, u32[]{:S(2)}) copy-start(bf16[64,2432]{1,0:T(8,128)(2,1)} %get-tuple-element.43) | copy-start | bytes 933892
  117.4 1.3 collective-permute-start.10
  118.7 6.1 %collective-permute-start.12 = (bf16[16,2944]{1,0:T(8,128)(2,1)S(1)}, bf16[16,2944]{1,0:T(8,128)(2,1)S(1)}, u32[]{:S(2)}, u32[]{:S(2)}) collective-permute-start(bf16[16,2944]{1,0:T(8,128)(2,1)S(1)} %get-tuple-element.56), channel_id=1, source_target_pairs={{0,2},{2,4},{4,6},{6,0},{1,3},{3,5},{5,7},{7,1},{8,10},{10,12},{12... | collective-permute-start | bytes 282632 | tf_op jit(solution)/shard_map/ppermute | solution.py:507
  119.2 6.8 %collective-permute-start.13 = (bf16[16,2944]{1,0:T(8,128)(2,1)S(1)}, bf16[16,2944]{1,0:T(8,128)(2,1)S(1)}, u32[]{:S(2)}, u32[]{:S(2)}) collective-permute-start(bf16[16,2944]{1,0:T(8,128)(2,1)S(1)} %get-tuple-element.57), channel_id=1, source_target_pairs={{0,6},{2,0},{4,2},{6,4},{1,7},{3,1},{5,3},{7,5},{8,14},{10,8},{12,... | collective-permute-start | bytes 282632 | tf_op jit(solution)/shard_map/ppermute | solution.py:507
  122.0 6.1 %collective-permute-start.11 = (bf16[16,2944]{1,0:T(8,128)(2,1)S(1)}, bf16[16,2944]{1,0:T(8,128)(2,1)S(1)}, u32[]{:S(2)}, u32[]{:S(2)}) collective-permute-start(bf16[16,2944]{1,0:T(8,128)(2,1)S(1)} %get-tuple-element.58), channel_id=1, source_target_pairs={{0,4},{2,6},{4,0},{6,2},{1,5},{3,7},{5,1},{7,3},{8,12},{10,14},{12... | collective-permute-start | bytes 282632 | tf_op jit(solution)/shard_map/ppermute | solution.py:507
  128.2 13.4 %collective-permute-start.14 = (bf16[8,3456]{1,0:T(8,128)(2,1)S(1)}, bf16[8,3456]{1,0:T(8,128)(2,1)S(1)}, u32[]{:S(2)}, u32[]{:S(2)}) collective-permute-start(bf16[8,3456]{1,0:T(8,128)(2,1)S(1)} %constant_dynamic-update-slice_fusion), channel_id=1, source_target_pairs={{0,8},{8,0},{1,9},{9,1},{2,10},{10,2},{3,11},{11,3},{4,12},{12,4},... | collective-permute-start | bytes 165896 | tf_op jit(solution)/shard_map/ppermute | solution.py:507
  129.9 42.3 %all-to-all-start.2 = ((bf16[256,16,128]{2,1,0:T(8,128)(2,1)}), bf16[256,16,128]{2,1,0:T(8,128)(2,1)S(1)}, u32[]{:S(2)}, u32[]{:S(2)}) async-start(bf16[256,16,128]{2,1,0:T(8,128)(2,1)} %bitcast.25), calls=%async_computation.2 | async-start | bytes 2097152 | tf_op jit(solution)/shard_map/all_to_all | solution.py:520
  141.7 23.9 %collective-permute-start.17 = (f32[16,256]{1,0:T(8,128)S(1)}, f32[16,256]{1,0:T(8,128)S(1)}, u32[]{:S(2)}, u32[]{:S(2)}) collective-permute-start(f32[16,256]{1,0:T(8,128)S(1)} %fusion.11), channel_id=1, source_target_pairs={{0,192},{64,0},{128,64},{192,128},{1,193},{65,1},{129,65},{193,129... | collective-permute-start | bytes 49160 | tf_op jit(solution)/shard_map/ppermute | solution.py:507
  145.7 21.1 %collective-permute-start.16 = (f32[16,256]{1,0:T(8,128)S(1)}, f32[16,256]{1,0:T(8,128)S(1)}, u32[]{:S(2)}, u32[]{:S(2)}) collective-permute-start(f32[16,256]{1,0:T(8,128)S(1)} %fusion.11), channel_id=1, source_target_pairs={{0,64},{64,128},{128,192},{192,0},{1,65},{65,129},{129,193},{193,1... | collective-permute-start | bytes 49160 | tf_op jit(solution)/shard_map/ppermute | solution.py:507
  145.7 21.1 %collective-permute-start.15 = (f32[16,256]{1,0:T(8,128)S(1)}, f32[16,256]{1,0:T(8,128)S(1)}, u32[]{:S(2)}, u32[]{:S(2)}) collective-permute-start(f32[16,256]{1,0:T(8,128)S(1)} %fusion.11), channel_id=1, source_target_pairs={{0,128},{64,192},{128,0},{192,64},{1,129},{65,193},{129,1},{193,65... | collective-permute-start | bytes 49160 | tf_op jit(solution)/shard_map/ppermute | solution.py:507
  166.8 10.0 %copy-start.11 = (f32[16,256]{1,0:T(8,128)}, f32[16,256]{1,0:T(8,128)S(1)}, u32[]{:S(2)}) copy-start(f32[16,256]{1,0:T(8,128)S(1)} %add_add_fusion) | copy-start | bytes 49156
